TPU v7x, 32 devices: a whole 2x2x4 slice. The times are simulated.
32 devices in a mesh: batch: 4 (over y, x), seq: 8 (over z, core).
Axes of the slice: x: 2, y: 2, z: 4, core: 2. Of those that a mesh axis runs over, the one named last changes fastest.
Arguments:
- layer_input: bfloat16 [4, 1024, 768], P('batch', 'seq'), may hold values from -6 to 6
- segment_ids: int32 [4, 1024], P('batch', 'seq'), may hold values from 0 to 3, never falling along the last dimension, each value on 1 to 640 neighbouring positions
- w_query: bfloat16 [768, 768], P('seq', 'batch'), may hold values from -0.21875 to 0.21875
- w_key: bfloat16 [768, 768], P('seq', 'batch'), may hold values from -0.21875 to 0.21875
- w_value: bfloat16 [768, 768], P('seq', 'batch'), may hold values from -0.21875 to 0.21875
- w_mix: bfloat16 [768, 768], P('seq', 'batch'), may hold values from -3.5 to 3.5
- rel_table: bfloat16 [512, 768], P('seq', 'batch'), may hold values from -6 to 6
- attn_biases: bfloat16 [4, 768], P(None, 'seq'), may hold values from -3 to 3
- norm_gains: bfloat16 [2, 768], P(None, 'seq'), may hold values from 0.5 to 1.5
- norm_shifts: bfloat16 [2, 768], P(None, 'seq'), may hold values from -3 to 3
- w_up: bfloat16 [768, 3072], P(None, 'seq'), may hold values from -0.21875 to 0.21875
- up_bias: bfloat16 [3072], P('seq'), may hold values from -3 to 3
- w_down: bfloat16 [3072, 768], P('seq'), may hold values from -0.109375 to 0.109375
- down_bias: bfloat16 [768], P('seq'), may hold values from -3 to 3
- out_grad: bfloat16 [4, 1024, 768], P('batch', 'seq'), may hold values from -6 to 6
Outputs:
- layer_output: bfloat16 [4, 1024, 768], P('batch', 'seq')
- input_grad: float32 [4, 1024, 768], P('batch', 'seq')
- query_grad: float32 [768, 768], P('seq', 'batch')
- key_grad: float32 [768, 768], P('seq', 'batch')
- value_grad: float32 [768, 768], P('seq', 'batch')
- mix_grad: float32 [768, 768], P('seq', 'batch')
- table_grad: float32 [512, 768], P('seq', 'batch')
- bias_grad: float32 [4, 768], P(None, 'seq')
- gain_grad: float32 [2, 768], P(None, 'seq')
- shift_grad: float32 [2, 768], P(None, 'seq')
- up_grad: float32 [768, 3072], P('batch', 'seq')
- up_bias_grad: float32 [3072], P('seq')
- down_grad: float32 [3072, 768], P('seq', 'batch')
- down_bias_grad: float32 [768], P('seq')
Inputs may be any that keep to these rules, and one draw needn't show every extreme that they name: `segment_ids`: within a row the ids never fall; each id marks one document of 1 to 640 tokens, and a document of exactly that many tokens occurs.
All inputs are finite; a program needn't handle non-finite values.
Results may differ from a plain program's by a relative error of at most 0.014.
Values may be sent and summed in bfloat16 or wider, within the bound.
A program may use at most 256 MiB of HBM per device.

v0:
```python
import math

import jax
import jax.numpy as jnp
from jax import lax
from jax.sharding import PartitionSpec as P

DH = 64


masked_score = -1e30
norm_eps = 1e-06
pair_heads = 2


def normalize(values, gain, shift):
    average = jnp.mean(values, axis=-1, keepdims=True)
    centered = values - average
    variance = jnp.mean(centered * centered, axis=-1, keepdims=True)
    return centered * lax.rsqrt(variance + norm_eps) * gain + shift


def exact_gelu(values):
    return jax.nn.gelu(values, approximate=False)


def split_heads(matrix):
    length, rows, width = matrix.shape
    groups = width // (pair_heads * DH)
    return matrix.reshape(length, rows, groups, pair_heads, DH).transpose(2, 1, 3, 0, 4)


def join_heads(matrix):
    groups, rows, pair, length, depth = matrix.shape
    return matrix.transpose(3, 1, 0, 2, 4).reshape(length, rows, groups * pair * depth)


def split_table(matrix):
    buckets, width = matrix.shape
    return matrix.reshape(buckets, width // (pair_heads * DH), pair_heads, DH).transpose(1, 2, 0, 3)


def join_table(matrix):
    groups, pair, buckets, depth = matrix.shape
    return matrix.transpose(2, 0, 1, 3).reshape(buckets, groups * pair * depth)


def table_ends(table):
    return jnp.stack([table[:, 0], table[:, -1]], axis=1)


def near_skew(table_prod, offset, full_len):
    lead = table_prod.shape[:-2]
    count, buckets = table_prod.shape[-2:]
    span = buckets // 2
    lead_pad = [(0, 0)] * len(lead)
    flipped = jnp.pad(table_prod[..., ::-1], lead_pad + [(0, 0), (0, count)])
    sheared = flipped.reshape(lead + (count * (buckets + count),))[
        ..., : count * (buckets + count - 1)
    ]
    sheared = sheared.reshape(lead + (count, buckets + count - 1))
    spread = jnp.pad(sheared, lead_pad + [(0, 0), (full_len, full_len)])
    band = lax.dynamic_slice_in_dim(
        spread, full_len + span - 1 - offset, full_len, axis=len(lead) + 1
    )
    distance = (offset + jnp.arange(count, dtype=jnp.int32))[:, None] - jnp.arange(
        full_len, dtype=jnp.int32
    )[None, :]
    return jnp.where(
        distance <= -span,
        table_prod[..., 0:1],
        jnp.where(distance >= span - 1, table_prod[..., buckets - 1 :], band),
    )


def far_place(cross, end_vals, offset, count, full_len):
    lead = cross.shape[:-2]
    band_len, buckets = cross.shape[-2:]
    span = buckets // 2
    lead_pad = [(0, 0)] * len(lead)
    turned = jnp.swapaxes(cross, -1, -2).reshape(lead + (buckets * band_len,))
    turned = jnp.pad(turned, lead_pad + [(0, buckets)])
    diagonal = turned.reshape(lead + (buckets, band_len + 1))[..., :count]
    aligned = jnp.pad(jnp.swapaxes(diagonal, -1, -2), lead_pad + [(0, 0), (0, count)])
    sheared = aligned.reshape(lead + (count * (buckets + count),))[
        ..., : count * (buckets + count - 1)
    ]
    sheared = sheared.reshape(lead + (count, buckets + count - 1))
    spread = jnp.pad(sheared, lead_pad + [(0, 0), (full_len, full_len)])
    band = lax.dynamic_slice_in_dim(spread, full_len + span - offset, full_len, axis=len(lead) + 1)
    distance = (
        jnp.arange(full_len, dtype=jnp.int32)[None, :]
        - (offset + jnp.arange(count, dtype=jnp.int32))[:, None]
    )
    return jnp.where(
        distance <= -span,
        end_vals[..., 0:1, :],
        jnp.where(distance >= span - 1, end_vals[..., 1:2, :], band),
    )


def band_rows(all_rows, offset, count, span):
    padded = jnp.pad(all_rows, [(0, 0), (0, 0), (span, span), (0, 0)])
    return lax.dynamic_slice_in_dim(padded, offset, count + 2 * span - 1, axis=2)


def unband(values, offset, full_len, span):
    lead = values.shape[:2]
    room = jnp.zeros(lead + (full_len + 2 * span, values.shape[3]), jnp.float32)
    placed = lax.dynamic_update_slice_in_dim(room, values, offset, axis=2)
    return placed[:, :, span : span + full_len]


def relative_scores(own_rows, all_rows, own_table, all_table, offset, full_len):
    count = own_rows.shape[2]
    content = jnp.einsum("rgid,rgjd->rgij", own_rows, all_rows, preferred_element_type=jnp.float32)
    own_prod = jnp.einsum("rgid,gbd->rgib", own_rows, own_table, preferred_element_type=jnp.float32)
    window = band_rows(all_rows, offset, count, all_table.shape[1] // 2)
    cross = jnp.einsum("rgmd,gbd->rgmb", window, all_table, preferred_element_type=jnp.float32)
    end_vals = jnp.einsum(
        "rgjd,ged->rgej", all_rows, table_ends(all_table), preferred_element_type=jnp.float32
    )
    near_vals, near_pull = jax.vjp(lambda product: near_skew(product, offset, full_len), own_prod)
    far_vals, far_pull = jax.vjp(
        lambda part, ends: far_place(part, ends, offset, count, full_len), cross, end_vals
    )
    return (content + near_vals + far_vals, near_pull, far_pull, window)


def end_columns(grad):
    return jnp.stack([grad[..., 0], grad[..., -1]], axis=2)


def end_terms(ends, table):
    return jnp.einsum(
        "rgei,ged->rgid",
        ends,
        table_ends(table),
        precision=lax.Precision.HIGHEST,
        preferred_element_type=jnp.float32,
    )


def end_rows(ends, rows_low):
    return jnp.einsum(
        "rgei,rgid->ged",
        ends,
        rows_low,
        precision=lax.Precision.HIGHEST,
        preferred_element_type=jnp.float32,
    )


def with_ends(inner_part, edge_rows):
    buckets = inner_part.shape[1]
    place = jnp.arange(buckets, dtype=jnp.int32)[None, :, None]
    return (
        inner_part
        + jnp.where(place == 0, edge_rows[:, 0:1], 0.0)
        + jnp.where(place == buckets - 1, edge_rows[:, 1:2], 0.0)
    )


def body(
    layer_input,
    segment_ids,
    w_query,
    w_key,
    w_value,
    w_mix,
    rel_table,
    attn_biases,
    norm_gains,
    norm_shifts,
    w_up,
    up_bias,
    w_down,
    down_bias,
    out_grad,
):
    rows, local_len, width = layer_input.shape
    full_len = local_len * lax.axis_size("seq")
    tokens_here = local_len * rows
    highest_prec = lax.Precision.HIGHEST
    parts = (
        lax.all_gather(w_query, "batch", axis=1, tiled=True),
        lax.all_gather(w_key, "batch", axis=1, tiled=True),
        lax.all_gather(w_value, "batch", axis=1, tiled=True),
        lax.all_gather(w_mix, "batch", axis=1, tiled=True),
        lax.all_gather(rel_table, "batch", axis=1, tiled=True),
    )
    whole = (
        lax.all_gather(parts[0], "seq", axis=0, tiled=True),
        lax.all_gather(parts[1], "seq", axis=0, tiled=True),
        lax.all_gather(parts[2], "seq", axis=0, tiled=True),
        lax.all_gather(parts[3], "seq", axis=0, tiled=True),
        lax.all_gather(parts[4], "seq", axis=0, tiled=True),
        lax.all_gather(attn_biases, "seq", axis=1, tiled=True),
        lax.all_gather(norm_gains, "seq", axis=1, tiled=True),
        lax.all_gather(norm_shifts, "seq", axis=1, tiled=True),
        lax.all_gather(down_bias, "seq", axis=0, tiled=True),
    )
    m_query, m_key, m_value, m_mix, table, biases, gains, shifts, bias_down = whole
    flat_input = jnp.swapaxes(layer_input, 0, 1).reshape(tokens_here, width)
    queries = (jnp.dot(flat_input, m_query, preferred_element_type=jnp.float32) + biases[0]).astype(
        jnp.bfloat16
    )
    keys_here = (jnp.dot(flat_input, m_key, preferred_element_type=jnp.float32) + biases[1]).astype(
        jnp.bfloat16
    )
    values_here = (
        jnp.dot(flat_input, m_value, preferred_element_type=jnp.float32) + biases[2]
    ).astype(jnp.bfloat16)
    query_rel = (jnp.dot(table, m_query, preferred_element_type=jnp.float32) + biases[0]).astype(
        jnp.bfloat16
    )
    key_rel = (jnp.dot(table, m_key, preferred_element_type=jnp.float32) + biases[1]).astype(
        jnp.bfloat16
    )
    local_seg = jnp.swapaxes(segment_ids, 0, 1).astype(jnp.bfloat16)
    keys_all, values_all, seg_all = (
        lax.all_gather(keys_here.reshape(local_len, rows, width), "seq", axis=0, tiled=True),
        lax.all_gather(values_here.reshape(local_len, rows, width), "seq", axis=0, tiled=True),
        lax.all_gather(local_seg, "seq", axis=0, tiled=True),
    )
    buckets = table.shape[0]
    offset = lax.axis_index("seq") * local_len
    bucket_iota = jnp.arange(buckets, dtype=jnp.int32)
    inner_cols = (bucket_iota > 0) & (bucket_iota < buckets - 1)
    same_doc = (
        jnp.swapaxes(local_seg, 0, 1)[:, None, :, None]
        == jnp.swapaxes(seg_all, 0, 1)[:, None, None, :]
    )
    score_scale = 1.0 / math.sqrt(3.0 * DH)
    head_queries = split_heads(queries.reshape(local_len, rows, width))
    head_keys = split_heads(keys_all)
    head_values = split_heads(values_all)
    rel_queries = split_table(query_rel)
    rel_keys = split_table(key_rel)

    def forward_group(carry, group):
        g_query, g_key, g_value, g_qrel, g_krel = group
        total, near_pull, far_pull, window = relative_scores(
            g_query, g_key, g_krel, g_qrel, offset, full_len
        )
        scores = jnp.where(same_doc, total * score_scale, masked_score)
        highest = jnp.max(scores, axis=-1, keepdims=True)
        exponent = jnp.exp(scores - highest)
        denominator = jnp.sum(exponent, axis=-1, keepdims=True)
        weights_low = (exponent / denominator).astype(jnp.bfloat16)
        context = jnp.einsum(
            "rgij,rgjd->rgid", weights_low, g_value, preferred_element_type=jnp.float32
        )
        return (carry, (context, (highest + jnp.log(denominator))[..., 0]))

    unused, (context_groups, log_totals) = lax.scan(
        forward_group, None, (head_queries, head_keys, head_values, rel_queries, rel_keys)
    )
    context_low = join_heads(context_groups).reshape(tokens_here, width).astype(jnp.bfloat16)
    pre_norm = (
        flat_input.astype(jnp.float32)
        + jnp.dot(context_low, m_mix, preferred_element_type=jnp.float32)
        + biases[3]
    )
    hidden, norm1_pull = jax.vjp(
        normalize, pre_norm, gains[0].astype(jnp.float32), shifts[0].astype(jnp.float32)
    )
    hidden_low = hidden.astype(jnp.bfloat16)

    def spread_rows(rows_low):
        return lax.all_gather(rows_low, "seq", axis=0, tiled=True)

    def hidden_sums(make_term):
        return lax.psum_scatter(
            make_term(jnp.int32(0), tokens_here * lax.axis_size("seq")),
            "seq",
            scatter_dimension=0,
            tiled=True,
        )

    hidden_rows = spread_rows(hidden_low)
    inner = jnp.dot(hidden_rows, w_up, preferred_element_type=jnp.float32) + up_bias
    act, gelu_pull = jax.vjp(exact_gelu, inner)
    act_low = act.astype(jnp.bfloat16)

    def down_rows(start, count):
        return jnp.dot(act_low, w_down, preferred_element_type=jnp.float32)

    ffn_result = hidden_sums(down_rows)
    mixed = hidden + ffn_result + bias_down
    output, norm2_pull = jax.vjp(
        normalize, mixed, gains[1].astype(jnp.float32), shifts[1].astype(jnp.float32)
    )
    flat_grad = jnp.swapaxes(out_grad, 0, 1).reshape(tokens_here, width).astype(jnp.float32)
    mixed_grad, gain2_grad, shift2_grad = norm2_pull(flat_grad)
    ffn_grad_low = mixed_grad.astype(jnp.bfloat16)
    grad_rows = spread_rows(ffn_grad_low)
    act_grad = jnp.einsum("nd,fd->nf", grad_rows, w_down, preferred_element_type=jnp.float32)
    inner_low = gelu_pull(act_grad)[0].astype(jnp.bfloat16)
    up_part = jnp.einsum("nd,nf->df", hidden_rows, inner_low, preferred_element_type=jnp.float32)
    upb_part = jnp.sum(inner_low.astype(jnp.float32), axis=0)
    down_part = jnp.einsum("nf,nd->fd", act_low, grad_rows, preferred_element_type=jnp.float32)

    def back_rows(start, count):
        return jnp.einsum("nf,df->nd", inner_low, w_up, preferred_element_type=jnp.float32)

    hidden_grad = mixed_grad + hidden_sums(back_rows)
    pre_grad, gain1_grad, shift1_grad = norm1_pull(hidden_grad)
    attn_low = pre_grad.astype(jnp.bfloat16)
    mix_whole = jnp.einsum("nd,ne->de", context_low, attn_low, preferred_element_type=jnp.float32)
    context_grad = jnp.einsum(
        "ne,de->nd", attn_low, m_mix, preferred_element_type=jnp.float32
    ).astype(jnp.bfloat16)
    head_context_grad = split_heads(context_grad.reshape(local_len, rows, width))

    def query_side(group):
        g_query, g_key, g_value, g_qrel, g_krel, g_dctx, g_lse = group
        total, near_pull, far_pull, window = relative_scores(
            g_query, g_key, g_krel, g_qrel, offset, full_len
        )
        scores = jnp.where(same_doc, total * score_scale, masked_score)
        weights_now = jnp.exp(scores - g_lse[..., None])
        prob_grad = jnp.einsum(
            "rgid,rgjd->rgij", g_dctx, g_value, preferred_element_type=jnp.float32
        )
        inner_sum = jnp.sum(weights_now * prob_grad, axis=-1)
        score_grad = (weights_now * (prob_grad - inner_sum[..., None])).astype(jnp.bfloat16)
        grad_wide = score_grad.astype(jnp.float32)
        near_grad = near_pull(grad_wide)[0]
        near_low = jnp.where(inner_cols, near_grad, 0.0).astype(jnp.bfloat16)
        near_ends = end_columns(near_grad)
        query_part = jnp.einsum(
            "rgij,rgjd->rgid", score_grad, g_key, preferred_element_type=jnp.float32
        )
        query_part = (
            query_part
            + jnp.einsum("rgib,gbd->rgid", near_low, g_krel, preferred_element_type=jnp.float32)
            + end_terms(near_ends, g_krel)
        )
        krel_part = with_ends(
            jnp.einsum("rgib,rgid->gbd", near_low, g_query, preferred_element_type=jnp.float32),
            end_rows(near_ends, g_query),
        )
        return (
            weights_now,
            score_grad,
            grad_wide,
            far_pull,
            window,
            inner_sum,
            query_part * score_scale,
            krel_part * score_scale,
        )

    query_groups = (
        head_queries,
        head_keys,
        head_values,
        rel_queries,
        rel_keys,
        head_context_grad,
        log_totals,
    )

    def all_grads(carry, group):
        weights_now, score_grad, grad_wide, far_pull, window, inner_sum, query_part, krel_part = (
            query_side(group)
        )
        g_query, g_key, g_value, g_qrel, g_krel, g_dctx, g_lse = group
        cross_grad, end_grad = far_pull(grad_wide)
        cross_low = cross_grad.astype(jnp.bfloat16)
        key_part = jnp.einsum(
            "rgij,rgid->rgjd", score_grad, g_query, preferred_element_type=jnp.float32
        )
        band_part = jnp.einsum(
            "rgmb,gbd->rgmd", cross_low, g_qrel, preferred_element_type=jnp.float32
        )
        key_part = (
            key_part
            + unband(band_part, offset, full_len, buckets // 2)
            + end_terms(end_grad, g_qrel)
        )
        value_part = jnp.einsum(
            "rgij,rgid->rgjd",
            weights_now.astype(jnp.bfloat16),
            g_dctx,
            preferred_element_type=jnp.float32,
        )
        qrel_part = with_ends(
            jnp.einsum("rgmb,rgmd->gbd", cross_low, window, preferred_element_type=jnp.float32),
            end_rows(end_grad, g_key),
        )
        return (
            carry,
            (query_part, key_part * score_scale, value_part, qrel_part * score_scale, krel_part),
        )

    unused, (dq_groups, dk_groups, dv_groups, dqrel_groups, dkrel_groups) = lax.scan(
        all_grads, None, query_groups
    )
    key_sum, value_sum = (
        lax.psum_scatter(join_heads(dk_groups), "seq", scatter_dimension=0, tiled=True),
        lax.psum_scatter(join_heads(dv_groups), "seq", scatter_dimension=0, tiled=True),
    )
    key_grads = key_sum.reshape(tokens_here, width).astype(jnp.bfloat16)
    value_grads = value_sum.reshape(tokens_here, width).astype(jnp.bfloat16)
    query_grads = join_heads(dq_groups).reshape(tokens_here, width).astype(jnp.bfloat16)
    qrel_grad = join_table(dqrel_groups)
    krel_grad = join_table(dkrel_groups)
    input_grad = pre_grad + jnp.einsum(
        "ne,de->nd", query_grads, m_query, preferred_element_type=jnp.float32
    )
    input_grad = input_grad + jnp.einsum(
        "ne,de->nd", key_grads, m_key, preferred_element_type=jnp.float32
    )
    input_grad = input_grad + jnp.einsum(
        "ne,de->nd", value_grads, m_value, preferred_element_type=jnp.float32
    )
    query_whole = jnp.einsum(
        "nd,ne->de", flat_input, query_grads, preferred_element_type=jnp.float32
    ) + jnp.einsum(
        "bd,be->de", table, qrel_grad, precision=highest_prec, preferred_element_type=jnp.float32
    )
    key_whole = jnp.einsum(
        "nd,ne->de", flat_input, key_grads, preferred_element_type=jnp.float32
    ) + jnp.einsum(
        "bd,be->de", table, krel_grad, precision=highest_prec, preferred_element_type=jnp.float32
    )
    value_whole = jnp.einsum(
        "nd,ne->de", flat_input, value_grads, preferred_element_type=jnp.float32
    )
    table_whole = jnp.einsum(
        "be,de->bd", qrel_grad, m_query, precision=highest_prec, preferred_element_type=jnp.float32
    ) + jnp.einsum(
        "be,de->bd", krel_grad, m_key, precision=highest_prec, preferred_element_type=jnp.float32
    )
    bias_whole = jnp.stack(
        [
            jnp.sum(query_grads.astype(jnp.float32), axis=0) + jnp.sum(qrel_grad, axis=0),
            jnp.sum(key_grads.astype(jnp.float32), axis=0) + jnp.sum(krel_grad, axis=0),
            jnp.sum(value_grads.astype(jnp.float32), axis=0),
            jnp.sum(pre_grad, axis=0),
        ]
    )
    gain_whole = jnp.stack([gain1_grad, gain2_grad])
    shift_whole = jnp.stack([shift1_grad, shift2_grad])
    downb_whole = jnp.sum(mixed_grad, axis=0)
    seq_parts = (
        lax.psum_scatter(query_whole, "seq", scatter_dimension=0, tiled=True),
        lax.psum_scatter(key_whole, "seq", scatter_dimension=0, tiled=True),
        lax.psum_scatter(value_whole, "seq", scatter_dimension=0, tiled=True),
        lax.psum_scatter(mix_whole, "seq", scatter_dimension=0, tiled=True),
        lax.psum_scatter(table_whole, "seq", scatter_dimension=0, tiled=True),
        lax.psum_scatter(bias_whole, "seq", scatter_dimension=1, tiled=True),
        lax.psum_scatter(gain_whole, "seq", scatter_dimension=1, tiled=True),
        lax.psum_scatter(shift_whole, "seq", scatter_dimension=1, tiled=True),
        lax.psum_scatter(downb_whole, "seq", scatter_dimension=0, tiled=True),
    )
    batch_parts = (
        lax.psum_scatter(seq_parts[0], "batch", scatter_dimension=1, tiled=True),
        lax.psum_scatter(seq_parts[1], "batch", scatter_dimension=1, tiled=True),
        lax.psum_scatter(seq_parts[2], "batch", scatter_dimension=1, tiled=True),
        lax.psum_scatter(seq_parts[3], "batch", scatter_dimension=1, tiled=True),
        lax.psum_scatter(seq_parts[4], "batch", scatter_dimension=1, tiled=True),
        lax.psum_scatter(up_part, "batch", scatter_dimension=0, tiled=True),
        lax.psum_scatter(down_part, "batch", scatter_dimension=1, tiled=True),
    )
    small_parts = lax.psum(
        (seq_parts[5], seq_parts[6], seq_parts[7], seq_parts[8], upb_part), "batch"
    )
    layer_output = jnp.swapaxes(output.reshape(local_len, rows, width), 0, 1).astype(jnp.bfloat16)
    input_back = jnp.swapaxes(input_grad.reshape(local_len, rows, width), 0, 1)
    return (
        layer_output,
        input_back,
        batch_parts[0],
        batch_parts[1],
        batch_parts[2],
        batch_parts[3],
        batch_parts[4],
        small_parts[0],
        small_parts[1],
        small_parts[2],
        batch_parts[5],
        small_parts[4],
        batch_parts[6],
        small_parts[3],
    )


def solution(mesh):
    return jax.shard_map(
        body,
        mesh=mesh,
        in_specs=(
            P("batch", "seq", None),
            P("batch", "seq"),
            P("seq", "batch"),
            P("seq", "batch"),
            P("seq", "batch"),
            P("seq", "batch"),
            P("seq", "batch"),
            P(None, "seq"),
            P(None, "seq"),
            P(None, "seq"),
            P(None, "seq"),
            P("seq"),
            P("seq", None),
            P("seq"),
            P("batch", "seq", None),
        ),
        out_specs=(
            P("batch", "seq", None),
            P("batch", "seq", None),
            P("seq", "batch"),
            P("seq", "batch"),
            P("seq", "batch"),
            P("seq", "batch"),
            P("seq", "batch"),
            P(None, "seq"),
            P(None, "seq"),
            P(None, "seq"),
            P("batch", "seq"),
            P("seq"),
            P("seq", "batch"),
            P("seq"),
        ),
        check_vma=False,
    )
```

profile of v0, /device:TPU:0, one launch (start us, length us, event | category | flops | bytes accessed | tf_op | source)
XLA Modules:
  0.0 1493.4 jit_solution(9989885892650190141)
XLA Ops:
  8.3 10.2 all_gather.66
  38.6 12.0 all-gather.3
  53.7 13.5 all-gather.18.cloned.1.call-done
  79.2 10.6 all-gather
  89.8 8.7 all-gather.5
  98.6 10.2 all-gather.6
  117.6 15.7 %all_gather.65 = bf16[512,768]{1,0:T(8,128)(2,1)S(1)} all-gather(bf16[64,768]{1,0:T(8,128)(2,1)S(1)} %bitcast.683), channel_id=1, replica_groups=mesh['batch'=4,'seq'=8] {'seq'}, dimensions={0}, use_global_device_ids=true | all-gather | bytes 884736 | tf_op jit(solution)/shard_map/all_gather | solution.py:197
  151.5 155.7 %while.36 = (s32[]{:T(128)}, bf16[6,1,2,128,64]{3,4,2,1,0:T(8,128)(2,1)}, f32[6,1,2,128]{3,2,1,0:T(2,128)S(1)}, bf16[6,1,2,128,64]{3,4,2,1,0:T(8,128)(2,1)}, bf1...) while((s32[]{:T(128)}, ...), condition=%wide.region_3.4_spmd.clone, body=%wide.region_0.3_spmd.clone.sunk | while | flops 172753792 | bytes 46621800 | solution.py:256
  310.2 22.9 %all-gather.24.cloned.1.call-done = bf16[1024,768]{1,0:T(8,128)(2,1)} async-done(((bf16[128,768]{1,0:T(8,128)(2,1)}), bf16[1024,768]{1,0:T(8,128)(2,1)}) %all-gather.24.cloned.1.call-update) | async-done | bytes 1572880 | tf_op jit(solution)/shard_map/all_gather | solution.py:271
  346.2 15.4 %all-reduce.19 = bf16[768]{0:T(1024)(128)(2,1)S(1)} all-reduce(bf16[768]{0:T(1024)(128)(2,1)S(1)} %dynamic-update-slice), channel_id=1, replica_groups=mesh['batch'=4,'seq'=8] {'seq'}, use_global_device_ids=true, to_apply=%add.19 | all-reduce | flops 768 | bytes 3072
  361.6 22.2 %reduce-scatter.36.cloned.1.call-done = f32[128,768]{1,0:T(8,128)} async-done(((f32[1024,768]{1,0:T(8,128)}), f32[128,768]{1,0:T(8,128)}) %reduce-scatter.36.cloned.1.call-update) | async-done | bytes 393232 | tf_op jit(solution)/shard_map/reduce_scatter | solution.py:274
  388.4 24.5 %all-gather.26.cloned.1.call-done = bf16[1024,768]{1,0:T(8,128)(2,1)} async-done(((bf16[128,768]{1,0:T(8,128)(2,1)}), bf16[1024,768]{1,0:T(8,128)(2,1)}) %all-gather.26.cloned.1.call-update) | async-done | bytes 1572880 | tf_op jit(solution)/shard_map/all_gather | solution.py:271
  420.1 39.6 %reduce-scatter.38.cloned.1.call-done = f32[128,768]{1,0:T(8,128)} async-done(((f32[1024,768]{1,0:T(8,128)}), f32[128,768]{1,0:T(8,128)}) %reduce-scatter.38.cloned.1.call-update) | async-done | bytes 393232 | tf_op jit(solution)/shard_map/reduce_scatter | solution.py:274
  463.8 453.8 %while.37 = (s32[]{:T(128)}, bf16[6,1,2,128,64]{3,4,2,1,0:T(8,128)(2,1)}, f32[6,1,2,1024,64]{3,4,2,1,0:T(8,128)}, f32[6,1,2,1024,64]{3,4,2,1,0:T(8,128)}, f32[6,...) while((s32[]{:T(128)}, ...), condition=%wide.region_20.21_spmd.clone, body=%wide.region_14.20_spmd.clone.sunk | while | flops 487253888 | bytes 111815504 | solution.py:398
  946.6 15.1 %reduce-scatter.40.cloned.1.call-done = f32[128,1,768]{0,2,1:T(8,128)} async-done(((f32[1024,1,768]{0,2,1:T(8,128)}), f32[128,1,768]{0,2,1:T(8,128)}) %reduce-scatter.40.cloned.1.call-update) | async-done | bytes 393232 | tf_op jit(solution)/shard_map/reduce_scatter | solution.py:402
  968.5 35.0 %reduce-scatter.42.cloned.1.call-done = f32[128,1,768]{0,2,1:T(8,128)} async-done(((f32[1024,1,768]{0,2,1:T(8,128)}), f32[128,1,768]{0,2,1:T(8,128)}) %reduce-scatter.42.cloned.1.call-update) | async-done | bytes 393232 | tf_op jit(solution)/shard_map/reduce_scatter | solution.py:403
  1012.6 26.8 %reduce-scatter.52.cloned.1.call-done = f32[64,768]{1,0:T(8,128)} async-done(((f32[512,768]{1,0:T(8,128)}), f32[64,768]{1,0:T(8,128)}) %reduce-scatter.52.cloned.1.call-update) | async-done | bytes 196624 | tf_op jit(solution)/shard_map/reduce_scatter | solution.py:453
  1041.2 35.9 %reduce-scatter.50.cloned.1.call-done = f32[96,768]{1,0:T(8,128)} async-done(((f32[768,768]{1,0:T(8,128)}), f32[96,768]{1,0:T(8,128)}) %reduce-scatter.50.cloned.1.call-update) | async-done | bytes 294928 | tf_op jit(solution)/shard_map/reduce_scatter | solution.py:452
  1081.4 33.7 %reduce-scatter.58.cloned.1.call-done = f32[96,768]{1,0:T(8,128)} async-done(((f32[768,768]{1,0:T(8,128)}), f32[96,768]{1,0:T(8,128)}) %reduce-scatter.58.cloned.1.call-update) | async-done | bytes 294928
  1119.5 33.8 %reduce-scatter.60.cloned.1.call-done = f32[96,768]{1,0:T(8,128)} async-done(((f32[768,768]{1,0:T(8,128)}), f32[96,768]{1,0:T(8,128)}) %reduce-scatter.60.cloned.1.call-update) | async-done | bytes 294928
  1155.3 36.2 %reduce-scatter.62.cloned.1.call-done = f32[96,768]{1,0:T(8,128)} async-done(((f32[768,768]{1,0:T(8,128)}), f32[96,768]{1,0:T(8,128)}) %reduce-scatter.62.cloned.1.call-update) | async-done | bytes 294928
  1201.3 14.8 all-reduce.20
  1224.6 30.5 %reduce-scatter.70.cloned.1.call-done = f32[96,2]{1,0:T(8,128)} async-done(((f32[768,2]{1,0:T(8,128)}), f32[96,2]{1,0:T(8,128)}) %reduce-scatter.70.cloned.1.call-update) | async-done | bytes 784
  1256.0 24.7 %reduce-scatter.66.cloned.1.call-done = f32[192,64]{1,0:T(8,128)} async-done(((f32[768,64]{1,0:T(8,128)}), f32[192,64]{1,0:T(8,128)}) %reduce-scatter.66.cloned.1.call-update) | async-done | bytes 49168
  1282.3 25.9 %reduce-scatter.64.cloned.1.call-done = f32[192,96]{1,0:T(8,128)} async-done(((f32[768,96]{1,0:T(8,128)}), f32[192,96]{1,0:T(8,128)}) %reduce-scatter.64.cloned.1.call-update) | async-done | bytes 73744
  1309.8 25.9 %reduce-scatter.44.cloned.1.call-done = f32[96,192]{0,1:T(8,128)} async-done(((f32[96,768]{0,1:T(8,128)}), f32[96,192]{0,1:T(8,128)}) %reduce-scatter.44.cloned.1.call-update) | async-done | bytes 73744 | tf_op jit(solution)/shard_map/reduce_scatter | solution.py:460
  1340.4 28.7 %reduce-scatter.68.cloned.1.call-done = f32[96,4]{1,0:T(8,128)} async-done(((f32[768,4]{1,0:T(8,128)}), f32[96,4]{1,0:T(8,128)}) %reduce-scatter.68.cloned.1.call-update) | async-done | bytes 1552
  1370.0 10.6 all-reduce.21
  1380.6 14.1 reduce-scatter.46.cloned.1.call-done
  1396.3 25.9 %reduce-scatter.48.cloned.1.call-done = f32[96,192]{0,1:T(8,128)} async-done(((f32[96,768]{0,1:T(8,128)}), f32[96,192]{0,1:T(8,128)}) %reduce-scatter.48.cloned.1.call-update) | async-done | bytes 73744 | tf_op jit(solution)/shard_map/reduce_scatter | solution.py:462
  1423.8 30.5 %reduce-scatter.54.cloned.1.call-done = f32[192,384]{1,0:T(8,128)} async-done(((f32[768,384]{1,0:T(8,128)}), f32[192,384]{1,0:T(8,128)}) %reduce-scatter.54.cloned.1.call-update) | async-done | bytes 294928 | tf_op jit(solution)/shard_map/reduce_scatter | solution.py:465
  1454.3 32.1 %reduce-scatter.56.cloned.1.call-done = f32[384,192]{0,1:T(8,128)} async-done(((f32[384,768]{0,1:T(8,128)}), f32[384,192]{0,1:T(8,128)}) %reduce-scatter.56.cloned.1.call-update) | async-done | bytes 294928 | tf_op jit(solution)/shard_map/reduce_scatter | solution.py:466
  (1148 shorter events, 786.4 us)
Async XLA Ops:
  7.2 325.9 %copy-start = (bf16[768,384]{1,0:T(8,128)(2,1)S(1)}, bf16[768,384]{1,0:T(8,128)(2,1)}, u32[]{:S(2)}) copy-start(bf16[768,384]{1,0:T(8,128)(2,1)} %param.29) | copy-start | bytes 1769476
  7.2 44.1 %all-gather.20.cloned.1.call-start = ((), (), s32[]{:S(2)}) async-start(), calls=%async_computation.21 | async-start | bytes 1327104 | tf_op jit(solution)/shard_map/all_gather | solution.py:195
  19.3 47.9 %all-gather.18.cloned.1.call-start = ((), (), s32[]{:S(2)}) async-start(), calls=%async_computation.20 | async-start | bytes 1327104 | tf_op jit(solution)/shard_map/all_gather | solution.py:194
  29.8 104.2 %all-gather.16.cloned.1.call-start = ((), (), s32[]{:S(2)}) async-start(), calls=%async_computation.19 | async-start | bytes 1327104 | tf_op jit(solution)/shard_map/all_gather | solution.py:193
  38.5 107.0 %all-gather.30.cloned.1.call-start = ((), (), s32[]{:S(2)}) async-start(), calls=%async_computation.37 | async-start | bytes 1769472 | tf_op jit(solution)/shard_map/all_gather | solution.py:223
  53.7 94.5 %all-gather.28.cloned.1.call-start = ((), (), s32[]{:S(2)}) async-start(), calls=%async_computation.36 | async-start | bytes 1769472 | tf_op jit(solution)/shard_map/all_gather | solution.py:222
  69.5 237.7 %all-gather.22.cloned.1.call-start = ((), (), s32[]{:S(2)}) async-start(), calls=%async_computation.22 | async-start | bytes 1327104 | tf_op jit(solution)/shard_map/all_gather | solution.py:196
  79.1 254.0 %all-gather.24.cloned.1.call-start = ((), (), s32[]{:S(2)}) async-start(), calls=%async_computation.23 | async-start | bytes 1769472 | tf_op jit(solution)/shard_map/all_gather | solution.py:271
  151.5 155.7 %copy-start.47 = (f32[768]{0:T(1024)S(1)}, f32[768]{0:T(1024)}, u32[]{:S(2)}) copy-start(f32[768]{0:T(1024)} %get-tuple-element.643) | copy-start | bytes 9220
  310.1 73.8 %reduce-scatter.36.cloned.1.call-start = ((), (), s32[]{:S(2)}) async-start(), calls=%async_computation.24 | async-start | bytes 3538944 | tf_op jit(solution)/shard_map/reduce_scatter | solution.py:274
  344.1 68.8 %all-gather.26.cloned.1.call-start = ((), (), s32[]{:S(2)}) async-start(), calls=%async_computation.25 | async-start | bytes 1769472 | tf_op jit(solution)/shard_map/all_gather | solution.py:271
  388.4 71.2 %reduce-scatter.38.cloned.1.call-start = ((), (), s32[]{:S(2)}) async-start(), calls=%async_computation.26 | async-start | bytes 3538944 | tf_op jit(solution)/shard_map/reduce_scatter | solution.py:274
  420.0 541.8 %reduce-scatter.40.cloned.1.call-start = ((), (), s32[]{:S(2)}) async-start(), calls=%async_computation.27 | async-start | bytes 3538944 | tf_op jit(solution)/shard_map/reduce_scatter | solution.py:402
  917.6 85.9 %reduce-scatter.42.cloned.1.call-start = ((), (), s32[]{:S(2)}) async-start(), calls=%async_computation.28 | async-start | bytes 3538944 | tf_op jit(solution)/shard_map/reduce_scatter | solution.py:403
  918.2 121.1 %reduce-scatter.52.cloned.1.call-start = ((), (), s32[]{:S(2)}) async-start(), calls=%async_computation.33 | async-start | bytes 1769472 | tf_op jit(solution)/shard_map/reduce_scatter | solution.py:453
  929.7 147.4 %reduce-scatter.50.cloned.1.call-start = ((), (), s32[]{:S(2)}) async-start(), calls=%async_computation.32 | async-start | bytes 2654208 | tf_op jit(solution)/shard_map/reduce_scatter | solution.py:452
  932.7 182.4 %reduce-scatter.58.cloned.1.call-start = ((), (), s32[]{:S(2)}) async-start(), calls=%async_computation.38 | async-start | bytes 2654208
  941.3 212.0 %reduce-scatter.60.cloned.1.call-start = ((), (), s32[]{:S(2)}) async-start(), calls=%async_computation.39 | async-start | bytes 2654208
  968.5 223.0 %reduce-scatter.62.cloned.1.call-start = ((), (), s32[]{:S(2)}) async-start(), calls=%async_computation.40 | async-start | bytes 2654208
  1009.5 214.2 %reduce-scatter.72.cloned.1.call-start = ((), (), s32[]{:S(2)}) async-start(), calls=%async_computation.45 | async-start | bytes 442368
  1011.5 243.6 %reduce-scatter.70.cloned.1.call-start = ((), (), s32[]{:S(2)}) async-start(), calls=%async_computation.44 | async-start | bytes 442368
  1012.5 268.2 %reduce-scatter.66.cloned.1.call-start = ((), (), s32[]{:S(2)}) async-start(), calls=%async_computation.42 | async-start | bytes 491520
  1041.2 267.0 %reduce-scatter.64.cloned.1.call-start = ((), (), s32[]{:S(2)}) async-start(), calls=%async_computation.41 | async-start | bytes 491520
  1079.0 256.7 %reduce-scatter.44.cloned.1.call-start = ((), (), s32[]{:S(2)}) async-start(), calls=%async_computation.29 | async-start | bytes 491520 | tf_op jit(solution)/shard_map/reduce_scatter | solution.py:460
  1117.0 252.1 %reduce-scatter.68.cloned.1.call-start = ((), (), s32[]{:S(2)}) async-start(), calls=%async_computation.43 | async-start | bytes 442368
  1119.5 275.2 %reduce-scatter.46.cloned.1.call-start = ((), (), s32[]{:S(2)}) async-start(), calls=%async_computation.30 | async-start | bytes 491520 | tf_op jit(solution)/shard_map/reduce_scatter | solution.py:461
  1155.2 267.0 %reduce-scatter.48.cloned.1.call-start = ((), (), s32[]{:S(2)}) async-start(), calls=%async_computation.31 | async-start | bytes 491520 | tf_op jit(solution)/shard_map/reduce_scatter | solution.py:462
  1193.4 260.9 %reduce-scatter.54.cloned.1.call-start = ((), (), s32[]{:S(2)}) async-start(), calls=%async_computation.34 | async-start | bytes 1474560 | tf_op jit(solution)/shard_map/reduce_scatter | solution.py:465
  1197.0 289.4 %reduce-scatter.56.cloned.1.call-start = ((), (), s32[]{:S(2)}) async-start(), calls=%async_computation.35 | async-start | bytes 1474560 | tf_op jit(solution)/shard_map/reduce_scatter | solution.py:466
  1217.5 121.6 %copy-start.24 = (bf16[768,768]{1,0:T(8,128)(2,1)S(1)}, bf16[768,768]{1,0:T(8,128)(2,1)}, u32[]{:S(2)}) copy-start(bf16[768,768]{1,0:T(8,128)(2,1)} %all-gather.20.cloned.1.call-done) | copy-start | bytes 3538948
  1217.5 121.6 %copy-start.26 = (f32[128,1,768]{0,2,1:T(8,128)S(1)}, f32[128,1,768]{0,2,1:T(8,128)}, u32[]{:S(2)}) copy-start(f32[128,1,768]{0,2,1:T(8,128)} %reduce-scatter.42.cloned.1.call-done) | copy-start | bytes 1179652
  1337.4 149.0 %copy-start.1 = (bf16[768,384]{1,0:T(8,128)(2,1)S(1)}, bf16[768,384]{1,0:T(8,128)(2,1)}, u32[]{:S(2)}) copy-start(bf16[768,384]{1,0:T(8,128)(2,1)} %param.29) | copy-start | bytes 1769476
  (144 other events, 907.3 us)
Sparse Core Ops, SparseCore 0:
  19.4 23.0 all-gather.19
  44.7 22.4 all-gather.17
  69.4 22.4 all-gather.15
  94.0 24.9 all-gather.29
  121.0 24.1 all-gather.27
  147.3 22.3 all-gather.21
  310.2 22.8 all-gather.23
  344.2 39.5 reduce-scatter.35
  388.5 24.4 all-gather.25
  420.1 39.4 reduce-scatter.37
  917.7 43.9 reduce-scatter.39
  963.9 39.5 reduce-scatter.41
  1005.8 33.4 reduce-scatter.51
  1041.5 35.5 reduce-scatter.49
  1079.3 35.8 reduce-scatter.57
  1117.3 35.9 reduce-scatter.59
  1155.5 35.9 reduce-scatter.61
  1193.6 30.0 reduce-scatter.71
  1226.0 29.0 reduce-scatter.69
  1257.7 22.8 reduce-scatter.65
  1283.5 24.6 reduce-scatter.63
  1311.0 24.7 reduce-scatter.43
  1338.0 31.0 reduce-scatter.67
  1371.8 22.8 reduce-scatter.45
  1397.5 24.6 reduce-scatter.47
  1425.6 28.6 reduce-scatter.53
  1457.6 28.6 reduce-scatter.55
where the time goes:
time: 1510 us; the launch traced here: 1490 us
  waiting for transfers between devices  585 us (39%)
  local copies, waits for them, and re-layouts  426 us (28%)
  matrix products  249 us (16%)
  blocking collectives  142 us (9%)
  other arithmetic  69.4 us (5%)
  between operations  16.8 us (1%)
    unnamed x35, waiting for transfers between devices  221 us
    reduce_scatter x2, waiting for transfers between devices, hidden_sums(): lax.psum_scatter(make_term(jnp.int32(0), tokens_here * lax.axis_size('seq...  61.8 us
    transpose x12, local copies, waits for them, and re-layouts, far_place(): turned = jnp.swapaxes(cross, -1, -2).reshape(lead + (buckets * band_len,))  61.1 us
    all_gather x2, waiting for transfers between devices, spread_rows(): return lax.all_gather(rows_low, 'seq', axis=0, tiled=True)  47.5 us
    unnamed x126, local copies, waits for them, and re-layouts  41.8 us
    pad x18, local copies, waits for them, and re-layouts, far_place(): turned = jnp.pad(turned, lead_pad + [(0, buckets)])  41.3 us
    dynamic_update_slice x6, local copies, waits for them, and re-layouts, near_skew(): lax.dynamic_slice_in_dim(spread, full_len + span - 1 - offset, full_len,...  37 us
    reduce_scatter x1, waiting for transfers between devices, body(): lax.psum_scatter(mix_whole, 'seq', scatter_dimension=0, tiled=True)  35.9 us
  transfers between devices with their start and end apart: 27, of which 22 were waited for; matrix products, arithmetic and copies ran while one was open for 17% of the time, Pallas kernels for 0%

commit v1 on v0

--- a/solution.py
+++ b/solution.py
@@ -3,6 +3,8 @@
 import jax
 import jax.numpy as jnp
 from jax import lax
+from jax.experimental import pallas as pl
+from jax.experimental.pallas import tpu as pltpu
 from jax.sharding import PartitionSpec as P
 
 DH = 64
@@ -161,6 +163,1030 @@
     )
 
 
+BLOCK = 128
+
+
+def dot_nn(a, b):
+    return lax.dot_general(a, b, (((1,), (0,)), ((), ())), preferred_element_type=jnp.float32)
+
+
+def dot_nt(a, b):
+    return lax.dot_general(a, b, (((1,), (1,)), ((), ())), preferred_element_type=jnp.float32)
+
+
+def dot_tn(a, b):
+    return lax.dot_general(a, b, (((0,), (0,)), ((), ())), preferred_element_type=jnp.float32)
+
+
+def turn_matrix(buckets):
+    row = lax.broadcasted_iota(jnp.int32, (buckets, buckets), 0)
+    col = lax.broadcasted_iota(jnp.int32, (buckets, buckets), 1)
+    return (row + col == buckets - 1).astype(jnp.bfloat16)
+
+
+def skew_band(product):
+    count, buckets = product.shape
+    row = lax.broadcasted_iota(jnp.int32, (count, BLOCK), 0)
+    lane = lax.broadcasted_iota(jnp.int32, (count, BLOCK), 1)
+    edge = jnp.where(row + lane <= BLOCK - 2, product[:, buckets - 1 :], product[:, 0:1])
+    wide = jnp.concatenate([product, edge], axis=1)
+    return pltpu.roll(wide, 1, 1, stride=1, stride_axis=0)
+
+
+def skew_back(turned, buckets):
+    return pltpu.roll(turned, turned.shape[1] - BLOCK, 1, stride=1, stride_axis=0)[:, :buckets]
+
+
+def attend_kernel(
+    first_ref,
+    x_ref,
+    w_ref,
+    bias_ref,
+    table_ref,
+    segc_ref,
+    segr_ref,
+    q_ref,
+    k_ref,
+    v_ref,
+    qrev_ref,
+    krev_ref,
+    p_ref,
+    ctx_ref,
+    place_ref,
+    wide_ref,
+    ends_ref,
+    held_ref,
+):
+    full_len = x_ref.shape[0]
+    buckets = table_ref.shape[0]
+    blocks = full_len // BLOCK
+    span = buckets // 2
+    side = span // BLOCK
+    band_width = buckets + BLOCK
+    band_blocks = band_width // BLOCK
+    group = 2 * DH
+    scale = 1.0 / math.sqrt(3.0 * DH)
+    units = p_ref.shape[0]
+    proj = (dot_nn(x_ref[...], w_ref[...]) + bias_ref[...]).astype(jnp.bfloat16)
+    rel = (dot_nn(table_ref[...], w_ref[:, : 2 * group]) + bias_ref[:, : 2 * group]).astype(
+        jnp.bfloat16
+    )
+    rel = dot_nn(turn_matrix(buckets), rel).astype(jnp.bfloat16)
+    for slot in range(2):
+        lo, hi = slot * DH, (slot + 1) * DH
+        q_ref[slot] = proj[:, lo:hi]
+        k_ref[slot] = proj[:, group + lo : group + hi]
+        v_ref[slot] = proj[:, 2 * group + lo : 2 * group + hi]
+        qrev_ref[slot] = rel[:, lo:hi]
+        krev_ref[slot] = rel[:, group + lo : group + hi]
+    held_ref[...] = jnp.zeros_like(held_ref)
+    for slot in range(2):
+        ends_ref[slot, 0] = dot_nt(qrev_ref[slot, 0:16], k_ref[slot])
+        ends_ref[slot, 1] = dot_nt(qrev_ref[slot, buckets - 16 : buckets], k_ref[slot])
+
+        def key_block(kb, carry):
+            rows = k_ref[slot, pl.ds(pl.multiple_of(kb * BLOCK, BLOCK), BLOCK)]
+            band = skew_band(dot_nt(rows, qrev_ref[slot]))
+            for e in range(band_blocks):
+                place_ref[
+                    slot,
+                    kb + e,
+                    :,
+                    (band_blocks - 1 - e) * BLOCK : (band_blocks - e) * BLOCK,
+                ] = band[:, e * BLOCK : (e + 1) * BLOCK].T
+            return carry
+
+        lax.fori_loop(0, blocks, key_block, 0)
+
+    first = first_ref[0]
+
+    def unit(u, carry):
+        g = u + first
+        slot = g // blocks
+        qb = g % blocks
+        start = pl.multiple_of(qb * BLOCK, BLOCK)
+        rows = q_ref[slot, pl.ds(start, BLOCK)]
+        own = dot_nt(rows, krev_ref[slot])
+        band = skew_band(own) + place_ref[slot, qb + side]
+        wide_ref[:, pl.ds(start, band_width)] = band
+        content = dot_nt(rows, k_ref[slot])
+        lane = lax.broadcasted_iota(jnp.int32, (BLOCK, full_len), 1)
+        near = jnp.where(
+            lane < start - span,
+            own[:, 0:1] + ends_ref[slot, 1, 15:16],
+            jnp.where(
+                lane >= start + band_width - span,
+                own[:, buckets - 1 :] + ends_ref[slot, 0, 0:1],
+                wide_ref[:, span : span + full_len],
+            ),
+        )
+        same = segc_ref[pl.ds(start, BLOCK)] == segr_ref[...]
+        scores = jnp.where(same, (content + near) * scale, masked_score)
+        highest = jnp.max(scores, axis=-1, keepdims=True)
+        exponent = jnp.exp(scores - highest)
+        total = jnp.sum(exponent, axis=-1, keepdims=True)
+        probs = (exponent / total).astype(jnp.bfloat16)
+        p_ref[u] = probs
+        held_ref[slot, pl.ds(start, BLOCK)] = dot_nn(probs, v_ref[slot]).astype(jnp.bfloat16)
+        return carry
+
+    lax.fori_loop(0, units, unit, 0)
+    ctx_ref[...] = jnp.concatenate([held_ref[0], held_ref[1]], axis=1)
+
+
+def attend(first, x_all, w_cat, bias_cat, table, seg_col, seg_row):
+    full_len, width = x_all.shape
+    buckets = table.shape[0]
+    blocks = full_len // BLOCK
+    units = 3 * blocks // 2
+    band_width = buckets + BLOCK
+    low, wide = jnp.bfloat16, jnp.float32
+    pad_blocks = blocks + band_width // BLOCK - 1
+    return pl.pallas_call(
+        attend_kernel,
+        out_shape=(
+            jax.ShapeDtypeStruct((2, full_len, DH), low),
+            jax.ShapeDtypeStruct((2, full_len, DH), low),
+            jax.ShapeDtypeStruct((2, full_len, DH), low),
+            jax.ShapeDtypeStruct((2, buckets, DH), low),
+            jax.ShapeDtypeStruct((2, buckets, DH), low),
+            jax.ShapeDtypeStruct((units, BLOCK, full_len), low),
+            jax.ShapeDtypeStruct((full_len, 2 * DH), low),
+        ),
+        in_specs=[pl.BlockSpec(memory_space=pltpu.SMEM)]
+        + [pl.BlockSpec(memory_space=pltpu.VMEM)] * 6,
+        out_specs=[pl.BlockSpec(memory_space=pltpu.VMEM)] * 7,
+        scratch_shapes=[
+            pltpu.VMEM((2, pad_blocks, BLOCK, band_width), wide),
+            pltpu.VMEM((BLOCK, full_len + buckets), wide),
+            pltpu.VMEM((2, 2, 16, full_len), wide),
+            pltpu.VMEM((2, full_len, DH), low),
+        ],
+        compiler_params=pltpu.CompilerParams(vmem_limit_bytes=60 * 1024 * 1024),
+        name="attend",
+    )(first, x_all, w_cat, bias_cat, table, seg_col, seg_row)
+
+
+def attend_back_kernel(
+    first_ref,
+    q_ref,
+    k_ref,
+    v_ref,
+    qrev_ref,
+    krev_ref,
+    p_ref,
+    dctx_ref,
+    dcat_ref,
+    rel_ref,
+    sum_ref,
+    heads_ref,
+    wide_ref,
+    low_ref,
+    place_ref,
+    dq_ref,
+    dkt_ref,
+    dvt_ref,
+    far_ref,
+    dkr_ref,
+    dqr_ref,
+):
+    full_len = q_ref.shape[1]
+    buckets = qrev_ref.shape[1]
+    blocks = full_len // BLOCK
+    span = buckets // 2
+    side = span // BLOCK
+    band_width = buckets + BLOCK
+    band_blocks = band_width // BLOCK
+    scale = 1.0 / math.sqrt(3.0 * DH)
+    units = p_ref.shape[0]
+    for ref in (wide_ref, low_ref, place_ref, dq_ref, dkt_ref, dvt_ref, far_ref, dkr_ref, dqr_ref):
+        ref[...] = jnp.zeros_like(ref)
+    for slot in range(2):
+        heads_ref[slot] = dctx_ref[:, slot * DH : (slot + 1) * DH]
+    first = first_ref[0]
+    turn = turn_matrix(BLOCK)
+    place8 = lax.broadcasted_iota(jnp.int32, (8, full_len), 0)
+
+    def unit(u, carry):
+        g = u + first
+        slot = g // blocks
+        qb = g % blocks
+        start = pl.multiple_of(qb * BLOCK, BLOCK)
+        rows = q_ref[slot, pl.ds(start, BLOCK)]
+        grad = heads_ref[slot, pl.ds(start, BLOCK)]
+        probs = p_ref[u]
+        wide_probs = probs.astype(jnp.float32)
+        prob_grad = dot_nt(grad, v_ref[slot])
+        inner = jnp.sum(wide_probs * prob_grad, axis=-1, keepdims=True)
+        low_grad = (wide_probs * (prob_grad - inner)).astype(jnp.bfloat16)
+        score_grad = low_grad.astype(jnp.float32)
+        wide_ref[:, span : span + full_len] = dot_nn(turn, low_grad)
+        low_ref[:, span : span + full_len] = low_grad
+        dvt_ref[slot] += dot_tn(grad, probs)
+        dkt_ref[slot] += dot_tn(rows, low_grad)
+        row = lax.broadcasted_iota(jnp.int32, (BLOCK, full_len), 0)
+        lane = lax.broadcasted_iota(jnp.int32, (BLOCK, full_len), 1)
+        gap = lane - row - start
+        right = jnp.where(gap > span, score_grad, 0.0)
+        left = jnp.where(gap < 1 - span, score_grad, 0.0)
+        end_right = jnp.sum(right, axis=-1, keepdims=True)
+        end_left = jnp.sum(left, axis=-1, keepdims=True)
+        far_right = jnp.sum(jnp.where(gap >= span, score_grad, 0.0), axis=0, keepdims=True)
+        far_left = jnp.sum(jnp.where(gap < -span, score_grad, 0.0), axis=0, keepdims=True)
+        far_ref[slot] += jnp.where(place8 == 0, far_right, jnp.where(place8 == 1, far_left, 0.0))
+        band = wide_ref[:, pl.ds(start, band_width)]
+        near = dot_nn(turn, skew_back(band, buckets).astype(jnp.bfloat16))
+        bucket = lax.broadcasted_iota(jnp.int32, (BLOCK, buckets), 1)
+        near = near + jnp.where(
+            bucket == 0, end_left, jnp.where(bucket == buckets - 1, end_right, 0.0)
+        )
+        near_low = near.astype(jnp.bfloat16)
+        dq = dot_nn(low_grad, k_ref[slot]) + dot_nn(near_low, krev_ref[slot])
+        dq_ref[slot, pl.ds(start, BLOCK)] = dq
+        dkr_ref[slot] += dot_tn(rows, near_low)
+        for e in range(band_blocks):
+            keys_at = pl.multiple_of(start + e * BLOCK, BLOCK)
+            place_ref[
+                slot, qb + e, :, (band_blocks - 1 - e) * BLOCK : (band_blocks - e) * BLOCK
+            ] = dot_nt(turn, low_ref[:, pl.ds(keys_at, BLOCK)])
+        return carry
+
+    lax.fori_loop(0, units, unit, 0)
+    parts_q, parts_k, parts_v = [], [], []
+    parts_r = [None] * 4
+    for slot in range(2):
+        far_low = far_ref[slot].astype(jnp.bfloat16)
+        mark = lax.broadcasted_iota(jnp.int32, (8, DH), 0)
+        ends = jnp.where(
+            mark == 0,
+            qrev_ref[slot, 0:1].astype(jnp.float32),
+            jnp.where(mark == 1, qrev_ref[slot, buckets - 1 : buckets].astype(jnp.float32), 0.0),
+        ).astype(jnp.bfloat16)
+        end_keys = dot_tn(ends, far_low)
+        end_rows = dot_nn(far_low, k_ref[slot])
+
+        whole_k = (dkt_ref[slot] + end_keys).T
+
+        def key_side(kb, carry):
+            start = pl.multiple_of(kb * BLOCK, BLOCK)
+            far = skew_back(place_ref[slot, kb + side], buckets).astype(jnp.bfloat16)
+            far = dot_nn(turn, far).astype(jnp.bfloat16)
+            keys = k_ref[slot, pl.ds(start, BLOCK)]
+            dqr_ref[slot] += dot_tn(keys, far)
+            dq_ref[2 + slot, pl.ds(start, BLOCK)] = dot_nn(far, qrev_ref[slot])
+            return carry
+
+        lax.fori_loop(0, blocks, key_side, 0)
+        parts_q.append((dq_ref[slot] * scale).astype(jnp.bfloat16))
+        parts_k.append(((dq_ref[2 + slot] + whole_k) * scale).astype(jnp.bfloat16))
+        parts_v.append(dvt_ref[slot].T.astype(jnp.bfloat16))
+        bucket = lax.broadcasted_iota(jnp.int32, (buckets, DH), 0)
+        qr = dqr_ref[slot].T + jnp.where(
+            bucket == 0, end_rows[0:1], jnp.where(bucket == buckets - 1, end_rows[1:2], 0.0)
+        )
+        dqr_out = qr * scale
+        dkr_out = dkr_ref[slot].T * scale
+        parts_r[slot] = dqr_out
+        parts_r[2 + slot] = dkr_out
+    dcat = jnp.concatenate(parts_q + parts_k + parts_v, axis=1)
+    dcat_ref[...] = dcat
+    rel = jnp.concatenate(parts_r, axis=1)
+    rel_ref[...] = dot_nn(turn_matrix(buckets), rel.astype(jnp.bfloat16)).astype(jnp.bfloat16)
+    rel_sum = jnp.sum(rel, axis=0, keepdims=True)
+    rel_sum = jnp.concatenate([rel_sum, jnp.zeros((1, 2 * DH), jnp.float32)], axis=1)
+    sum_ref[...] = jnp.sum(dcat.astype(jnp.float32), axis=0, keepdims=True) + rel_sum
+
+
+def attend_back(first, q, k, v, qrev, krev, probs, dctx):
+    full_len = q.shape[1]
+    buckets = qrev.shape[1]
+    blocks = full_len // BLOCK
+    band_width = buckets + BLOCK
+    low, wide = jnp.bfloat16, jnp.float32
+    pad_blocks = blocks + band_width // BLOCK - 1
+    return pl.pallas_call(
+        attend_back_kernel,
+        out_shape=(
+            jax.ShapeDtypeStruct((full_len, 6 * DH), low),
+            jax.ShapeDtypeStruct((buckets, 4 * DH), low),
+            jax.ShapeDtypeStruct((1, 6 * DH), wide),
+        ),
+        in_specs=[pl.BlockSpec(memory_space=pltpu.SMEM)]
+        + [pl.BlockSpec(memory_space=pltpu.VMEM)] * 7,
+        out_specs=[pl.BlockSpec(memory_space=pltpu.VMEM)] * 3,
+        scratch_shapes=[
+            pltpu.VMEM((2, full_len, DH), low),
+            pltpu.VMEM((BLOCK, full_len + buckets), wide),
+            pltpu.VMEM((BLOCK, full_len + buckets), low),
+            pltpu.VMEM((2, pad_blocks, BLOCK, band_width), wide),
+            pltpu.VMEM((4, full_len, DH), wide),
+            pltpu.VMEM((2, DH, full_len), wide),
+            pltpu.VMEM((2, DH, full_len), wide),
+            pltpu.VMEM((2, 8, full_len), wide),
+            pltpu.VMEM((2, DH, buckets), wide),
+            pltpu.VMEM((2, DH, buckets), wide),
+        ],
+        compiler_params=pltpu.CompilerParams(vmem_limit_bytes=60 * 1024 * 1024),
+        name="attend_back",
+    )(first, q, k, v, qrev, krev, probs, dctx)
+
+
+MESH = pl.DeviceIdType.MESH
+VMEM_SPEC = pl.BlockSpec(memory_space=pltpu.VMEM)
+ANY_SPEC = pl.BlockSpec(memory_space=pl.ANY)
+
+
+class Place:
+    def __init__(self):
+        self.batches = lax.axis_size("batch")
+        self.tokens = lax.axis_size("seq")
+        self.chips = self.tokens // 2
+        self.row = lax.axis_index("batch")
+        self.part = lax.axis_index("seq")
+        self.chip = self.part // 2
+        self.core = self.part % 2
+
+    def along_chips(self, k):
+        chip = lax.rem(self.chip + k, self.chips)
+        return chip, (self.row, 2 * chip + self.core)
+
+    def from_chips(self, k):
+        return lax.rem(self.chip + self.chips - k, self.chips)
+
+    def partner(self):
+        return (self.row, self.part + 1 - 2 * self.core)
+
+    def along_rows(self, k):
+        row = lax.rem(self.row + k, self.batches)
+        return row, (row, self.part)
+
+    def from_rows(self, k):
+        return lax.rem(self.row + self.batches - k, self.batches)
+
+    def along_seq(self, k):
+        part = lax.rem(self.part + k, self.tokens)
+        return part, (self.row, part)
+
+    def along_plane(self, k):
+        index = lax.rem(2 * self.row + self.core + k, 2 * self.batches)
+        row, core = index // 2, index % 2
+        return row, core, (row, 2 * self.chip + core)
+
+    def chip_peers(self):
+        return [self.along_chips(k)[1] for k in range(1, self.chips)]
+
+    def row_peers(self):
+        return [self.along_rows(k)[1] for k in range(1, self.batches)]
+
+    def cross_peers(self):
+        other = self.part + 1 - 2 * self.core
+        return [(self.along_rows(k)[0], other) for k in range(1, self.batches)]
+
+    def seq_peers(self):
+        return [self.along_seq(k)[1] for k in range(1, self.tokens)]
+
+    def plane_peers(self):
+        return [self.along_plane(k)[2] for k in range(1, 2 * self.batches)]
+
+
+def meet(peers):
+    barrier = pltpu.get_barrier_semaphore()
+    for peer in peers:
+        pl.semaphore_signal(barrier, inc=1, device_id=peer, device_id_type=MESH)
+    pl.semaphore_wait(barrier, len(peers))
+
+
+class Wires:
+    def __init__(self, send_sems, recv_sems, local_sems):
+        self.sems = (send_sems, recv_sems, local_sems)
+        self.used = [0, 0]
+        self.ends = []
+
+    def send(self, src, dst, peer):
+        k = self.used[0]
+        self.used[0] += 1
+        copy = pltpu.make_async_remote_copy(
+            src_ref=src,
+            dst_ref=dst,
+            send_sem=self.sems[0].at[k],
+            recv_sem=self.sems[1].at[k],
+            device_id=peer,
+            device_id_type=MESH,
+        )
+        copy.start()
+        self.ends.append(copy.wait_send)
+        return copy
+
+    def local(self, src, dst):
+        k = self.used[1]
+        self.used[1] += 1
+        copy = pltpu.make_async_copy(src, dst, self.sems[2].at[k])
+        copy.start()
+        return copy
+
+    def finish(self):
+        for end in self.ends:
+            end()
+
+
+def wire_scratch(sends, locals_count):
+    return [
+        pltpu.SemaphoreType.DMA((sends,)),
+        pltpu.SemaphoreType.DMA((sends,)),
+        pltpu.SemaphoreType.DMA((locals_count,)),
+    ]
+
+
+def comm_call(kernel, name, ident, out_shapes, inputs, sends, locals_count, scratch=()):
+    return pl.pallas_call(
+        kernel,
+        out_shape=tuple(out_shapes),
+        in_specs=[VMEM_SPEC] * len(inputs),
+        out_specs=tuple([ANY_SPEC] * len(out_shapes)),
+        scratch_shapes=list(scratch) + wire_scratch(sends, locals_count),
+        compiler_params=pltpu.CompilerParams(
+            collective_id=ident, has_side_effects=True, vmem_limit_bytes=40 * 1024 * 1024
+        ),
+        name=name,
+    )(*inputs)
+
+
+def like(array, *lead):
+    return jax.ShapeDtypeStruct(tuple(lead) + tuple(array.shape), array.dtype)
+
+
+def gather_kernel(
+    x_ref, qkv_ref, mt_ref, vec_ref, up_ref, down_ref,
+    xs_ref, qkvs_ref, mts_ref, vecs_ref, up2_ref, down2_ref, *sems,
+):
+    at = Place()
+    wires = Wires(*sems)
+    b, s, z, c = at.row, at.part, at.chip, at.core
+    off_diagonal = b != z
+    turned = (z, 2 * b + c)
+    barrier = pltpu.get_barrier_semaphore()
+    peers = at.chip_peers() + at.plane_peers()
+    for peer in peers:
+        pl.semaphore_signal(barrier, inc=1, device_id=peer, device_id_type=MESH)
+
+    @pl.when(off_diagonal)
+    def _():
+        pl.semaphore_signal(barrier, inc=1, device_id=turned, device_id_type=MESH)
+
+    pl.semaphore_wait(barrier, len(peers) + off_diagonal.astype(jnp.int32))
+
+    k = wires.used[0]
+    wires.used[0] += 1
+    swap = pltpu.make_async_remote_copy(
+        src_ref=qkv_ref,
+        dst_ref=qkvs_ref.at[2 * z + c],
+        send_sem=sems[0].at[k],
+        recv_sem=sems[1].at[k],
+        device_id=turned,
+        device_id_type=MESH,
+    )
+    stay = pltpu.make_async_copy(qkv_ref, qkvs_ref.at[2 * b + c], sems[2].at[0])
+    wires.used[1] += 1
+
+    @pl.when(off_diagonal)
+    def _():
+        swap.start()
+
+    @pl.when(jnp.logical_not(off_diagonal))
+    def _():
+        stay.start()
+
+    mt_sends = []
+    for k in range(1, at.chips):
+        peer = at.along_chips(k)[1]
+        mt_sends.append(wires.send(mt_ref, mts_ref.at[c, b, z], peer))
+    x_sends, vec_sends = [], []
+    for k in range(1, at.chips):
+        peer = at.along_chips(k)[1]
+        x_sends.append(wires.send(x_ref, xs_ref.at[s], peer))
+        vec_sends.append(wires.send(vec_ref, vecs_ref.at[s], peer))
+    own = [
+        wires.local(x_ref, xs_ref.at[s]),
+        wires.local(mt_ref, mts_ref.at[c, b, z]),
+        wires.local(vec_ref, vecs_ref.at[s]),
+    ]
+    last = [
+        wires.send(x_ref, xs_ref.at[s], at.partner()),
+        wires.send(vec_ref, vecs_ref.at[s], at.partner()),
+        wires.send(up_ref, up2_ref, at.partner()),
+        wires.send(down_ref, down2_ref, at.partner()),
+    ]
+
+    @pl.when(off_diagonal)
+    def _():
+        swap.wait_recv()
+
+    @pl.when(jnp.logical_not(off_diagonal))
+    def _():
+        stay.wait()
+
+    for k in range(1, 2 * at.batches):
+        peer = at.along_plane(k)[2]
+        last.append(wires.send(qkvs_ref.at[2 * b + c], qkvs_ref.at[2 * b + c], peer))
+    for copy in mt_sends:
+        copy.wait_recv()
+    for copy in own:
+        copy.wait()
+    row_sends = []
+    for k in range(1, at.batches):
+        peer = at.along_rows(k)[1]
+        row_sends.append(wires.send(mts_ref.at[c, b], mts_ref.at[c, b], peer))
+    last.append(wires.send(mts_ref.at[c, b], mts_ref.at[c, b], at.partner()))
+    for k in range(1, at.batches):
+        row = at.from_rows(k)
+        row_sends[k - 1].wait_recv()
+        last.append(wires.send(mts_ref.at[c, row], mts_ref.at[c, row], at.partner()))
+    for k in range(1, at.chips):
+        index = 2 * at.from_chips(k) + c
+        x_sends[k - 1].wait_recv()
+        last.append(wires.send(xs_ref.at[index], xs_ref.at[index], at.partner()))
+        vec_sends[k - 1].wait_recv()
+        last.append(wires.send(vecs_ref.at[index], vecs_ref.at[index], at.partner()))
+    for copy in last:
+        copy.wait_recv()
+    wires.finish()
+
+    @pl.when(off_diagonal)
+    def _():
+        swap.wait_send()
+
+
+def gather_inputs(x, qkv, mt, vec, up, down):
+    tokens, batches = lax.axis_size("seq"), lax.axis_size("batch")
+    chips = tokens // 2
+    outs = (
+        like(x, tokens),
+        like(qkv, tokens),
+        like(mt, 2, batches, chips),
+        like(vec, tokens),
+        like(up),
+        like(down),
+    )
+    sends = 1 + 3 * (chips - 1) + 4 + 2 * batches - 1 + 2 * (batches - 1) + 1 + 2 * (chips - 1)
+    return comm_call(
+        gather_kernel, "gather_inputs", 0, outs, (x, qkv, mt, vec, up, down), sends, 4
+    )
+
+
+def swap_kernel(src_ref, dst_ref, *sems):
+    at = Place()
+    wires = Wires(*sems)
+    meet(at.seq_peers())
+    copies = []
+    for k in range(1, at.tokens):
+        part, peer = at.along_seq(k)
+        copies.append(wires.send(src_ref.at[part], dst_ref.at[at.part], peer))
+    own = wires.local(src_ref.at[at.part], dst_ref.at[at.part])
+    for copy in copies:
+        copy.wait_recv()
+    own.wait()
+    wires.finish()
+
+
+def swap_seq(blocks, ident):
+    tokens = lax.axis_size("seq")
+    return comm_call(
+        swap_kernel, "swap_seq", ident, (like(blocks),), (blocks,), tokens - 1, 1
+    )[0]
+
+
+def class_gather_kernel(src_ref, dst_ref, *sems):
+    at = Place()
+    wires = Wires(*sems)
+    meet(at.chip_peers())
+    copies = [
+        wires.send(src_ref, dst_ref.at[at.chip], at.along_chips(k)[1])
+        for k in range(1, at.chips)
+    ]
+    own = wires.local(src_ref, dst_ref.at[at.chip])
+    for copy in copies:
+        copy.wait_recv()
+    own.wait()
+    wires.finish()
+
+
+def class_gather(block, ident):
+    chips = lax.axis_size("seq") // 2
+    return comm_call(
+        class_gather_kernel, "class_gather", ident, (like(block, chips),), (block,), chips - 1, 1
+    )[0]
+
+
+def class_scatter_kernel(src_ref, dst_ref, *sems):
+    at = Place()
+    wires = Wires(*sems)
+    meet(at.chip_peers())
+    copies = []
+    for k in range(1, at.chips):
+        chip, peer = at.along_chips(k)
+        copies.append(wires.send(src_ref.at[chip], dst_ref.at[at.chip], peer))
+    own = wires.local(src_ref.at[at.chip], dst_ref.at[at.chip])
+    for copy in copies:
+        copy.wait_recv()
+    own.wait()
+    wires.finish()
+
+
+def class_scatter(blocks, ident):
+    chips = lax.axis_size("seq") // 2
+    return comm_call(
+        class_scatter_kernel, "class_scatter", ident, (like(blocks),), (blocks,), chips - 1, 1
+    )[0]
+
+
+def plane_sends(at, wires, src_ref, dst_ref):
+    mine = 2 * at.row + at.core
+    copies = []
+    for k in range(1, 2 * at.batches):
+        row, core, peer = at.along_plane(k)
+        other = lax.rem(core + at.core, 2)
+        copies.append(wires.send(src_ref.at[other, row], dst_ref.at[mine], peer))
+    return copies, wires.local(src_ref.at[0, at.row], dst_ref.at[mine])
+
+
+def spread_kernel(src_ref, up_ref, upb_ref, dst_ref, ups_ref, upbs_ref, *sems):
+    at = Place()
+    wires = Wires(*sems)
+    meet(at.chip_peers() + at.plane_peers())
+    copies = [
+        wires.send(src_ref, dst_ref.at[at.part], at.along_chips(k)[1])
+        for k in range(1, at.chips)
+    ]
+    last = [wires.send(src_ref, dst_ref.at[at.part], at.partner())]
+    own = [wires.local(src_ref, dst_ref.at[at.part])]
+    for src, dst in ((up_ref, ups_ref), (upb_ref, upbs_ref)):
+        more, kept = plane_sends(at, wires, src, dst)
+        last += more
+        own.append(kept)
+    for k in range(1, at.chips):
+        index = 2 * at.from_chips(k) + at.core
+        copies[k - 1].wait_recv()
+        last.append(wires.send(dst_ref.at[index], dst_ref.at[index], at.partner()))
+    for copy in last:
+        copy.wait_recv()
+    for copy in own:
+        copy.wait()
+    wires.finish()
+
+
+def spread_grads(block, up, upb, ident):
+    tokens, batches = lax.axis_size("seq"), lax.axis_size("batch")
+    chips = tokens // 2
+    outs = (
+        like(block, tokens),
+        jax.ShapeDtypeStruct((2 * batches,) + up.shape[2:], up.dtype),
+        jax.ShapeDtypeStruct((2 * batches,) + upb.shape[2:], upb.dtype),
+    )
+    sends = 2 * (chips - 1) + 1 + 2 * (2 * batches - 1)
+    return comm_call(spread_kernel, "spread_grads", ident, outs, (block, up, upb), sends, 3)
+
+
+def reduce_kernel(
+    in_ref, vec_ref, dw_ref, tab_ref, mix_ref,
+    ins_ref, vecs_ref, dws_ref, tabs_ref, mixs_ref, half_ref, sum_ref, *sems,
+):
+    at = Place()
+    wires = Wires(*sems)
+    meet(at.seq_peers() + at.row_peers())
+    c = at.core
+    halves = [
+        wires.send(in_ref.at[chip, 1 - c], half_ref.at[chip], at.partner())
+        for chip in range(at.chips)
+    ]
+    last, own = [], []
+    for k in range(1, at.batches):
+        row, peer = at.along_rows(k)
+        for src, dst in ((dw_ref, dws_ref), (tab_ref, tabs_ref), (mix_ref, mixs_ref)):
+            last.append(wires.send(src.at[row], dst.at[at.row], peer))
+    for src, dst in ((dw_ref, dws_ref), (tab_ref, tabs_ref), (mix_ref, mixs_ref)):
+        own.append(wires.local(src.at[at.row], dst.at[at.row]))
+    for k in range(1, at.tokens):
+        part, peer = at.along_seq(k)
+        last.append(wires.send(vec_ref.at[part], vecs_ref.at[at.part], peer))
+    own.append(wires.local(vec_ref.at[at.part], vecs_ref.at[at.part]))
+    for copy in halves:
+        copy.wait_recv()
+    sum_ref[...] = (
+        in_ref[:, c].astype(jnp.float32) + half_ref[...].astype(jnp.float32)
+    ).astype(jnp.bfloat16)
+    for k in range(1, at.chips):
+        chip, peer = at.along_chips(k)
+        last.append(wires.send(sum_ref.at[chip], ins_ref.at[at.chip], peer))
+    own.append(wires.local(sum_ref.at[at.chip], ins_ref.at[at.chip]))
+    for copy in last:
+        copy.wait_recv()
+    for copy in own:
+        copy.wait()
+    wires.finish()
+
+
+def reduce_grads(in_part, vec, dw, tab, mix, ident):
+    tokens, batches = lax.axis_size("seq"), lax.axis_size("batch")
+    chips = tokens // 2
+    half = (chips,) + in_part.shape[2:]
+    outs = (jax.ShapeDtypeStruct(half, in_part.dtype), like(vec), like(dw), like(tab), like(mix))
+    sends = chips + 3 * (batches - 1) + tokens - 1 + chips - 1
+    return comm_call(
+        reduce_kernel,
+        "reduce_grads",
+        ident,
+        outs,
+        (in_part, vec, dw, tab, mix),
+        sends,
+        5,
+        scratch=(pltpu.VMEM(half, in_part.dtype), pltpu.VMEM(half, in_part.dtype)),
+    )
+
+
+def settle_kernel(
+    dw_ref, tab_ref, mix_ref, vec_ref, down_ref,
+    dws_ref, tabs_ref, mixs_ref, vecs_ref, downs_ref, *sems,
+):
+    at = Place()
+    wires = Wires(*sems)
+    b, z, c = at.row, at.chip, at.core
+    off_diagonal = b != z
+    same, cross = (z, 2 * b + c), (z, 2 * b + 1 - c)
+    peers = at.seq_peers() + at.row_peers() + at.cross_peers()
+    barrier = pltpu.get_barrier_semaphore()
+    for peer in peers:
+        pl.semaphore_signal(barrier, inc=1, device_id=peer, device_id_type=MESH)
+
+    @pl.when(off_diagonal)
+    def _():
+        pl.semaphore_signal(barrier, inc=1, device_id=same, device_id_type=MESH)
+        pl.semaphore_signal(barrier, inc=1, device_id=cross, device_id_type=MESH)
+
+    pl.semaphore_wait(barrier, len(peers) + 2 * off_diagonal.astype(jnp.int32))
+
+    k = wires.used[0]
+    wires.used[0] += 1
+    move = pltpu.make_async_remote_copy(
+        src_ref=dw_ref.at[c],
+        dst_ref=dws_ref.at[c],
+        send_sem=sems[0].at[k],
+        recv_sem=sems[1].at[k],
+        device_id=same,
+        device_id_type=MESH,
+    )
+    stay = pltpu.make_async_copy(dw_ref.at[c], dws_ref.at[c], sems[2].at[0])
+    wires.used[1] += 1
+
+    @pl.when(off_diagonal)
+    def _():
+        move.start()
+
+    @pl.when(jnp.logical_not(off_diagonal))
+    def _():
+        stay.start()
+
+    last, own = [wires.send(dw_ref.at[1 - c], dws_ref.at[c], cross)], []
+    for k in range(1, at.tokens):
+        part, peer = at.along_seq(k)
+        last.append(wires.send(tab_ref.at[part], tabs_ref.at[at.part], peer))
+    own.append(wires.local(tab_ref.at[at.part], tabs_ref.at[at.part]))
+    last.append(wires.send(mix_ref, mixs_ref, at.partner()))
+    for k in range(1, at.batches):
+        last.append(wires.send(vec_ref, vecs_ref.at[b], at.along_rows(k)[1]))
+    own.append(wires.local(vec_ref, vecs_ref.at[b]))
+    more, kept = plane_sends(at, wires, down_ref, downs_ref)
+    last += more
+    own.append(kept)
+    for copy in last:
+        copy.wait_recv()
+    for copy in own:
+        copy.wait()
+    wires.finish()
+
+    @pl.when(off_diagonal)
+    def _():
+        move.wait()
+
+    @pl.when(jnp.logical_not(off_diagonal))
+    def _():
+        stay.wait()
+
+
+def settle_grads(dw, tab, mix, vec, down, ident):
+    tokens, batches = lax.axis_size("seq"), lax.axis_size("batch")
+    outs = (
+        like(dw),
+        like(tab),
+        like(mix),
+        like(vec, batches),
+        jax.ShapeDtypeStruct((2 * batches,) + down.shape[2:], down.dtype),
+    )
+    sends = 2 + tokens - 1 + 1 + batches - 1 + 2 * batches - 1
+    return comm_call(
+        settle_kernel, "settle_grads", ident, outs, (dw, tab, mix, vec, down), sends, 4
+    )
+
+
+def fits_fast(layer_input, table_shard, w_query):
+    rows, local_len, width = layer_input.shape
+    tokens, batches = lax.axis_size("seq"), lax.axis_size("batch")
+    return (
+        rows == 1
+        and local_len == BLOCK
+        and tokens == 2 * batches
+        and width == 3 * DH * batches
+        and (table_shard.shape[0] * tokens) % (4 * BLOCK) == 0
+        and tokens % 4 == 0
+    )
+
+
+def fast_body(
+    layer_input, segment_ids, w_query, w_key, w_value, w_mix, rel_table, attn_biases,
+    norm_gains, norm_shifts, w_up, up_bias, w_down, down_bias, out_grad,
+):
+    local_len, width = layer_input.shape[1:]
+    at = Place()
+    tokens, batches, chips = at.tokens, at.batches, at.chips
+    full_len = local_len * tokens
+    low, wide = jnp.bfloat16, jnp.float32
+    pair = 2 * DH
+    shard_rows, shard_cols = w_query.shape
+    table_rows = rel_table.shape[0]
+    lanes = attn_biases.shape[1]
+    hidden_here = w_up.shape[1]
+    x = layer_input[0]
+
+    pack = jnp.concatenate([attn_biases, norm_gains, norm_shifts, down_bias[None]], axis=0)
+    pack = jnp.pad(pack, ((0, 0), (0, BLOCK - lanes)))
+    pack = jnp.concatenate(
+        [pack, segment_ids.astype(low), up_bias.reshape(hidden_here // BLOCK, BLOCK)], axis=0
+    )
+    used = pack.shape[0]
+    pack = jnp.pad(pack, ((0, 16 - used), (0, 0)))
+    qkv = jnp.stack([w_query, w_key, w_value])
+    mt = jnp.concatenate([w_mix, rel_table], axis=0)
+    x_all, qkv_all, mt_all, vec_all, up_other, down_other = gather_inputs(
+        x, qkv, mt, pack, w_up, w_down
+    )
+    x_all = x_all.reshape(full_len, width)
+    vecs = vec_all[:, :9, :lanes].transpose(1, 0, 2).reshape(9, width)
+    biases, gains, shifts = vecs[0:4], vecs[4:6].astype(wide), vecs[6:8].astype(wide)
+    bias_down = vecs[8]
+    seg = vec_all[:, 9].reshape(full_len).astype(wide)
+    other_vec = lax.dynamic_index_in_dim(
+        vec_all, at.part + 1 - 2 * at.core, axis=0, keepdims=False
+    )
+    bias_up = jnp.concatenate([up_bias, other_vec[10:used].reshape(hidden_here)])
+    column = at.core * DH
+    wcols = qkv_all.transpose(0, 2, 1, 3).reshape(width, 3, shard_cols)
+    w_cat = lax.dynamic_slice_in_dim(wcols, column, pair, axis=2).reshape(width, 3 * pair)
+    first_col = at.chip * shard_cols + column
+    bias_cat = (
+        lax.dynamic_slice_in_dim(biases[:3], first_col, pair, axis=1)
+        .reshape(1, 3 * pair)
+        .astype(wide)
+    )
+    m_mix = mt_all[..., :shard_rows, :].transpose(2, 0, 3, 1, 4).reshape(width, width)
+    table = (
+        mt_all[..., shard_rows:, :].transpose(2, 0, 3, 1, 4).reshape(tokens * table_rows, width)
+    )
+
+    first = (at.core * (full_len // BLOCK // 2)).astype(jnp.int32).reshape(1)
+    q, k, v, qrev, krev, probs, ctx = attend(
+        first, x_all, w_cat, bias_cat, table, seg[:, None], seg[None, :]
+    )
+    got = swap_seq(ctx.reshape(tokens, local_len, pair), 1)
+    got = got.reshape(chips, 2, local_len, pair)
+    left, right = got[:, 0], got[:, 1]
+    context = jnp.concatenate(
+        [left[..., :DH], left[..., DH:] + right[..., :DH], right[..., DH:]], axis=-1
+    )
+    context_low = context.transpose(1, 0, 2).reshape(local_len, width)
+    pre_norm = (
+        x.astype(wide) + jnp.dot(context_low, m_mix, preferred_element_type=wide) + biases[3]
+    )
+    hidden, norm1_pull = jax.vjp(normalize, pre_norm, gains[0], shifts[0])
+    hidden_rows = class_gather(hidden.astype(low), 2).reshape(chips * local_len, width)
+    up_pair = jnp.concatenate([w_up, up_other], axis=1)
+    down_pair = jnp.concatenate([w_down, down_other], axis=0)
+    inner = jnp.dot(hidden_rows, up_pair, preferred_element_type=wide) + bias_up
+    act, gelu_pull = jax.vjp(exact_gelu, inner)
+    act_low = act.astype(low)
+    ffn_part = jnp.dot(act_low, down_pair, preferred_element_type=wide).astype(low)
+    ffn_parts = class_scatter(ffn_part.reshape(chips, local_len, width), 3)
+    mixed = hidden + jnp.sum(ffn_parts.astype(wide), axis=0) + bias_down
+    output, norm2_pull = jax.vjp(normalize, mixed, gains[1], shifts[1])
+    mixed_grad, gain2_grad, shift2_grad = norm2_pull(out_grad[0].astype(wide))
+    grad_rows = class_gather(mixed_grad.astype(low), 4).reshape(chips * local_len, width)
+    act_grad = jnp.einsum("nd,fd->nf", grad_rows, down_pair, preferred_element_type=wide)
+    inner_low = gelu_pull(act_grad)[0].astype(low)
+    back_part = jnp.einsum("nf,df->nd", inner_low, up_pair, preferred_element_type=wide).astype(
+        low
+    )
+    back_parts = class_scatter(back_part.reshape(chips, local_len, width), 5)
+    hidden_grad = mixed_grad + jnp.sum(back_parts.astype(wide), axis=0)
+    pre_grad, gain1_grad, shift1_grad = norm1_pull(hidden_grad)
+    up_part = jnp.einsum(
+        "nd,nkf->kdf",
+        hidden_rows,
+        inner_low.reshape(-1, 2, hidden_here),
+        preferred_element_type=wide,
+    ).astype(low)
+    up_part = up_part.reshape(2, batches, width // batches, hidden_here)
+    upb_part = jnp.sum(inner_low.astype(wide), axis=0).reshape(2, 1, 1, hidden_here)
+    upb_part = jnp.broadcast_to(upb_part, (2, batches, 8, hidden_here))
+    down_part = jnp.einsum(
+        "nkf,nge->kgfe",
+        act_low.reshape(-1, 2, hidden_here),
+        grad_rows.reshape(-1, batches, width // batches),
+        preferred_element_type=wide,
+    ).astype(low)
+    attn_all, up_parts, upb_parts = spread_grads(pre_grad.astype(low), up_part, upb_part, 6)
+    attn_all = attn_all.reshape(full_len, width)
+    mix_rows = lax.dynamic_slice_in_dim(m_mix, first_col, pair, axis=0)
+    context_grad = jnp.einsum(
+        "ne,de->nd", attn_all, mix_rows, preferred_element_type=wide
+    ).astype(low)
+    dcat, rel_grad, col_sums = attend_back(first, q, k, v, qrev, krev, probs, context_grad)
+    in_part = jnp.einsum("ne,de->nd", dcat, w_cat, preferred_element_type=wide).astype(low)
+    in_part = in_part.reshape(chips, 2, local_len, width)
+    dw_part = jnp.einsum("nd,ne->de", x_all, dcat, preferred_element_type=wide)
+    dw_rel = jnp.einsum("bd,be->de", table, rel_grad, preferred_element_type=wide)
+    dw_part = dw_part + jnp.pad(dw_rel, ((0, 0), (0, pair)))
+    dw_part = dw_part.astype(low).reshape(batches, width // batches, 3 * pair)
+    tab_part = jnp.einsum(
+        "be,gde->gbd",
+        rel_grad,
+        w_cat[:, : 2 * pair].reshape(batches, width // batches, 2 * pair),
+        preferred_element_type=wide,
+    ).astype(low)
+    mix_part = jnp.einsum(
+        "nk,nge->gke",
+        ctx,
+        attn_all.reshape(full_len, batches, width // batches),
+        preferred_element_type=wide,
+    ).astype(low)
+    bias_rows = lax.dynamic_update_slice(
+        jnp.zeros((3, width), wide), col_sums.reshape(3, pair), (jnp.int32(0), first_col)
+    )
+    vec_part = jnp.concatenate(
+        [
+            bias_rows,
+            jnp.sum(pre_grad, axis=0)[None],
+            gain1_grad[None],
+            gain2_grad[None],
+            shift1_grad[None],
+            shift2_grad[None],
+            jnp.sum(mixed_grad, axis=0)[None],
+        ],
+        axis=0,
+    )
+    vec_part = jnp.pad(
+        vec_part.reshape(9, tokens, lanes).transpose(1, 0, 2), ((0, 0), (0, 7), (0, BLOCK - lanes))
+    )
+    ins, vec_parts, dws, tabs, mixs = reduce_grads(in_part, vec_part, dw_part, tab_part, mix_part, 7)
+    input_grad = pre_grad + jnp.sum(ins.astype(wide), axis=0)
+    dw_sum = jnp.sum(dws.astype(wide), axis=0).astype(low)
+    tab_sum = jnp.sum(tabs.astype(wide), axis=0).astype(low)
+    mix_sum = jnp.sum(mixs.astype(wide), axis=0).astype(low)
+    vec_sum = jnp.sum(vec_parts, axis=0)
+    dw_got, tab_got, mix_other, vec_got, downs = settle_grads(
+        dw_sum.reshape(2, shard_rows, 3 * pair),
+        tab_sum.reshape(tokens, table_rows, shard_cols),
+        mix_sum,
+        vec_sum,
+        down_part,
+        8,
+    )
+    dw_got = dw_got.astype(wide).reshape(2, shard_rows, 3, pair)
+    dw_all = jnp.pad(dw_got[0], ((0, 0), (0, 0), (0, DH))) + jnp.pad(
+        dw_got[1], ((0, 0), (0, 0), (DH, 0))
+    )
+    table_grad = jnp.sum(tab_got.astype(wide), axis=0)
+    mix_own, mix_other = mix_sum.astype(wide), mix_other.astype(wide)
+    lower = jnp.where(at.core == 0, mix_own, mix_other)
+    upper = jnp.where(at.core == 0, mix_other, mix_own)
+    mix_grad = jnp.pad(lower, ((0, DH), (0, 0))) + jnp.pad(upper, ((DH, 0), (0, 0)))
+    mix_grad = lax.dynamic_slice_in_dim(mix_grad, at.core * shard_rows, shard_rows, axis=0)
+    small = jnp.sum(vec_got, axis=0)[:, :lanes]
+    return (
+        output.astype(low)[None],
+        input_grad[None],
+        dw_all[:, 0],
+        dw_all[:, 1],
+        dw_all[:, 2],
+        mix_grad,
+        table_grad,
+        small[0:4],
+        small[4:6],
+        small[6:8],
+        jnp.sum(up_parts.astype(wide), axis=0),
+        jnp.sum(upb_parts[:, 0], axis=0),
+        jnp.sum(downs.astype(wide), axis=0),
+        small[8],
+    )
+
+
 def body(
     layer_input,
     segment_ids,
@@ -178,6 +1204,11 @@
     down_bias,
     out_grad,
 ):
+    if fits_fast(layer_input, rel_table, w_query):
+        return fast_body(
+            layer_input, segment_ids, w_query, w_key, w_value, w_mix, rel_table, attn_biases,
+            norm_gains, norm_shifts, w_up, up_bias, w_down, down_bias, out_grad,
+        )
     rows, local_len, width = layer_input.shape
     full_len = local_len * lax.axis_size("seq")
     tokens_here = local_len * rows

time: 1510 us -> 377 us (0.25); the launches traced: 1490 us -> 376 us
  waiting for transfers between devices: 585 us -> 0 us
  local copies, waits for them, and re-layouts: 426 us -> 58.8 us
  Pallas kernels: 0 us -> 266 us
  matrix products: 249 us -> 31.5 us
  blocking collectives: 142 us -> 0 us
  other arithmetic: 69.4 us -> 18.3 us
  between operations: 16.8 us -> 1.38 us
    reduce_scatter x11 -> x0, waiting for transfers between devices: 303 us -> none  [the longest x2 61.8 us: hidden_sums(): lax.psum_scatter(make_term(jnp.int32(0), tokens_here * lax.axis_size('seq...]
    pallas_call x0 -> x11, Pallas kernels: none -> 266 us  [the longest x9 210 us: comm_call(): pl.pallas_call(kernel, out_shape=tuple(out_shapes), in_specs=[VMEM_SPEC]...]
    unnamed x35 -> x0, waiting for transfers between devices: 221 us -> none
    dot_general x150 -> x13, matrix products: 249 us -> 31.5 us  [the longest x1 5.7 us: fast_body(): inner = jnp.dot(hidden_rows, up_pair, preferred_element_type=wide) + bias_up]
    all_gather x10 -> x0, blocking collectives: 101 us -> none  [the longest x1 15.7 us: body(): lax.all_gather(parts[4], 'seq', axis=0, tiled=True)]
    dynamic_update_slice x18 -> x1, local copies, waits for them, and re-layouts: 78.7 us -> 0.16 us  [fast_body(): lax.dynamic_update_slice(jnp.zeros((3, width), wide), col_sums.reshape(3,...]
    all_gather x8 -> x0, waiting for transfers between devices: 61 us -> none  [the longest x2 47.5 us: spread_rows(): return lax.all_gather(rows_low, 'seq', axis=0, tiled=True)]
    pad x84 -> x1, local copies, waits for them, and re-layouts: 58.4 us -> 0.01 us  [fast_body(): jnp.pad(vec_part.reshape(9, tokens, lanes).transpose(1, 0, 2), ((0, 0), (...]
  transfers between devices with their start and end apart: 27 -> 0, of which waited for: 22 -> 0; matrix products, arithmetic and copies ran while one was open for 17% -> 0% of each run, Pallas kernels for 0% -> 0%
where the time goes in v1:
time: 377 us; the launch traced here: 376 us
  Pallas kernels  266 us (71%)
  local copies, waits for them, and re-layouts  58.8 us (16%)
  matrix products  31.5 us (8%)
  other arithmetic  18.3 us (5%)
    pallas_call x9, Pallas kernels, comm_call(): pl.pallas_call(kernel, out_shape=tuple(out_shapes), in_specs=[VMEM_SPEC]...  210 us
    pallas_call x1, Pallas kernels, attend_back(): pl.pallas_call(attend_back_kernel, out_shape=(jax.ShapeDtypeStruct((full_...  28.6 us
    pallas_call x1, Pallas kernels, attend(): pl.pallas_call(attend_kernel, out_shape=(jax.ShapeDtypeStruct((2, full_le...  27.4 us
    unnamed x107, local copies, waits for them, and re-layouts  19.8 us

profile of v1, /device:TPU:0, one launch (start us, length us, event | category | flops | bytes accessed | tf_op | source)
XLA Modules:
  0.0 375.6 jit_solution(1022133256848270090)
XLA Ops:
  7.5 48.8 %gather_inputs.1 = (bf16[8,128,768]{2,1,0:T(8,128)(2,1)S(1)}, bf16[8,3,96,192]{3,2,1,0:T(8,128)(2,1)S(1)}, bf16[2,4,4,160,192]{4,3,2,1,0:T(8,128)(2,1)S(1)}, bf1...) custom-call(bf16[128,768]{1,0:T(8,128)(2,1)S(1)} %bitcast.147, ...), custom_call_target="tpu_custom_call" | custom-call | tf_op jit(solution)/shard_map/gather_inputs/pallas_call | solution.py:601
  59.5 2.6 copy.78
  62.1 2.9 reshape.276
  65.0 2.0 constant_dynamic-slice_fusion.2
  66.9 2.1 copy.81.w_ref
  69.9 1.8 copy.80
  71.7 3.0 reshape.278.table_ref
  76.4 27.4 %attend.1 = (bf16[2,1024,64]{2,1,0:T(8,128)(2,1)}, bf16[2,1024,64]{2,1,0:T(8,128)(2,1)}, bf16[2,1024,64]{2,1,0:T(8,128)(2,1)}, bf16[2,512,64]{2,1,0:T(8,128)(2,1...) custom-call(s32[1]{0:T(128)} %bitcast.1.first_ref, ...), custom_call_target="tpu_custom_call" | custom-call | tf_op jit(solution)/shard_map/attend/pallas_call | solution.py:305
  104.7 7.9 %swap_seq.1 = bf16[8,128,128]{2,1,0:T(8,128)(2,1)S(1)} custom-call(bf16[8,128,128]{2,1,0:T(8,128)(2,1)S(1)} %bitcast.146), custom_call_target="tpu_custom_call" | custom-call | tf_op jit(solution)/shard_map/swap_seq/pallas_call | solution.py:601
  115.8 2.3 reshape.282
  118.1 1.8 fusion.49
  120.5 17.8 %class_gather.2 = bf16[4,128,768]{2,1,0:T(8,128)(2,1)S(1)} custom-call(bf16[128,768]{1,0:T(8,128)(2,1)S(1)} %fusion.17.src_ref), custom_call_target="tpu_custom_call" | custom-call | tf_op jit(solution)/shard_map/class_gather/pallas_call | solution.py:601
  138.5 5.7 %multiply_convert_fusion = (bf16[512,768]{1,0:T(8,128)(2,1)S(1)}, f32[512,768]{1,0:T(8,128)}, f32[512,768]{1,0:T(8,128)}) fusion(f32[768]{0:T(1024)S(1)} %maximum_convert_fusion, bf16[512,768]{1,0:T(8,128)(2,1)S(1)} %bitcast.150, bf16[768,768]{1,0:T(8,128)(2,1)S(1)} %constant_dynamic-update-slice_fusion), kind=kOutput, calls=%fused_computation.10 | convolution fusion | flops 629932032 | bytes 5901312 | tf_op jit(solution)/shard_map/dot_general | solution.py:1072
  145.5 19.2 %class_scatter.2 = bf16[4,128,768]{2,1,0:T(8,128)(2,1)S(1)} custom-call(bf16[4,128,768]{2,1,0:T(8,128)(2,1)S(1)} %bitcast.149), custom_call_target="tpu_custom_call" | custom-call | tf_op jit(solution)/shard_map/class_scatter/pallas_call | solution.py:601
  166.9 20.2 %class_gather.3 = bf16[4,128,768]{2,1,0:T(8,128)(2,1)S(1)} custom-call(bf16[128,768]{1,0:T(8,128)(2,1)S(1)} %get-tuple-element.124.src_ref), custom_call_target="tpu_custom_call" | custom-call | tf_op jit(solution)/shard_map/class_gather/pallas_call | solution.py:601
  187.1 3.5 convert_reduce_fusion.3
  191.5 18.7 %class_scatter.3 = bf16[4,128,768]{2,1,0:T(8,128)(2,1)S(1)} custom-call(bf16[4,128,768]{2,1,0:T(8,128)(2,1)S(1)} %bitcast.148), custom_call_target="tpu_custom_call" | custom-call | tf_op jit(solution)/shard_map/class_scatter/pallas_call | solution.py:601
  213.4 3.0 fusion.6
  216.4 1.7 copy.87
  219.0 21.2 %spread_grads.1 = (bf16[8,128,768]{2,1,0:T(8,128)(2,1)S(1)}, bf16[8,192,384]{2,1,0:T(8,128)(2,1)S(1)}, f32[8,8,384]{2,1,0:T(8,128)S(1)}) custom-call(bf16[128,768]{1,0:T(8,128)(2,1)S(1)} %copy-done.16, bf16[2,4,192,384]{3,2,1,0:T(8,128)(2,1)S(1)} %bitcast.136, f32[2,4,8,384]{3,2,1,0:T(8,128)S(1)} %broadcast_in_dim.53.upb_ref), custom_call_target="tpu_custom_call" | custom-call | tf_op jit(solution)/shard_map/spread_grads/pallas_call | solution.py:601
  241.9 2.2 convolution_convert_fusion.6.dctx_ref
  244.1 28.6 %attend_back.1 = (bf16[1024,384]{1,0:T(8,128)(2,1)}, bf16[512,256]{1,0:T(8,128)(2,1)}, f32[1,384]{1,0:T(1,128)}) custom-call(s32[1]{0:T(128)} %bitcast.1.first_ref, bf16[2,1024,64]{2,1,0:T(8,128)(2,1)} %get-tuple-element.50.q_ref, bf16[2,1024,64]{2,1,0:T(8,128)(2,1)} %get-tuple-element.51.k_ref, bf16[2,1024,64]{2,1,0:T(8,128)(2,1)} %get-tuple-element.52.v_ref, ...), custom_call_target="tpu_custom_call" | custom-call | tf_op jit(solution)/shard_map/attend_back/pallas_call | solution.py:467
  272.7 3.5 convolution_convert_fusion
  278.7 3.0 fusion.7
  281.9 2.2 convolution_convert_fusion.5
  285.6 2.0 copy.91
  287.5 3.7 reshape_reshape.6
  291.2 2.8 convolution_convert_fusion.7
  294.0 1.8 copy.92
  297.8 29.8 %reduce_grads.1 = (bf16[4,128,768]{2,1,0:T(8,128)(2,1)S(1)}, f32[8,16,128]{2,1,0:T(8,128)S(1)}, bf16[4,192,384]{2,1,0:T(8,128)(2,1)S(1)}, bf16[4,512,192]{2,1,0:T(8,128)(2,1)S(1)}, bf16[4,128,192]{2,1,0:T(8,128)(2,1)S(1)}) custom-call(bf16[4,2,128,768]{3,2,1,0:T(8,128)(2,1)S(1)} %bitcast.139, f32[8,16,128]{2,1,0:T(8,128)S(1)} %pad.34.vec_ref, ...), custom_call_target="tpu_custom_call" | custom-call | tf_op jit(solution)/shard_map/reduce_grads/pallas_call | solution.py:601
  336.6 26.1 %settle_grads.1 = (bf16[2,96,384]{2,1,0:T(8,128)(2,1)S(1)}, bf16[8,64,192]{2,1,0:T(8,128)(2,1)S(1)}, bf16[128,192]{1,0:T(8,128)(2,1)S(1)}, f32[4,16,128]{2,1,0:T(8,128)S(1)}, bf16[8,384,192]{2,1,0:T(8,128)(2,1)S(1)}) custom-call(bf16[2,96,384]{2,1,0:T(8,128)(2,1)S(1)} %bitcast.152, bf16[8,64,192]{2,1,0:T(8,128)(2,1)S(1)} %bitcast.145, ...), custom_call_target="tpu_custom_call" | custom-call | tf_op jit(solution)/shard_map/settle_grads/pallas_call | solution.py:601
  365.3 1.8 pad_add_fusion
  (204 shorter events, 53.4 us)
Async XLA Ops:
  0.6 58.8 %copy-start.43 = (bf16[384]{0:T(512)(128)(2,1)S(1)}, bf16[384]{0:T(512)(128)(2,1)}, u32[]{:S(2)}) copy-start(bf16[384]{0:T(512)(128)(2,1)} %param.26) | copy-start | bytes 2308
  4.5 1.1 copy-start
  5.5 1.1 copy-start.2
  56.3 1.1 copy-start.5
  115.8 2.3 copy-start.15
  118.1 20.2 %copy-start.1 = (bf16[768,384]{1,0:T(8,128)(2,1)S(1)}, bf16[768,384]{1,0:T(8,128)(2,1)}, u32[]{:S(2)}) copy-start(bf16[768,384]{1,0:T(8,128)(2,1)} %up_ref.1) | copy-start | bytes 1769476
  120.1 18.2 %copy-start.21 = (bf16[768,384]{1,0:T(8,128)(2,1)S(1)}, bf16[768,384]{1,0:T(8,128)(2,1)}, u32[]{:S(2)}) copy-start(bf16[768,384]{1,0:T(8,128)(2,1)} %copy-done.20) | copy-start | bytes 1769476
  138.5 5.7 %copy-start.40 = (bf16[768,768]{1,0:T(8,128)(2,1)}, bf16[768,768]{1,0:T(8,128)(2,1)S(1)}, u32[]{:S(2)}) copy-start(bf16[768,768]{1,0:T(8,128)(2,1)S(1)} %constant_dynamic-update-slice_fusion) | copy-start | bytes 3538948
  138.5 5.7 %copy-start.3 = (bf16[384,768]{1,0:T(8,128)(2,1)S(1)}, bf16[384,768]{1,0:T(8,128)(2,1)}, u32[]{:S(2)}) copy-start(bf16[384,768]{1,0:T(8,128)(2,1)} %down_ref.1) | copy-start | bytes 1769476
  144.3 1.1 copy-start.39
  187.1 3.5 copy-start.41
  210.8 5.5 %copy-start.35 = (f32[128,768]{1,0:T(8,128)}, f32[128,768]{1,0:T(8,128)S(1)}, u32[]{:S(2)}) copy-start(f32[128,768]{1,0:T(8,128)S(1)} %get-tuple-element.114) | copy-start | bytes 1179652
  210.8 2.6 copy-start.44
  240.2 1.1 copy-start.7
  272.7 3.5 copy-start.46
  272.7 3.8 %copy-start.42 = (f32[768]{0:T(1024)S(1)}, f32[768]{0:T(1024)}, u32[]{:S(2)}) copy-start(f32[768]{0:T(1024)} %get-tuple-element.125) | copy-start | bytes 9220
  272.7 4.1 %copy-start.38 = (bf16[1,128,768]{2,1,0:T(8,128)(2,1)S(1)}, bf16[1,128,768]{2,1,0:T(8,128)(2,1)}, u32[]{:S(2)}) copy-start(bf16[1,128,768]{2,1,0:T(8,128)(2,1)} %param.29) | copy-start | bytes 589828
  272.7 4.4 %copy-start.33 = (bf16[512,768]{1,0:T(8,128)(2,1)S(1)}, bf16[512,768]{1,0:T(8,128)(2,1)}, u32[]{:S(2)}) copy-start(bf16[512,768]{1,0:T(8,128)(2,1)} %reshape.278.table_ref) | copy-start | bytes 2359300
  277.1 1.5 copy-start.6
  278.7 3.0 copy-start.34
  291.2 4.6 %copy-start.4 = (bf16[1024,768]{1,0:T(8,128)(2,1)S(1)}, bf16[1024,768]{1,0:T(8,128)(2,1)}, u32[]{:S(2)}) copy-start(bf16[1024,768]{1,0:T(8,128)(2,1)} %convolution_convert_fusion) | copy-start | bytes 4718596
  296.8 1.1 copy-start.17
  297.8 30.9 %copy-start.36 = (f32[128,768]{1,0:T(8,128)S(1)}, f32[128,768]{1,0:T(8,128)}, u32[]{:S(2)}) copy-start(f32[128,768]{1,0:T(8,128)} %copy-done.35) | copy-start | bytes 1179652
  297.8 30.9 %copy-start.45 = (f32[128]{0:T(128)S(1)}, f32[128]{0:T(128)}, u32[]{:S(2)}) copy-start(f32[128]{0:T(128)} %copy-done.44) | copy-start | bytes 1540
  328.6 2.2 copy-start.12
  329.6 1.5 copy-start.26
  332.4 1.1 copy-start.48
  362.7 6.3 %copy-start.19 = (bf16[128,192]{1,0:T(8,128)(2,1)S(1)}, bf16[128,192]{1,0:T(8,128)(2,1)}, u32[]{:S(2)}) copy-start(bf16[128,192]{1,0:T(8,128)(2,1)} %reduce_sum.304.mix_ref) | copy-start | bytes 147460
  363.4 8.1 %copy-start.8 = (bf16[8,192,384]{2,1,0:T(8,128)(2,1)S(1)}, bf16[8,192,384]{2,1,0:T(8,128)(2,1)}, u32[]{:S(2)}) copy-start(bf16[8,192,384]{2,1,0:T(8,128)(2,1)} %copy-done.7) | copy-start | bytes 3538948
  363.4 5.6 %copy-start.28 = (bf16[128,192]{1,0:T(8,128)(2,1)S(1)}, bf16[128,192]{1,0:T(8,128)(2,1)}, u32[]{:S(2)}) copy-start(bf16[128,192]{1,0:T(8,128)(2,1)} %copy-done.27) | copy-start | bytes 147460
  363.4 6.3 %copy-start.24 = (bf16[8,64,192]{2,1,0:T(8,128)(2,1)S(1)}, bf16[8,64,192]{2,1,0:T(8,128)(2,1)}, u32[]{:S(2)}) copy-start(bf16[8,64,192]{2,1,0:T(8,128)(2,1)} %copy-done.23) | copy-start | bytes 589828
  363.4 6.9 %copy-start.31 = (f32[4,16,128]{2,1,0:T(8,128)S(1)}, f32[4,16,128]{2,1,0:T(8,128)}, u32[]{:S(2)}) copy-start(f32[4,16,128]{2,1,0:T(8,128)} %copy-done.30) | copy-start | bytes 98308
  (17 other events, 14.9 us)

commit v2 on v1

--- a/solution.py
+++ b/solution.py
@@ -197,14 +197,23 @@
     return pltpu.roll(turned, turned.shape[1] - BLOCK, 1, stride=1, stride_axis=0)[:, :buckets]
 
 
+def chip_columns(vec_ref, chip, index, core):
+    width = 3 * DH // 2
+    both = jnp.concatenate(
+        [
+            vec_ref[2 * chip, index : index + 1, :width].astype(jnp.float32),
+            vec_ref[2 * chip + 1, index : index + 1, :width].astype(jnp.float32),
+        ],
+        axis=1,
+    )
+    return jnp.where(core == 0, both[:, : 2 * DH], both[:, DH:])
+
+
 def attend_kernel(
-    first_ref,
-    x_ref,
-    w_ref,
-    bias_ref,
-    table_ref,
-    segc_ref,
-    segr_ref,
+    xs_ref,
+    qkvs_ref,
+    mts_ref,
+    vecs_ref,
     q_ref,
     k_ref,
     v_ref,
@@ -212,11 +221,17 @@
     krev_ref,
     p_ref,
     ctx_ref,
+    w_ref,
+    mix_ref,
+    table_ref,
+    x_ref,
+    segc_ref,
     place_ref,
     wide_ref,
     ends_ref,
     held_ref,
 ):
+    at = Place()
     full_len = x_ref.shape[0]
     buckets = table_ref.shape[0]
     blocks = full_len // BLOCK
@@ -227,8 +242,34 @@
     group = 2 * DH
     scale = 1.0 / math.sqrt(3.0 * DH)
     units = p_ref.shape[0]
-    proj = (dot_nn(x_ref[...], w_ref[...]) + bias_ref[...]).astype(jnp.bfloat16)
-    rel = (dot_nn(table_ref[...], w_ref[:, : 2 * group]) + bias_ref[:, : 2 * group]).astype(
+    shard_rows = qkvs_ref.shape[2]
+    table_rows = mts_ref.shape[3] - shard_rows
+    batches = mts_ref.shape[1]
+    for part in range(at.tokens):
+        pieces = []
+        for i in range(3):
+            piece = qkvs_ref[part, i]
+            pieces.append(jnp.where(at.core == 0, piece[:, :group], piece[:, DH:]))
+        w_ref[part * shard_rows : (part + 1) * shard_rows] = jnp.concatenate(pieces, axis=1)
+        core, chip = part % 2, part // 2
+        whole = [mts_ref[core, row, chip] for row in range(batches)]
+        mix_ref[part * shard_rows : (part + 1) * shard_rows] = jnp.concatenate(
+            [piece[:shard_rows] for piece in whole], axis=1
+        )
+        table_ref[part * table_rows : (part + 1) * table_rows] = jnp.concatenate(
+            [piece[shard_rows:] for piece in whole], axis=1
+        )
+        x_ref[part * BLOCK : (part + 1) * BLOCK] = xs_ref[part]
+        own_seg = vecs_ref[part, 9:10].astype(jnp.float32)
+        segc_ref[part * BLOCK : (part + 1) * BLOCK] = jnp.broadcast_to(own_seg, (BLOCK, BLOCK)).T
+    seg_row = jnp.concatenate(
+        [vecs_ref[part, 9:10].astype(jnp.float32) for part in range(at.tokens)], axis=1
+    )
+    bias = jnp.concatenate(
+        [chip_columns(vecs_ref, at.chip, i, at.core) for i in range(3)], axis=1
+    )
+    proj = (dot_nn(x_ref[...], w_ref[...]) + bias).astype(jnp.bfloat16)
+    rel = (dot_nn(table_ref[...], w_ref[:, : 2 * group]) + bias[:, : 2 * group]).astype(
         jnp.bfloat16
     )
     rel = dot_nn(turn_matrix(buckets), rel).astype(jnp.bfloat16)
@@ -258,7 +299,7 @@
 
         lax.fori_loop(0, blocks, key_block, 0)
 
-    first = first_ref[0]
+    first = at.core * (blocks // 2)
 
     def unit(u, carry):
         g = u + first
@@ -280,7 +321,7 @@
                 wide_ref[:, span : span + full_len],
             ),
         )
-        same = segc_ref[pl.ds(start, BLOCK)] == segr_ref[...]
+        same = segc_ref[pl.ds(start, BLOCK), 0:1] == seg_row
         scores = jnp.where(same, (content + near) * scale, masked_score)
         highest = jnp.max(scores, axis=-1, keepdims=True)
         exponent = jnp.exp(scores - highest)
@@ -291,12 +332,16 @@
         return carry
 
     lax.fori_loop(0, units, unit, 0)
-    ctx_ref[...] = jnp.concatenate([held_ref[0], held_ref[1]], axis=1)
-
-
-def attend(first, x_all, w_cat, bias_cat, table, seg_col, seg_row):
-    full_len, width = x_all.shape
-    buckets = table.shape[0]
+    for part in range(at.tokens):
+        rows = slice(part * BLOCK, (part + 1) * BLOCK)
+        ctx_ref[part] = jnp.concatenate([held_ref[0, rows], held_ref[1, rows]], axis=1)
+
+
+def attend(xs, qkvs, mts, vecs):
+    tokens, local_len, width = xs.shape
+    full_len = tokens * local_len
+    shard_rows = qkvs.shape[2]
+    buckets = tokens * (mts.shape[3] - shard_rows)
     blocks = full_len // BLOCK
     units = 3 * blocks // 2
     band_width = buckets + BLOCK
@@ -311,12 +356,16 @@
             jax.ShapeDtypeStruct((2, buckets, DH), low),
             jax.ShapeDtypeStruct((2, buckets, DH), low),
             jax.ShapeDtypeStruct((units, BLOCK, full_len), low),
-            jax.ShapeDtypeStruct((full_len, 2 * DH), low),
+            jax.ShapeDtypeStruct((tokens, local_len, 2 * DH), low),
+            jax.ShapeDtypeStruct((width, 6 * DH), low),
+            jax.ShapeDtypeStruct((width, width), low),
+            jax.ShapeDtypeStruct((buckets, width), low),
         ),
-        in_specs=[pl.BlockSpec(memory_space=pltpu.SMEM)]
-        + [pl.BlockSpec(memory_space=pltpu.VMEM)] * 6,
-        out_specs=[pl.BlockSpec(memory_space=pltpu.VMEM)] * 7,
+        in_specs=[pl.BlockSpec(memory_space=pltpu.VMEM)] * 4,
+        out_specs=[pl.BlockSpec(memory_space=pltpu.VMEM)] * 10,
         scratch_shapes=[
+            pltpu.VMEM((full_len, width), low),
+            pltpu.VMEM((full_len, BLOCK), wide),
             pltpu.VMEM((2, pad_blocks, BLOCK, band_width), wide),
             pltpu.VMEM((BLOCK, full_len + buckets), wide),
             pltpu.VMEM((2, 2, 16, full_len), wide),
@@ -324,21 +373,28 @@
         ],
         compiler_params=pltpu.CompilerParams(vmem_limit_bytes=60 * 1024 * 1024),
         name="attend",
-    )(first, x_all, w_cat, bias_cat, table, seg_col, seg_row)
+    )(xs, qkvs, mts, vecs)
 
 
 def attend_back_kernel(
-    first_ref,
     q_ref,
     k_ref,
     v_ref,
     qrev_ref,
     krev_ref,
     p_ref,
-    dctx_ref,
-    dcat_ref,
-    rel_ref,
+    ctx_ref,
+    w_ref,
+    mix_ref,
+    table_ref,
+    xs_ref,
+    attn_ref,
+    in_ref,
+    dw_ref,
+    tab_ref,
+    mixpart_ref,
     sum_ref,
+    x_ref,
     heads_ref,
     wide_ref,
     low_ref,
@@ -361,9 +417,25 @@
     units = p_ref.shape[0]
     for ref in (wide_ref, low_ref, place_ref, dq_ref, dkt_ref, dvt_ref, far_ref, dkr_ref, dqr_ref):
         ref[...] = jnp.zeros_like(ref)
-    for slot in range(2):
-        heads_ref[slot] = dctx_ref[:, slot * DH : (slot + 1) * DH]
-    first = first_ref[0]
+    at = Place()
+    group = 2 * DH
+    width = x_ref.shape[1]
+    first_row = pl.multiple_of((3 * at.chip + at.core) * DH, DH)
+    mix_rows = mix_ref[pl.ds(first_row, group)]
+    mix_part = jnp.zeros((group, width), jnp.float32)
+    for part in range(at.tokens):
+        x_ref[part * BLOCK : (part + 1) * BLOCK] = xs_ref[part]
+        low_part = attn_ref[part]
+        mix_part = mix_part + dot_tn(ctx_ref[part], low_part)
+        dctx = dot_nt(low_part, mix_rows).astype(jnp.bfloat16)
+        for slot in range(2):
+            heads_ref[slot, part * BLOCK : (part + 1) * BLOCK] = dctx[
+                :, slot * DH : (slot + 1) * DH
+            ]
+    columns = width // at.batches
+    for row in range(at.batches):
+        mixpart_ref[row] = mix_part[:, row * columns : (row + 1) * columns].astype(jnp.bfloat16)
+    first = at.core * (blocks // 2)
     turn = turn_matrix(BLOCK)
     place8 = lax.broadcasted_iota(jnp.int32, (8, full_len), 0)
 
@@ -449,32 +521,47 @@
         parts_r[slot] = dqr_out
         parts_r[2 + slot] = dkr_out
     dcat = jnp.concatenate(parts_q + parts_k + parts_v, axis=1)
-    dcat_ref[...] = dcat
+    in_part = dot_nt(dcat, w_ref[...]).astype(jnp.bfloat16)
+    for part in range(at.tokens):
+        in_ref[part // 2, part % 2] = in_part[part * BLOCK : (part + 1) * BLOCK]
     rel = jnp.concatenate(parts_r, axis=1)
-    rel_ref[...] = dot_nn(turn_matrix(buckets), rel.astype(jnp.bfloat16)).astype(jnp.bfloat16)
+    rel_low = dot_nn(turn_matrix(buckets), rel.astype(jnp.bfloat16)).astype(jnp.bfloat16)
+    dw = dot_tn(x_ref[...], dcat)
+    dw_rel = dot_tn(table_ref[...], rel_low)
+    dw = jnp.concatenate([dw[:, : 2 * group] + dw_rel, dw[:, 2 * group :]], axis=1)
+    dw_low = dw.astype(jnp.bfloat16)
+    for row in range(at.batches):
+        rows = slice(row * columns, (row + 1) * columns)
+        dw_ref[row] = dw_low[rows]
+        tab_ref[row] = dot_nt(rel_low, w_ref[rows, : 2 * group]).astype(jnp.bfloat16)
     rel_sum = jnp.sum(rel, axis=0, keepdims=True)
     rel_sum = jnp.concatenate([rel_sum, jnp.zeros((1, 2 * DH), jnp.float32)], axis=1)
-    sum_ref[...] = jnp.sum(dcat.astype(jnp.float32), axis=0, keepdims=True) + rel_sum
-
-
-def attend_back(first, q, k, v, qrev, krev, probs, dctx):
+    sums = jnp.sum(dcat.astype(jnp.float32), axis=0, keepdims=True) + rel_sum
+    sum_ref[...] = jnp.broadcast_to(sums, sum_ref.shape)
+
+
+def attend_back(q, k, v, qrev, krev, probs, ctx, w_cat, m_mix, table, xs, attn_all):
     full_len = q.shape[1]
-    buckets = qrev.shape[1]
+    buckets, width = table.shape
     blocks = full_len // BLOCK
+    tokens, batches = lax.axis_size("seq"), lax.axis_size("batch")
+    columns = width // batches
     band_width = buckets + BLOCK
     low, wide = jnp.bfloat16, jnp.float32
     pad_blocks = blocks + band_width // BLOCK - 1
     return pl.pallas_call(
         attend_back_kernel,
         out_shape=(
-            jax.ShapeDtypeStruct((full_len, 6 * DH), low),
-            jax.ShapeDtypeStruct((buckets, 4 * DH), low),
-            jax.ShapeDtypeStruct((1, 6 * DH), wide),
+            jax.ShapeDtypeStruct((tokens // 2, 2, BLOCK, width), low),
+            jax.ShapeDtypeStruct((batches, columns, 6 * DH), low),
+            jax.ShapeDtypeStruct((batches, buckets, columns), low),
+            jax.ShapeDtypeStruct((batches, 2 * DH, columns), low),
+            jax.ShapeDtypeStruct((8, 6 * DH), wide),
         ),
-        in_specs=[pl.BlockSpec(memory_space=pltpu.SMEM)]
-        + [pl.BlockSpec(memory_space=pltpu.VMEM)] * 7,
-        out_specs=[pl.BlockSpec(memory_space=pltpu.VMEM)] * 3,
+        in_specs=[pl.BlockSpec(memory_space=pltpu.VMEM)] * 12,
+        out_specs=[pl.BlockSpec(memory_space=pltpu.VMEM)] * 5,
         scratch_shapes=[
+            pltpu.VMEM((full_len, width), low),
             pltpu.VMEM((2, full_len, DH), low),
             pltpu.VMEM((BLOCK, full_len + buckets), wide),
             pltpu.VMEM((BLOCK, full_len + buckets), low),
@@ -488,7 +575,7 @@
         ],
         compiler_params=pltpu.CompilerParams(vmem_limit_bytes=60 * 1024 * 1024),
         name="attend_back",
-    )(first, q, k, v, qrev, krev, probs, dctx)
+    )(q, k, v, qrev, krev, probs, ctx, w_cat, m_mix, table, xs, attn_all)
 
 
 MESH = pl.DeviceIdType.MESH
@@ -541,6 +628,9 @@
     def cross_peers(self):
         other = self.part + 1 - 2 * self.core
         return [(self.along_rows(k)[0], other) for k in range(1, self.batches)]
+
+    def cross_row_peers(self):
+        return self.row_peers() + self.cross_peers()
 
     def seq_peers(self):
         return [self.along_seq(k)[1] for k in range(1, self.tokens)]
@@ -616,7 +706,7 @@
 
 
 def gather_kernel(
-    x_ref, qkv_ref, mt_ref, vec_ref, up_ref, down_ref,
+    x_ref, wq_ref, wk_ref, wv_ref, mix_ref, table_ref, vec_ref, up_ref, down_ref,
     xs_ref, qkvs_ref, mts_ref, vecs_ref, up2_ref, down2_ref, *sems,
 ):
     at = Place()
@@ -635,31 +725,42 @@
 
     pl.semaphore_wait(barrier, len(peers) + off_diagonal.astype(jnp.int32))
 
-    k = wires.used[0]
-    wires.used[0] += 1
-    swap = pltpu.make_async_remote_copy(
-        src_ref=qkv_ref,
-        dst_ref=qkvs_ref.at[2 * z + c],
-        send_sem=sems[0].at[k],
-        recv_sem=sems[1].at[k],
-        device_id=turned,
-        device_id_type=MESH,
-    )
-    stay = pltpu.make_async_copy(qkv_ref, qkvs_ref.at[2 * b + c], sems[2].at[0])
-    wires.used[1] += 1
+    swaps, stays = [], []
+    for i, ref in enumerate((wq_ref, wk_ref, wv_ref)):
+        k = wires.used[0]
+        wires.used[0] += 1
+        swaps.append(
+            pltpu.make_async_remote_copy(
+                src_ref=ref,
+                dst_ref=qkvs_ref.at[2 * z + c, i],
+                send_sem=sems[0].at[k],
+                recv_sem=sems[1].at[k],
+                device_id=turned,
+                device_id_type=MESH,
+            )
+        )
+        stays.append(pltpu.make_async_copy(ref, qkvs_ref.at[2 * b + c, i], sems[2].at[i]))
+        wires.used[1] += 1
 
     @pl.when(off_diagonal)
     def _():
-        swap.start()
+        for swap in swaps:
+            swap.start()
 
     @pl.when(jnp.logical_not(off_diagonal))
     def _():
-        stay.start()
-
+        for stay in stays:
+            stay.start()
+
+    rows = mix_ref.shape[0]
+    table_rows = table_ref.shape[0]
+    mix_home = mts_ref.at[c, b, z, pl.ds(0, rows)]
+    table_home = mts_ref.at[c, b, z, pl.ds(rows, table_rows)]
     mt_sends = []
     for k in range(1, at.chips):
         peer = at.along_chips(k)[1]
-        mt_sends.append(wires.send(mt_ref, mts_ref.at[c, b, z], peer))
+        mt_sends.append(wires.send(mix_ref, mix_home, peer))
+        mt_sends.append(wires.send(table_ref, table_home, peer))
     x_sends, vec_sends = [], []
     for k in range(1, at.chips):
         peer = at.along_chips(k)[1]
@@ -667,7 +768,8 @@
         vec_sends.append(wires.send(vec_ref, vecs_ref.at[s], peer))
     own = [
         wires.local(x_ref, xs_ref.at[s]),
-        wires.local(mt_ref, mts_ref.at[c, b, z]),
+        wires.local(mix_ref, mix_home),
+        wires.local(table_ref, table_home),
         wires.local(vec_ref, vecs_ref.at[s]),
     ]
     last = [
@@ -679,11 +781,13 @@
 
     @pl.when(off_diagonal)
     def _():
-        swap.wait_recv()
+        for swap in swaps:
+            swap.wait_recv()
 
     @pl.when(jnp.logical_not(off_diagonal))
     def _():
-        stay.wait()
+        for stay in stays:
+            stay.wait()
 
     for k in range(1, 2 * at.batches):
         peer = at.along_plane(k)[2]
@@ -713,120 +817,211 @@
 
     @pl.when(off_diagonal)
     def _():
-        swap.wait_send()
-
-
-def gather_inputs(x, qkv, mt, vec, up, down):
+        for swap in swaps:
+            swap.wait_send()
+
+
+def gather_inputs(x, w_query, w_key, w_value, w_mix, rel_table, vec, up, down):
     tokens, batches = lax.axis_size("seq"), lax.axis_size("batch")
     chips = tokens // 2
+    rows, columns = w_mix.shape
     outs = (
         like(x, tokens),
-        like(qkv, tokens),
-        like(mt, 2, batches, chips),
+        like(w_query, tokens, 3),
+        jax.ShapeDtypeStruct(
+            (2, batches, chips, rows + rel_table.shape[0], columns), w_mix.dtype
+        ),
         like(vec, tokens),
         like(up),
         like(down),
     )
-    sends = 1 + 3 * (chips - 1) + 4 + 2 * batches - 1 + 2 * (batches - 1) + 1 + 2 * (chips - 1)
-    return comm_call(
-        gather_kernel, "gather_inputs", 0, outs, (x, qkv, mt, vec, up, down), sends, 4
-    )
-
-
-def swap_kernel(src_ref, dst_ref, *sems):
+    sends = 3 + 4 * (chips - 1) + 4 + 2 * batches - 1 + 2 * (batches - 1) + 1 + 2 * (chips - 1)
+    inputs = (x, w_query, w_key, w_value, w_mix, rel_table, vec, up, down)
+    return comm_call(gather_kernel, "gather_inputs", 0, outs, inputs, sends, 7)
+
+
+def norm_parts(values):
+    average = jnp.mean(values, axis=-1, keepdims=True)
+    centered = values - average
+    variance = jnp.mean(centered * centered, axis=-1, keepdims=True)
+    scale = lax.rsqrt(variance + norm_eps)
+    return centered * scale, scale
+
+
+def norm_back(grad, gain, unit, scale):
+    inner = grad * gain
+    mean = jnp.mean(inner, axis=-1, keepdims=True)
+    slope = jnp.mean(inner * unit, axis=-1, keepdims=True)
+    return scale * (inner - mean - unit * slope)
+
+
+def feed_kernel(
+    ctx_ref, x_ref, mix_ref, vecs_ref, up_ref, down_ref, up2_ref, down2_ref, out_grad_ref,
+    output_ref, pre_grad_ref, sums_ref, attn_ref, ups_ref, downs_ref, upbs_ref,
+    got_ref, hid_ref, act_ref, slope_ref, part_ref, ffn_ref, grad_ref, inner_ref,
+    back_ref, backs_ref, low_ref, upg_ref, downg_ref, upb_ref, vec_ref, *sems,
+):
     at = Place()
     wires = Wires(*sems)
-    meet(at.seq_peers())
-    copies = []
+    low, wide = jnp.bfloat16, jnp.float32
+    s, z, c = at.part, at.chip, at.core
+    meet(at.seq_peers() + at.cross_row_peers())
+    last, own = [], []
+    swaps = []
     for k in range(1, at.tokens):
         part, peer = at.along_seq(k)
-        copies.append(wires.send(src_ref.at[part], dst_ref.at[at.part], peer))
-    own = wires.local(src_ref.at[at.part], dst_ref.at[at.part])
-    for copy in copies:
+        swaps.append(wires.send(ctx_ref.at[part], got_ref.at[s], peer))
+    kept = wires.local(ctx_ref.at[s], got_ref.at[s])
+    lanes = x_ref.shape[1] // at.tokens
+    hidden_here = up_ref.shape[1]
+    vec_ref[...] = jnp.concatenate(
+        [vecs_ref[part, :, :lanes].astype(wide) for part in range(at.tokens)], axis=1
+    )
+    bias3 = vec_ref[3:4]
+    gain1, gain2 = vec_ref[4:5], vec_ref[5:6]
+    shift1, shift2 = vec_ref[6:7], vec_ref[7:8]
+    bias_down = vec_ref[8:9]
+    partner = s + 1 - 2 * c
+    up_rows = hidden_here // BLOCK
+    bias_up = jnp.concatenate(
+        [vecs_ref[s, 10 + i : 11 + i].astype(wide) for i in range(up_rows)]
+        + [vecs_ref[partner, 10 + i : 11 + i].astype(wide) for i in range(up_rows)],
+        axis=1,
+    )
+    for copy in swaps:
         copy.wait_recv()
-    own.wait()
-    wires.finish()
-
-
-def swap_seq(blocks, ident):
-    tokens = lax.axis_size("seq")
-    return comm_call(
-        swap_kernel, "swap_seq", ident, (like(blocks),), (blocks,), tokens - 1, 1
-    )[0]
-
-
-def class_gather_kernel(src_ref, dst_ref, *sems):
-    at = Place()
-    wires = Wires(*sems)
-    meet(at.chip_peers())
-    copies = [
-        wires.send(src_ref, dst_ref.at[at.chip], at.along_chips(k)[1])
+    kept.wait()
+    pieces = []
+    for chip in range(at.chips):
+        left, right = got_ref[2 * chip], got_ref[2 * chip + 1]
+        middle = left[:, DH:].astype(wide) + right[:, :DH].astype(wide)
+        pieces += [left[:, :DH], middle.astype(low), right[:, DH:]]
+    context = jnp.concatenate(pieces, axis=1)
+    pre_norm = x_ref[...].astype(wide) + dot_nn(context, mix_ref[...]) + bias3
+    unit1, scale1 = norm_parts(pre_norm)
+    hidden = unit1 * gain1 + shift1
+    hid_ref[z] = hidden.astype(low)
+    spread = [
+        wires.send(hid_ref.at[z], hid_ref.at[z], at.along_chips(k)[1]) for k in range(1, at.chips)
+    ]
+
+    ffn_sends = []
+    for k in range(at.chips):
+        chip = at.from_chips(k)
+        if k:
+            spread[k - 1].wait_recv()
+        rows = hid_ref[chip]
+        inner = jnp.concatenate(
+            [dot_nn(rows, up_ref[...]), dot_nn(rows, up2_ref[...])], axis=1
+        )
+        inner = inner + bias_up
+        cdf = 0.5 * (1.0 + lax.erf(inner * math.sqrt(0.5)))
+        act = (inner * cdf).astype(low)
+        slope_ref[chip] = cdf + inner * (
+            jnp.exp(-0.5 * inner * inner) * (1.0 / math.sqrt(2.0 * math.pi))
+        )
+        act_ref[chip] = act
+        part_ref[chip] = (
+            dot_nn(act[:, :hidden_here], down_ref[...])
+            + dot_nn(act[:, hidden_here:], down2_ref[...])
+        ).astype(low)
+        if k:
+            peer = (at.row, 2 * chip + c)
+            ffn_sends.append(wires.send(part_ref.at[chip], ffn_ref.at[at.chips - 1 - k], peer))
+    total = part_ref[z].astype(wide)
+    for k in range(1, at.chips):
+        ffn_sends[k - 1].wait_recv()
+        total = total + ffn_ref[at.chips - 1 - k].astype(wide)
+    mixed = hidden + total + bias_down
+    unit2, scale2 = norm_parts(mixed)
+    output_ref[...] = (unit2 * gain2 + shift2).astype(low)
+    out_grad = out_grad_ref[...].astype(wide)
+    mixed_grad = norm_back(out_grad, gain2, unit2, scale2)
+    grad_ref[z] = mixed_grad.astype(low)
+    spread = [
+        wires.send(grad_ref.at[z], grad_ref.at[z], at.along_chips(k)[1])
         for k in range(1, at.chips)
     ]
-    own = wires.local(src_ref, dst_ref.at[at.chip])
-    for copy in copies:
-        copy.wait_recv()
-    own.wait()
-    wires.finish()
-
-
-def class_gather(block, ident):
-    chips = lax.axis_size("seq") // 2
-    return comm_call(
-        class_gather_kernel, "class_gather", ident, (like(block, chips),), (block,), chips - 1, 1
-    )[0]
-
-
-def class_scatter_kernel(src_ref, dst_ref, *sems):
-    at = Place()
-    wires = Wires(*sems)
-    meet(at.chip_peers())
-    copies = []
-    for k in range(1, at.chips):
-        chip, peer = at.along_chips(k)
-        copies.append(wires.send(src_ref.at[chip], dst_ref.at[at.chip], peer))
-    own = wires.local(src_ref.at[at.chip], dst_ref.at[at.chip])
-    for copy in copies:
-        copy.wait_recv()
-    own.wait()
-    wires.finish()
-
-
-def class_scatter(blocks, ident):
-    chips = lax.axis_size("seq") // 2
-    return comm_call(
-        class_scatter_kernel, "class_scatter", ident, (like(blocks),), (blocks,), chips - 1, 1
-    )[0]
-
-
-def plane_sends(at, wires, src_ref, dst_ref):
-    mine = 2 * at.row + at.core
-    copies = []
+    gain2_grad = jnp.sum(out_grad * unit2, axis=0, keepdims=True)
+    shift2_grad = jnp.sum(out_grad, axis=0, keepdims=True)
+    downb_grad = jnp.sum(mixed_grad, axis=0, keepdims=True)
+
+    back_sends = []
+    for k in range(at.chips):
+        chip = at.from_chips(k)
+        if k:
+            spread[k - 1].wait_recv()
+        rows = grad_ref[chip]
+        act_grad = jnp.concatenate(
+            [dot_nt(rows, down_ref[...]), dot_nt(rows, down2_ref[...])], axis=1
+        )
+        inner_low = (act_grad * slope_ref[chip]).astype(low)
+        inner_ref[chip] = inner_low
+        back_ref[chip] = (
+            dot_nt(inner_low[:, :hidden_here], up_ref[...])
+            + dot_nt(inner_low[:, hidden_here:], up2_ref[...])
+        ).astype(low)
+        if k:
+            peer = (at.row, 2 * chip + c)
+            back_sends.append(wires.send(back_ref.at[chip], backs_ref.at[at.chips - 1 - k], peer))
+
+    width = x_ref.shape[1]
+    columns = width // at.batches
+    inner_all = inner_ref[...].reshape(at.chips * BLOCK, 2 * hidden_here)
+    act_all = act_ref[...].reshape(at.chips * BLOCK, 2 * hidden_here)
+    hid_all = hid_ref[...].reshape(at.chips * BLOCK, width)
+    grad_all = grad_ref[...].reshape(at.chips * BLOCK, width)
+    up_grad = dot_tn(hid_all, inner_all).astype(low)
+    down_grad = dot_tn(act_all, grad_all).astype(low)
+    upb_grad = jnp.sum(inner_all.astype(wide), axis=0, keepdims=True)
+    for d in range(2):
+        half = slice(d * hidden_here, (d + 1) * hidden_here)
+        upb_ref[d] = jnp.broadcast_to(upb_grad[:, half], upb_ref.shape[1:])
+        for row in range(at.batches):
+            piece = slice(row * columns, (row + 1) * columns)
+            upg_ref[d, row] = up_grad[piece, half]
+            downg_ref[d, row] = down_grad[half, piece]
+    mine = 2 * at.row + c
     for k in range(1, 2 * at.batches):
         row, core, peer = at.along_plane(k)
-        other = lax.rem(core + at.core, 2)
-        copies.append(wires.send(src_ref.at[other, row], dst_ref.at[mine], peer))
-    return copies, wires.local(src_ref.at[0, at.row], dst_ref.at[mine])
-
-
-def spread_kernel(src_ref, up_ref, upb_ref, dst_ref, ups_ref, upbs_ref, *sems):
-    at = Place()
-    wires = Wires(*sems)
-    meet(at.chip_peers() + at.plane_peers())
-    copies = [
-        wires.send(src_ref, dst_ref.at[at.part], at.along_chips(k)[1])
-        for k in range(1, at.chips)
+        other = lax.rem(core + c, 2)
+        last.append(wires.send(upg_ref.at[other, row], ups_ref.at[mine], peer))
+        last.append(wires.send(downg_ref.at[other, row], downs_ref.at[mine], peer))
+        last.append(wires.send(upb_ref.at[other], upbs_ref.at[mine], peer))
+    own.append(wires.local(upg_ref.at[0, at.row], ups_ref.at[mine]))
+    own.append(wires.local(downg_ref.at[0, at.row], downs_ref.at[mine]))
+    own.append(wires.local(upb_ref.at[0], upbs_ref.at[mine]))
+
+    total = back_ref[z].astype(wide)
+    for k in range(1, at.chips):
+        back_sends[k - 1].wait_recv()
+        total = total + backs_ref[at.chips - 1 - k].astype(wide)
+    hidden_grad = mixed_grad + total
+    pre_grad = norm_back(hidden_grad, gain1, unit1, scale1)
+    low_ref[...] = pre_grad.astype(low)
+    spread = [
+        wires.send(low_ref, attn_ref.at[s], at.along_chips(k)[1]) for k in range(1, at.chips)
     ]
-    last = [wires.send(src_ref, dst_ref.at[at.part], at.partner())]
-    own = [wires.local(src_ref, dst_ref.at[at.part])]
-    for src, dst in ((up_ref, ups_ref), (upb_ref, upbs_ref)):
-        more, kept = plane_sends(at, wires, src, dst)
-        last += more
-        own.append(kept)
+    last.append(wires.send(low_ref, attn_ref.at[s], at.partner()))
+    own.append(wires.local(low_ref, attn_ref.at[s]))
+    pre_grad_ref[...] = pre_grad
+    gain1_grad = jnp.sum(hidden_grad * unit1, axis=0, keepdims=True)
+    shift1_grad = jnp.sum(hidden_grad, axis=0, keepdims=True)
+    bias3_grad = jnp.sum(pre_grad, axis=0, keepdims=True)
+    sums = jnp.concatenate(
+        [bias3_grad, gain1_grad, gain2_grad, shift1_grad, shift2_grad, downb_grad]
+        + [jnp.zeros((2, width), wide)],
+        axis=0,
+    )
+    spare = jnp.zeros((8, BLOCK - lanes), wide)
+    for part in range(at.tokens):
+        sums_ref[part] = jnp.concatenate(
+            [sums[:, part * lanes : (part + 1) * lanes], spare], axis=1
+        )
     for k in range(1, at.chips):
-        index = 2 * at.from_chips(k) + at.core
-        copies[k - 1].wait_recv()
-        last.append(wires.send(dst_ref.at[index], dst_ref.at[index], at.partner()))
+        index = 2 * at.from_chips(k) + c
+        spread[k - 1].wait_recv()
+        last.append(wires.send(attn_ref.at[index], attn_ref.at[index], at.partner()))
     for copy in last:
         copy.wait_recv()
     for copy in own:
@@ -834,135 +1029,178 @@
     wires.finish()
 
 
-def spread_grads(block, up, upb, ident):
+def feed_forward(ctx, x, m_mix, vecs, up, down, up2, down2, out_grad, ident):
     tokens, batches = lax.axis_size("seq"), lax.axis_size("batch")
     chips = tokens // 2
+    width = x.shape[1]
+    columns = width // batches
+    hidden_here = up.shape[1]
+    low, wide = jnp.bfloat16, jnp.float32
     outs = (
-        like(block, tokens),
-        jax.ShapeDtypeStruct((2 * batches,) + up.shape[2:], up.dtype),
-        jax.ShapeDtypeStruct((2 * batches,) + upb.shape[2:], upb.dtype),
-    )
-    sends = 2 * (chips - 1) + 1 + 2 * (2 * batches - 1)
-    return comm_call(spread_kernel, "spread_grads", ident, outs, (block, up, upb), sends, 3)
-
-
-def reduce_kernel(
-    in_ref, vec_ref, dw_ref, tab_ref, mix_ref,
-    ins_ref, vecs_ref, dws_ref, tabs_ref, mixs_ref, half_ref, sum_ref, *sems,
+        jax.ShapeDtypeStruct(x.shape, low),
+        jax.ShapeDtypeStruct(x.shape, wide),
+        jax.ShapeDtypeStruct((tokens, 8, BLOCK), wide),
+        jax.ShapeDtypeStruct((tokens,) + x.shape, low),
+        jax.ShapeDtypeStruct((2 * batches, columns, hidden_here), low),
+        jax.ShapeDtypeStruct((2 * batches, hidden_here, columns), low),
+        jax.ShapeDtypeStruct((2 * batches, 8, hidden_here), wide),
+    )
+    block = (chips,) + x.shape
+    wide_block = (chips, x.shape[0], 2 * hidden_here)
+    others = (chips - 1,) + x.shape
+    scratch = (
+        pltpu.VMEM(ctx.shape, low),
+        pltpu.VMEM(block, low),
+        pltpu.VMEM(wide_block, low),
+        pltpu.VMEM(wide_block, wide),
+        pltpu.VMEM(block, low),
+        pltpu.VMEM(others, low),
+        pltpu.VMEM(block, low),
+        pltpu.VMEM(wide_block, low),
+        pltpu.VMEM(block, low),
+        pltpu.VMEM(others, low),
+        pltpu.VMEM(x.shape, low),
+        pltpu.VMEM((2, batches, columns, hidden_here), low),
+        pltpu.VMEM((2, batches, hidden_here, columns), low),
+        pltpu.VMEM((2, 8, hidden_here), wide),
+        pltpu.VMEM((16, width), wide),
+    )
+    inputs = (ctx, x, m_mix, vecs, up, down, up2, down2, out_grad)
+    sends = tokens - 1 + 4 * (chips - 1) + 3 * (2 * batches - 1) + 2 * (chips - 1) + 1
+    return pl.pallas_call(
+        feed_kernel,
+        out_shape=outs,
+        in_specs=[VMEM_SPEC] * len(inputs),
+        out_specs=(VMEM_SPEC,) * 3 + (ANY_SPEC,) * 4,
+        scratch_shapes=list(scratch) + wire_scratch(sends, 5),
+        compiler_params=pltpu.CompilerParams(
+            collective_id=ident, has_side_effects=True, vmem_limit_bytes=60 * 1024 * 1024
+        ),
+        name="feed_forward",
+    )(*inputs)
+
+
+def settle_kernel(
+    in_ref, vec_ref, col_ref, dw_ref, tab_ref, mix_ref,
+    ins_ref, vec_all_ref, cols_ref, dw_all_ref, tab_all_ref, mix_all_ref,
+    half_ref, sum_ref, vecs_ref, vec_low_ref, dws_ref, dw_low_ref, tabs_ref, tab_low_ref,
+    mixs_ref, mix_low_ref, *sems,
 ):
     at = Place()
     wires = Wires(*sems)
-    meet(at.seq_peers() + at.row_peers())
-    c = at.core
+    low, wide = jnp.bfloat16, jnp.float32
+    b, s, z, c = at.row, at.part, at.chip, at.core
+    off_diagonal = b != z
+    same, cross = (z, 2 * b + c), (z, 2 * b + 1 - c)
+    peers = at.seq_peers() + at.cross_row_peers()
+    barrier = pltpu.get_barrier_semaphore()
+    for peer in peers:
+        pl.semaphore_signal(barrier, inc=1, device_id=peer, device_id_type=MESH)
+
+    @pl.when(off_diagonal)
+    def _():
+        pl.semaphore_signal(barrier, inc=1, device_id=same, device_id_type=MESH)
+        pl.semaphore_signal(barrier, inc=1, device_id=cross, device_id_type=MESH)
+
+    pl.semaphore_wait(barrier, len(peers) + 2 * off_diagonal.astype(jnp.int32))
+
+    dw_sends, tab_sends, mix_sends, vec_sends, last, own = [], [], [], [], [], []
+    for k in range(1, at.batches):
+        row, peer = at.along_rows(k)
+        dw_sends.append(wires.send(dw_ref.at[row], dws_ref.at[k - 1], peer))
     halves = [
         wires.send(in_ref.at[chip, 1 - c], half_ref.at[chip], at.partner())
         for chip in range(at.chips)
     ]
-    last, own = [], []
     for k in range(1, at.batches):
         row, peer = at.along_rows(k)
-        for src, dst in ((dw_ref, dws_ref), (tab_ref, tabs_ref), (mix_ref, mixs_ref)):
-            last.append(wires.send(src.at[row], dst.at[at.row], peer))
-    for src, dst in ((dw_ref, dws_ref), (tab_ref, tabs_ref), (mix_ref, mixs_ref)):
-        own.append(wires.local(src.at[at.row], dst.at[at.row]))
+        tab_sends.append(wires.send(tab_ref.at[row], tabs_ref.at[k - 1], peer))
+    for k in range(1, at.batches):
+        row, peer = at.along_rows(k)
+        mix_sends.append(wires.send(mix_ref.at[row], mixs_ref.at[k - 1], peer))
     for k in range(1, at.tokens):
         part, peer = at.along_seq(k)
-        last.append(wires.send(vec_ref.at[part], vecs_ref.at[at.part], peer))
-    own.append(wires.local(vec_ref.at[at.part], vecs_ref.at[at.part]))
-    for copy in halves:
-        copy.wait_recv()
-    sum_ref[...] = (
-        in_ref[:, c].astype(jnp.float32) + half_ref[...].astype(jnp.float32)
-    ).astype(jnp.bfloat16)
+        vec_sends.append(wires.send(vec_ref.at[part], vecs_ref.at[k - 1], peer))
+    mine = 2 * b + c
+    for k in range(1, 2 * at.batches):
+        last.append(wires.send(col_ref, cols_ref.at[mine], at.along_plane(k)[2]))
+    own.append(wires.local(col_ref, cols_ref.at[mine]))
+
+    total = dw_ref[b].astype(wide)
+    for k in range(1, at.batches):
+        dw_sends[k - 1].wait_recv()
+        total = total + dws_ref[k - 1].astype(wide)
+    shard_rows = dw_low_ref.shape[1]
+    for half in range(2):
+        dw_low_ref[half] = total[half * shard_rows : (half + 1) * shard_rows].astype(low)
+    k = wires.used[0]
+    wires.used[0] += 1
+    move = pltpu.make_async_remote_copy(
+        src_ref=dw_low_ref.at[c],
+        dst_ref=dw_all_ref.at[c],
+        send_sem=sems[0].at[k],
+        recv_sem=sems[1].at[k],
+        device_id=same,
+        device_id_type=MESH,
+    )
+    stay = pltpu.make_async_copy(
+        dw_low_ref.at[c], dw_all_ref.at[c], sems[2].at[wires.used[1]]
+    )
+    wires.used[1] += 1
+
+    @pl.when(off_diagonal)
+    def _():
+        move.start()
+
+    @pl.when(jnp.logical_not(off_diagonal))
+    def _():
+        stay.start()
+
+    last.append(wires.send(dw_low_ref.at[1 - c], dw_all_ref.at[c], cross))
+
+    for chip in range(at.chips):
+        halves[chip].wait_recv()
+        sum_ref[chip] = (in_ref[chip, c].astype(wide) + half_ref[chip].astype(wide)).astype(low)
     for k in range(1, at.chips):
         chip, peer = at.along_chips(k)
-        last.append(wires.send(sum_ref.at[chip], ins_ref.at[at.chip], peer))
-    own.append(wires.local(sum_ref.at[at.chip], ins_ref.at[at.chip]))
+        last.append(wires.send(sum_ref.at[chip], ins_ref.at[z], peer))
+    own.append(wires.local(sum_ref.at[z], ins_ref.at[z]))
+
+    total = tab_ref[b].astype(wide)
+    for k in range(1, at.batches):
+        tab_sends[k - 1].wait_recv()
+        total = total + tabs_ref[k - 1].astype(wide)
+    table_rows = tab_low_ref.shape[1]
+    for part in range(at.tokens):
+        tab_low_ref[part] = total[part * table_rows : (part + 1) * table_rows].astype(low)
+    for k in range(1, at.tokens):
+        part, peer = at.along_seq(k)
+        last.append(wires.send(tab_low_ref.at[part], tab_all_ref.at[s], peer))
+    own.append(wires.local(tab_low_ref.at[s], tab_all_ref.at[s]))
+
+    total = mix_ref[b].astype(wide)
+    for k in range(1, at.batches):
+        mix_sends[k - 1].wait_recv()
+        total = total + mixs_ref[k - 1].astype(wide)
+    mix_low_ref[...] = total.astype(low)
+    last.append(wires.send(mix_low_ref, mix_all_ref.at[c], at.partner()))
+    own.append(wires.local(mix_low_ref, mix_all_ref.at[c]))
+
+    total = vec_ref[s]
+    for k in range(1, at.tokens):
+        vec_sends[k - 1].wait_recv()
+        total = total + vecs_ref[k - 1]
+    vec_low_ref[...] = total
+    for k in range(1, at.batches):
+        last.append(wires.send(vec_low_ref, vec_all_ref.at[b], at.along_rows(k)[1]))
+    own.append(wires.local(vec_low_ref, vec_all_ref.at[b]))
+
     for copy in last:
         copy.wait_recv()
     for copy in own:
         copy.wait()
     wires.finish()
 
-
-def reduce_grads(in_part, vec, dw, tab, mix, ident):
-    tokens, batches = lax.axis_size("seq"), lax.axis_size("batch")
-    chips = tokens // 2
-    half = (chips,) + in_part.shape[2:]
-    outs = (jax.ShapeDtypeStruct(half, in_part.dtype), like(vec), like(dw), like(tab), like(mix))
-    sends = chips + 3 * (batches - 1) + tokens - 1 + chips - 1
-    return comm_call(
-        reduce_kernel,
-        "reduce_grads",
-        ident,
-        outs,
-        (in_part, vec, dw, tab, mix),
-        sends,
-        5,
-        scratch=(pltpu.VMEM(half, in_part.dtype), pltpu.VMEM(half, in_part.dtype)),
-    )
-
-
-def settle_kernel(
-    dw_ref, tab_ref, mix_ref, vec_ref, down_ref,
-    dws_ref, tabs_ref, mixs_ref, vecs_ref, downs_ref, *sems,
-):
-    at = Place()
-    wires = Wires(*sems)
-    b, z, c = at.row, at.chip, at.core
-    off_diagonal = b != z
-    same, cross = (z, 2 * b + c), (z, 2 * b + 1 - c)
-    peers = at.seq_peers() + at.row_peers() + at.cross_peers()
-    barrier = pltpu.get_barrier_semaphore()
-    for peer in peers:
-        pl.semaphore_signal(barrier, inc=1, device_id=peer, device_id_type=MESH)
-
-    @pl.when(off_diagonal)
-    def _():
-        pl.semaphore_signal(barrier, inc=1, device_id=same, device_id_type=MESH)
-        pl.semaphore_signal(barrier, inc=1, device_id=cross, device_id_type=MESH)
-
-    pl.semaphore_wait(barrier, len(peers) + 2 * off_diagonal.astype(jnp.int32))
-
-    k = wires.used[0]
-    wires.used[0] += 1
-    move = pltpu.make_async_remote_copy(
-        src_ref=dw_ref.at[c],
-        dst_ref=dws_ref.at[c],
-        send_sem=sems[0].at[k],
-        recv_sem=sems[1].at[k],
-        device_id=same,
-        device_id_type=MESH,
-    )
-    stay = pltpu.make_async_copy(dw_ref.at[c], dws_ref.at[c], sems[2].at[0])
-    wires.used[1] += 1
-
-    @pl.when(off_diagonal)
-    def _():
-        move.start()
-
-    @pl.when(jnp.logical_not(off_diagonal))
-    def _():
-        stay.start()
-
-    last, own = [wires.send(dw_ref.at[1 - c], dws_ref.at[c], cross)], []
-    for k in range(1, at.tokens):
-        part, peer = at.along_seq(k)
-        last.append(wires.send(tab_ref.at[part], tabs_ref.at[at.part], peer))
-    own.append(wires.local(tab_ref.at[at.part], tabs_ref.at[at.part]))
-    last.append(wires.send(mix_ref, mixs_ref, at.partner()))
-    for k in range(1, at.batches):
-        last.append(wires.send(vec_ref, vecs_ref.at[b], at.along_rows(k)[1]))
-    own.append(wires.local(vec_ref, vecs_ref.at[b]))
-    more, kept = plane_sends(at, wires, down_ref, downs_ref)
-    last += more
-    own.append(kept)
-    for copy in last:
-        copy.wait_recv()
-    for copy in own:
-        copy.wait()
-    wires.finish()
-
     @pl.when(off_diagonal)
     def _():
         move.wait()
@@ -972,22 +1210,107 @@
         stay.wait()
 
 
-def settle_grads(dw, tab, mix, vec, down, ident):
+def settle_grads(in_part, vec, cols, dw, tab, mix, ident):
     tokens, batches = lax.axis_size("seq"), lax.axis_size("batch")
+    chips = tokens // 2
+    low, wide = jnp.bfloat16, jnp.float32
+    half = (chips,) + in_part.shape[2:]
+    columns, group = dw.shape[1:]
+    buckets, table_cols = tab.shape[1:]
+    dw_pieces = (2, columns // 2, group)
+    tab_pieces = (tokens, buckets // tokens, table_cols)
+    mix_piece = mix.shape[1:]
     outs = (
-        like(dw),
-        like(tab),
-        like(mix),
-        like(vec, batches),
-        jax.ShapeDtypeStruct((2 * batches,) + down.shape[2:], down.dtype),
-    )
-    sends = 2 + tokens - 1 + 1 + batches - 1 + 2 * batches - 1
-    return comm_call(
-        settle_kernel, "settle_grads", ident, outs, (dw, tab, mix, vec, down), sends, 4
-    )
-
-
-def fits_fast(layer_input, table_shard, w_query):
+        jax.ShapeDtypeStruct(half, low),
+        jax.ShapeDtypeStruct((batches,) + vec.shape[1:], wide),
+        like(cols, 2 * batches),
+        jax.ShapeDtypeStruct(dw_pieces, low),
+        jax.ShapeDtypeStruct(tab_pieces, low),
+        jax.ShapeDtypeStruct((2,) + mix_piece, low),
+    )
+    scratch = (
+        pltpu.VMEM(half, low),
+        pltpu.VMEM(half, low),
+        pltpu.VMEM((tokens - 1,) + vec.shape[1:], wide),
+        pltpu.VMEM(vec.shape[1:], wide),
+        pltpu.VMEM((batches - 1,) + dw.shape[1:], low),
+        pltpu.VMEM(dw_pieces, low),
+        pltpu.VMEM((batches - 1,) + tab.shape[1:], low),
+        pltpu.VMEM(tab_pieces, low),
+        pltpu.VMEM((batches - 1,) + mix_piece, low),
+        pltpu.VMEM(mix_piece, low),
+    )
+    sends = (
+        3 * (batches - 1) + chips + tokens - 1 + 2 * batches - 1
+        + 2 + chips - 1 + tokens - 1 + 1 + batches - 1
+    )
+    inputs = (in_part, vec, cols, dw, tab, mix)
+    return comm_call(settle_kernel, "settle_grads", ident, outs, inputs, sends, 6, scratch=scratch)
+
+
+def finish_kernel(
+    pre_ref, ins_ref, vecs_ref, cols_ref, dws_ref, tabs_ref, mixs_ref, ups_ref, downs_ref,
+    upbs_ref,
+    input_ref, dq_ref, dk_ref, dv_ref, mix_ref, table_ref, bias_ref, gain_ref, shift_ref,
+    up_ref, upb_ref, down_ref, downb_ref,
+):
+    at = Place()
+    wide = jnp.float32
+
+    def total(ref):
+        out = ref[0].astype(wide)
+        for k in range(1, ref.shape[0]):
+            out = out + ref[k].astype(wide)
+        return out
+
+    input_ref[...] = pre_ref[...] + total(ins_ref)
+    up_ref[...] = total(ups_ref)
+    down_ref[...] = total(downs_ref)
+    upb_ref[...] = total(upbs_ref)[0:1]
+    table_ref[...] = total(tabs_ref)
+    group = 2 * DH
+    spare = jnp.zeros((dws_ref.shape[1], DH), wide)
+    for i, ref in enumerate((dq_ref, dk_ref, dv_ref)):
+        lower = dws_ref[0, :, i * group : (i + 1) * group].astype(wide)
+        upper = dws_ref[1, :, i * group : (i + 1) * group].astype(wide)
+        ref[...] = jnp.concatenate([lower, spare], axis=1) + jnp.concatenate(
+            [spare, upper], axis=1
+        )
+    rows = mix_ref.shape[0]
+    lower, upper = mixs_ref[0].astype(wide), mixs_ref[1].astype(wide)
+    spare = jnp.zeros((DH, lower.shape[1]), wide)
+    whole = jnp.concatenate([lower, spare], axis=0) + jnp.concatenate([spare, upper], axis=0)
+    mix_ref[...] = jnp.where(at.core == 0, whole[:rows], whole[rows:])
+    small = total(vecs_ref)
+    lanes = bias_ref.shape[1]
+    cols = [cols_ref[core, 0:1] for core in range(2)]
+    for row in range(1, at.batches):
+        cols = [cols[core] + cols_ref[2 * row + core, 0:1] for core in range(2)]
+    spare = jnp.zeros((1, DH), wide)
+    biases = []
+    for i in range(3):
+        lower, upper = [part[:, i * group : (i + 1) * group] for part in cols]
+        both = jnp.concatenate([lower, spare], axis=1) + jnp.concatenate([spare, upper], axis=1)
+        biases.append(jnp.where(at.core == 0, both[:, :lanes], both[:, lanes:]))
+    bias_ref[...] = jnp.concatenate(biases + [small[0:1, :lanes]], axis=0)
+    gain_ref[...] = small[1:3, :lanes]
+    shift_ref[...] = small[3:5, :lanes]
+    downb_ref[...] = small[5:6, :lanes]
+
+
+def finish(pre_grad, parts, shapes):
+    inputs = (pre_grad,) + tuple(parts)
+    return pl.pallas_call(
+        finish_kernel,
+        out_shape=tuple(jax.ShapeDtypeStruct(shape, jnp.float32) for shape in shapes),
+        in_specs=[VMEM_SPEC] * len(inputs),
+        out_specs=(VMEM_SPEC,) * len(shapes),
+        compiler_params=pltpu.CompilerParams(vmem_limit_bytes=40 * 1024 * 1024),
+        name="finish",
+    )(*inputs)
+
+
+def fits_fast(layer_input, table_shard, hidden_here):
     rows, local_len, width = layer_input.shape
     tokens, batches = lax.axis_size("seq"), lax.axis_size("batch")
     return (
@@ -997,6 +1320,8 @@
         and width == 3 * DH * batches
         and (table_shard.shape[0] * tokens) % (4 * BLOCK) == 0
         and tokens % 4 == 0
+        and 10 + hidden_here // BLOCK <= 16
+        and hidden_here % BLOCK == 0
     )
 
 
@@ -1005,185 +1330,45 @@
     norm_gains, norm_shifts, w_up, up_bias, w_down, down_bias, out_grad,
 ):
     local_len, width = layer_input.shape[1:]
-    at = Place()
-    tokens, batches, chips = at.tokens, at.batches, at.chips
-    full_len = local_len * tokens
-    low, wide = jnp.bfloat16, jnp.float32
-    pair = 2 * DH
+    low = jnp.bfloat16
     shard_rows, shard_cols = w_query.shape
-    table_rows = rel_table.shape[0]
     lanes = attn_biases.shape[1]
     hidden_here = w_up.shape[1]
     x = layer_input[0]
-
     pack = jnp.concatenate([attn_biases, norm_gains, norm_shifts, down_bias[None]], axis=0)
     pack = jnp.pad(pack, ((0, 0), (0, BLOCK - lanes)))
     pack = jnp.concatenate(
         [pack, segment_ids.astype(low), up_bias.reshape(hidden_here // BLOCK, BLOCK)], axis=0
     )
-    used = pack.shape[0]
-    pack = jnp.pad(pack, ((0, 16 - used), (0, 0)))
-    qkv = jnp.stack([w_query, w_key, w_value])
-    mt = jnp.concatenate([w_mix, rel_table], axis=0)
-    x_all, qkv_all, mt_all, vec_all, up_other, down_other = gather_inputs(
-        x, qkv, mt, pack, w_up, w_down
-    )
-    x_all = x_all.reshape(full_len, width)
-    vecs = vec_all[:, :9, :lanes].transpose(1, 0, 2).reshape(9, width)
-    biases, gains, shifts = vecs[0:4], vecs[4:6].astype(wide), vecs[6:8].astype(wide)
-    bias_down = vecs[8]
-    seg = vec_all[:, 9].reshape(full_len).astype(wide)
-    other_vec = lax.dynamic_index_in_dim(
-        vec_all, at.part + 1 - 2 * at.core, axis=0, keepdims=False
-    )
-    bias_up = jnp.concatenate([up_bias, other_vec[10:used].reshape(hidden_here)])
-    column = at.core * DH
-    wcols = qkv_all.transpose(0, 2, 1, 3).reshape(width, 3, shard_cols)
-    w_cat = lax.dynamic_slice_in_dim(wcols, column, pair, axis=2).reshape(width, 3 * pair)
-    first_col = at.chip * shard_cols + column
-    bias_cat = (
-        lax.dynamic_slice_in_dim(biases[:3], first_col, pair, axis=1)
-        .reshape(1, 3 * pair)
-        .astype(wide)
-    )
-    m_mix = mt_all[..., :shard_rows, :].transpose(2, 0, 3, 1, 4).reshape(width, width)
-    table = (
-        mt_all[..., shard_rows:, :].transpose(2, 0, 3, 1, 4).reshape(tokens * table_rows, width)
-    )
-
-    first = (at.core * (full_len // BLOCK // 2)).astype(jnp.int32).reshape(1)
-    q, k, v, qrev, krev, probs, ctx = attend(
-        first, x_all, w_cat, bias_cat, table, seg[:, None], seg[None, :]
-    )
-    got = swap_seq(ctx.reshape(tokens, local_len, pair), 1)
-    got = got.reshape(chips, 2, local_len, pair)
-    left, right = got[:, 0], got[:, 1]
-    context = jnp.concatenate(
-        [left[..., :DH], left[..., DH:] + right[..., :DH], right[..., DH:]], axis=-1
-    )
-    context_low = context.transpose(1, 0, 2).reshape(local_len, width)
-    pre_norm = (
-        x.astype(wide) + jnp.dot(context_low, m_mix, preferred_element_type=wide) + biases[3]
-    )
-    hidden, norm1_pull = jax.vjp(normalize, pre_norm, gains[0], shifts[0])
-    hidden_rows = class_gather(hidden.astype(low), 2).reshape(chips * local_len, width)
-    up_pair = jnp.concatenate([w_up, up_other], axis=1)
-    down_pair = jnp.concatenate([w_down, down_other], axis=0)
-    inner = jnp.dot(hidden_rows, up_pair, preferred_element_type=wide) + bias_up
-    act, gelu_pull = jax.vjp(exact_gelu, inner)
-    act_low = act.astype(low)
-    ffn_part = jnp.dot(act_low, down_pair, preferred_element_type=wide).astype(low)
-    ffn_parts = class_scatter(ffn_part.reshape(chips, local_len, width), 3)
-    mixed = hidden + jnp.sum(ffn_parts.astype(wide), axis=0) + bias_down
-    output, norm2_pull = jax.vjp(normalize, mixed, gains[1], shifts[1])
-    mixed_grad, gain2_grad, shift2_grad = norm2_pull(out_grad[0].astype(wide))
-    grad_rows = class_gather(mixed_grad.astype(low), 4).reshape(chips * local_len, width)
-    act_grad = jnp.einsum("nd,fd->nf", grad_rows, down_pair, preferred_element_type=wide)
-    inner_low = gelu_pull(act_grad)[0].astype(low)
-    back_part = jnp.einsum("nf,df->nd", inner_low, up_pair, preferred_element_type=wide).astype(
-        low
-    )
-    back_parts = class_scatter(back_part.reshape(chips, local_len, width), 5)
-    hidden_grad = mixed_grad + jnp.sum(back_parts.astype(wide), axis=0)
-    pre_grad, gain1_grad, shift1_grad = norm1_pull(hidden_grad)
-    up_part = jnp.einsum(
-        "nd,nkf->kdf",
-        hidden_rows,
-        inner_low.reshape(-1, 2, hidden_here),
-        preferred_element_type=wide,
-    ).astype(low)
-    up_part = up_part.reshape(2, batches, width // batches, hidden_here)
-    upb_part = jnp.sum(inner_low.astype(wide), axis=0).reshape(2, 1, 1, hidden_here)
-    upb_part = jnp.broadcast_to(upb_part, (2, batches, 8, hidden_here))
-    down_part = jnp.einsum(
-        "nkf,nge->kgfe",
-        act_low.reshape(-1, 2, hidden_here),
-        grad_rows.reshape(-1, batches, width // batches),
-        preferred_element_type=wide,
-    ).astype(low)
-    attn_all, up_parts, upb_parts = spread_grads(pre_grad.astype(low), up_part, upb_part, 6)
-    attn_all = attn_all.reshape(full_len, width)
-    mix_rows = lax.dynamic_slice_in_dim(m_mix, first_col, pair, axis=0)
-    context_grad = jnp.einsum(
-        "ne,de->nd", attn_all, mix_rows, preferred_element_type=wide
-    ).astype(low)
-    dcat, rel_grad, col_sums = attend_back(first, q, k, v, qrev, krev, probs, context_grad)
-    in_part = jnp.einsum("ne,de->nd", dcat, w_cat, preferred_element_type=wide).astype(low)
-    in_part = in_part.reshape(chips, 2, local_len, width)
-    dw_part = jnp.einsum("nd,ne->de", x_all, dcat, preferred_element_type=wide)
-    dw_rel = jnp.einsum("bd,be->de", table, rel_grad, preferred_element_type=wide)
-    dw_part = dw_part + jnp.pad(dw_rel, ((0, 0), (0, pair)))
-    dw_part = dw_part.astype(low).reshape(batches, width // batches, 3 * pair)
-    tab_part = jnp.einsum(
-        "be,gde->gbd",
-        rel_grad,
-        w_cat[:, : 2 * pair].reshape(batches, width // batches, 2 * pair),
-        preferred_element_type=wide,
-    ).astype(low)
-    mix_part = jnp.einsum(
-        "nk,nge->gke",
-        ctx,
-        attn_all.reshape(full_len, batches, width // batches),
-        preferred_element_type=wide,
-    ).astype(low)
-    bias_rows = lax.dynamic_update_slice(
-        jnp.zeros((3, width), wide), col_sums.reshape(3, pair), (jnp.int32(0), first_col)
-    )
-    vec_part = jnp.concatenate(
-        [
-            bias_rows,
-            jnp.sum(pre_grad, axis=0)[None],
-            gain1_grad[None],
-            gain2_grad[None],
-            shift1_grad[None],
-            shift2_grad[None],
-            jnp.sum(mixed_grad, axis=0)[None],
-        ],
-        axis=0,
-    )
-    vec_part = jnp.pad(
-        vec_part.reshape(9, tokens, lanes).transpose(1, 0, 2), ((0, 0), (0, 7), (0, BLOCK - lanes))
-    )
-    ins, vec_parts, dws, tabs, mixs = reduce_grads(in_part, vec_part, dw_part, tab_part, mix_part, 7)
-    input_grad = pre_grad + jnp.sum(ins.astype(wide), axis=0)
-    dw_sum = jnp.sum(dws.astype(wide), axis=0).astype(low)
-    tab_sum = jnp.sum(tabs.astype(wide), axis=0).astype(low)
-    mix_sum = jnp.sum(mixs.astype(wide), axis=0).astype(low)
-    vec_sum = jnp.sum(vec_parts, axis=0)
-    dw_got, tab_got, mix_other, vec_got, downs = settle_grads(
-        dw_sum.reshape(2, shard_rows, 3 * pair),
-        tab_sum.reshape(tokens, table_rows, shard_cols),
-        mix_sum,
-        vec_sum,
-        down_part,
-        8,
-    )
-    dw_got = dw_got.astype(wide).reshape(2, shard_rows, 3, pair)
-    dw_all = jnp.pad(dw_got[0], ((0, 0), (0, 0), (0, DH))) + jnp.pad(
-        dw_got[1], ((0, 0), (0, 0), (DH, 0))
-    )
-    table_grad = jnp.sum(tab_got.astype(wide), axis=0)
-    mix_own, mix_other = mix_sum.astype(wide), mix_other.astype(wide)
-    lower = jnp.where(at.core == 0, mix_own, mix_other)
-    upper = jnp.where(at.core == 0, mix_other, mix_own)
-    mix_grad = jnp.pad(lower, ((0, DH), (0, 0))) + jnp.pad(upper, ((DH, 0), (0, 0)))
-    mix_grad = lax.dynamic_slice_in_dim(mix_grad, at.core * shard_rows, shard_rows, axis=0)
-    small = jnp.sum(vec_got, axis=0)[:, :lanes]
+    pack = jnp.pad(pack, ((0, 16 - pack.shape[0]), (0, 0)))
+    xs, qkvs, mts, vecs, up2, down2 = gather_inputs(
+        x, w_query, w_key, w_value, w_mix, rel_table, pack, w_up, w_down
+    )
+    q, k, v, qrev, krev, probs, ctx, w_cat, m_mix, table = attend(xs, qkvs, mts, vecs)
+    output, pre_grad, sums, attn_all, ups, downs, upbs = feed_forward(
+        ctx, x, m_mix, vecs, w_up, w_down, up2, down2, out_grad[0], 1
+    )
+    in_part, dw_part, tab_part, mix_part, cols = attend_back(
+        q, k, v, qrev, krev, probs, ctx, w_cat, m_mix, table, xs, attn_all
+    )
+    ins, vec_all, cols_all, dw_all, tab_all, mix_all = settle_grads(
+        in_part, sums, cols, dw_part, tab_part, mix_part, 2
+    )
+    shard = (shard_rows, shard_cols)
+    shapes = (
+        x.shape, shard, shard, shard, shard, rel_table.shape, (4, lanes), (2, lanes), (2, lanes),
+        (width // lax.axis_size("batch"), hidden_here), (1, hidden_here),
+        (hidden_here, width // lax.axis_size("batch")), (1, lanes),
+    )
+    grads = finish(
+        pre_grad,
+        (ins, vec_all, cols_all, dw_all, tab_all, mix_all, ups, downs, upbs),
+        shapes,
+    )
+    input_grad, dq, dk, dv, dmix, dtable, dbias, dgain, dshift, dup, dupb, ddown, ddownb = grads
     return (
-        output.astype(low)[None],
-        input_grad[None],
-        dw_all[:, 0],
-        dw_all[:, 1],
-        dw_all[:, 2],
-        mix_grad,
-        table_grad,
-        small[0:4],
-        small[4:6],
-        small[6:8],
-        jnp.sum(up_parts.astype(wide), axis=0),
-        jnp.sum(upb_parts[:, 0], axis=0),
-        jnp.sum(downs.astype(wide), axis=0),
-        small[8],
+        output[None], input_grad[None], dq, dk, dv, dmix, dtable, dbias, dgain, dshift,
+        dup, dupb[0], ddown, ddownb[0],
     )
 
 
@@ -1204,7 +1389,7 @@
     down_bias,
     out_grad,
 ):
-    if fits_fast(layer_input, rel_table, w_query):
+    if fits_fast(layer_input, rel_table, w_up.shape[1]):
         return fast_body(
             layer_input, segment_ids, w_query, w_key, w_value, w_mix, rel_table, attn_biases,
             norm_gains, norm_shifts, w_up, up_bias, w_down, down_bias, out_grad,

time: 377 us -> 291 us (0.77)
  local copies, waits for them, and re-layouts: 58.8 us -> 19.9 us
  matrix products: 31.5 us -> 0 us
  other arithmetic: 18.3 us -> 2.69 us
    pallas_call x9 -> x2, Pallas kernels: 210 us -> 94.3 us  [comm_call(): pl.pallas_call(kernel, out_shape=tuple(out_shapes), in_specs=[VMEM_SPEC]...]
    pallas_call x1 -> x3, Pallas kernels: 28.6 us -> 144 us  [the longest x1 109 us: feed_forward(): pl.pallas_call(feed_kernel, out_shape=outs, in_specs=[VMEM_SPEC] * len(in...]
    dot_general x13 -> x0, matrix products: 31.5 us -> none  [the longest x1 5.7 us: fast_body(): inner = jnp.dot(hidden_rows, up_pair, preferred_element_type=wide) + bias_up]
    reshape x5 -> x0, local copies, waits for them, and re-layouts: 11.5 us -> none  [the longest x1 3.01 us: fast_body(): mt_all[..., shard_rows:, :].transpose(2, 0, 3, 1, 4)]
    reduce_sum x22 -> x0, other arithmetic: 10.2 us -> none  [the longest x1 1.49 us: fast_body(): jnp.sum(upb_parts[:, 0], axis=0)]
    convert_element_type x7 -> x0, local copies, waits for them, and re-layouts: 6.77 us -> none  [the longest x1 1.77 us: fast_body(): mix_part = jnp.einsum('nk,nge->gke', ctx, attn_all.reshape(full_len, batc...]
    transpose x6 -> x0, local copies, waits for them, and re-layouts: 5.78 us -> none  [the longest x1 2.56 us: fast_body(): wcols = qkv_all.transpose(0, 2, 1, 3).reshape(width, 3, shard_cols)]
    another operation x2 -> x0, local copies, waits for them, and re-layouts: 4 us -> none  [the longest x1 3.7 us: fast_body(): attn_all.reshape(full_len, batches, width // batches)]
where the time goes in v2:
time: 291 us; the launch traced here: 290 us
  Pallas kernels  267 us (92%)
  local copies, waits for them, and re-layouts  19.9 us (7%)
    pallas_call x1, Pallas kernels, feed_forward(): pl.pallas_call(feed_kernel, out_shape=outs, in_specs=[VMEM_SPEC] * len(in...  109 us
    pallas_call x2, Pallas kernels, comm_call(): pl.pallas_call(kernel, out_shape=tuple(out_shapes), in_specs=[VMEM_SPEC]...  94.3 us
    pallas_call x1, Pallas kernels, attend_back(): pl.pallas_call(attend_back_kernel, out_shape=(jax.ShapeDtypeStruct((token...  33.8 us
    pallas_call x1, Pallas kernels, attend(): pl.pallas_call(attend_kernel, out_shape=(jax.ShapeDtypeStruct((2, full_le...  28.8 us
    unnamed x52, local copies, waits for them, and re-layouts  19.9 us

profile of v2, /device:TPU:0, one launch (start us, length us, event | category | flops | bytes accessed | tf_op | source)
XLA Modules:
  0.0 290.3 jit_solution(16672458407548927867)
XLA Ops:
  0.6 0.7 convert_element_type.7
  1.3 0.7 fusion.9
  2.0 0.7 fusion.11.vec_ref
  2.7 1.1 copy-done.2
  3.8 1.1 copy-done.3
  4.9 0.9 copy-done.9
  5.8 0.8 copy-done.17
  6.6 0.8 copy-done.18
  7.4 0.8 copy-done.19
  8.2 0.8 copy-done.20
  9.0 0.8 copy-done.22
  9.7 48.9 %gather_inputs.1 = (bf16[8,128,768]{2,1,0:T(8,128)(2,1)S(1)}, bf16[8,3,96,192]{3,2,1,0:T(8,128)(2,1)S(1)}, bf16[2,4,4,160,192]{4,3,2,1,0:T(8,128)(2,1)S(1)}, bf1...) custom-call(bf16[128,768]{1,0:T(8,128)(2,1)S(1)} %bitcast.8, ...), custom_call_target="tpu_custom_call" | custom-call | tf_op jit(solution)/shard_map/gather_inputs/pallas_call | solution.py:691
  58.7 1.1 copy-done
  59.8 1.5 copy-done.1
  61.3 1.1 copy-done.7
  62.4 0.8 copy-done.10
  63.3 0.8 copy-done.11
  64.1 0.6 copy-done.15
  64.7 28.8 %attend.1 = (bf16[2,1024,64]{2,1,0:T(8,128)(2,1)}, bf16[2,1024,64]{2,1,0:T(8,128)(2,1)}, bf16[2,1024,64]{2,1,0:T(8,128)(2,1)}, bf16[2,512,64]{2,1,0:T(8,128)(2,1...) custom-call(bf16[8,128,768]{2,1,0:T(8,128)(2,1)} %copy-done, ...), custom_call_target="tpu_custom_call" | custom-call | tf_op jit(solution)/shard_map/attend/pallas_call | solution.py:350
  93.5 108.5 %feed_forward.1 = (bf16[128,768]{1,0:T(8,128)(2,1)}, f32[128,768]{1,0:T(8,128)}, f32[8,8,128]{2,1,0:T(8,128)}, bf16[8,128,768]{2,1,0:T(8,128)(2,1)}, bf16[8,192,...) custom-call(bf16[8,128,128]{2,1,0:T(8,128)(2,1)} %get-tuple-element.65.ctx_ref, ...), custom_call_target="tpu_custom_call" | custom-call | tf_op jit(solution)/shard_map/feed_forward/pallas_call | solution.py:1070
  202.0 0.0 copy-start.21
  202.0 33.8 %attend_back.1 = (bf16[4,2,128,768]{3,2,1,0:T(8,128)(2,1)}, bf16[4,192,384]{2,1,0:T(8,128)(2,1)}, bf16[4,512,192]{2,1,0:T(8,128)(2,1)}, bf16[4,128,192]{2,1,0:T(8,128)(2,1)}, f32[8,384]{1,0:T(8,128)}) custom-call(bf16[2,1024,64]{2,1,0:T(8,128)(2,1)} %get-tuple-element.71.q_ref, bf16[2,1024,64]{2,1,0:T(8,128)(2,1)} %get-tuple-element.72.k_ref, ...), custom_call_target="tpu_custom_call" | custom-call | tf_op jit(solution)/shard_map/attend_back/pallas_call | solution.py:552
  235.8 1.4 copy-done.4
  237.2 1.2 copy-done.8
  238.4 1.1 copy-done.12
  239.5 0.9 copy-done.14
  240.5 0.7 copy-done.23
  241.2 45.4 %settle_grads.1 = (bf16[4,128,768]{2,1,0:T(8,128)(2,1)S(1)}, f32[4,8,128]{2,1,0:T(8,128)S(1)}, f32[8,8,384]{2,1,0:T(8,128)S(1)}, bf16[2,96,384]{2,1,0:T(8,128)(2...) custom-call(bf16[4,2,128,768]{3,2,1,0:T(8,128)(2,1)S(1)} %copy-done.4, ...), custom_call_target="tpu_custom_call" | custom-call | tf_op jit(solution)/shard_map/settle_grads/pallas_call | solution.py:691
  286.7 1.6 finish.1
  288.2 0.6 reduce
  288.8 0.9 copy.29
  289.7 0.7 copy.31
  (30 shorter events, 0.1 us)
Async XLA Ops:
  2.7 1.1 copy-start.2
  3.8 1.1 copy-start.3
  4.9 0.9 copy-start.9
  5.8 0.8 copy-start.17
  6.6 0.8 copy-start.18
  7.4 0.8 copy-start.19
  8.2 0.8 copy-start.20
  9.0 0.8 copy-start.22
  58.7 1.1 copy-start
  59.8 1.5 copy-start.1
  61.3 1.1 copy-start.7
  62.4 0.8 copy-start.10
  63.3 0.8 copy-start.11
  64.1 0.6 copy-start.15
  202.0 33.8 %copy-start.21 = (f32[8,8,128]{2,1,0:T(8,128)S(1)}, f32[8,8,128]{2,1,0:T(8,128)}, u32[]{:S(2)}) copy-start(f32[8,8,128]{2,1,0:T(8,128)} %get-tuple-element.81.vec_ref) | copy-start | bytes 98308
  235.8 1.4 copy-start.4
  237.2 1.2 copy-start.8
  238.4 1.1 copy-start.12
  239.5 0.9 copy-start.14
  240.5 0.7 copy-start.23
  241.2 45.4 %copy-start.5 = (bf16[8,384,192]{2,1,0:T(8,128)(2,1)S(1)}, bf16[8,384,192]{2,1,0:T(8,128)(2,1)}, u32[]{:S(2)}) copy-start(bf16[8,384,192]{2,1,0:T(8,128)(2,1)} %get-tuple-element.93.downs_ref) | copy-start | bytes 3538948
  241.2 45.5 %copy-start.6 = (bf16[8,192,384]{2,1,0:T(8,128)(2,1)S(1)}, bf16[8,192,384]{2,1,0:T(8,128)(2,1)}, u32[]{:S(2)}) copy-start(bf16[8,192,384]{2,1,0:T(8,128)(2,1)} %get-tuple-element.92.ups_ref) | copy-start | bytes 3538948
  241.2 45.5 %copy-start.13 = (f32[128,768]{1,0:T(8,128)S(1)}, f32[128,768]{1,0:T(8,128)}, u32[]{:S(2)}) copy-start(f32[128,768]{1,0:T(8,128)} %get-tuple-element.70.pre_ref) | copy-start | bytes 1179652
  241.2 45.5 %copy-start.16 = (f32[8,8,384]{2,1,0:T(8,128)S(1)}, f32[8,8,384]{2,1,0:T(8,128)}, u32[]{:S(2)}) copy-start(f32[8,8,384]{2,1,0:T(8,128)} %get-tuple-element.94.upbs_ref) | copy-start | bytes 294916
  286.6 3.0 %copy-start.24 = (bf16[128,768]{1,0:T(8,128)(2,1)S(1)}, bf16[128,768]{1,0:T(8,128)(2,1)}, u32[]{:S(2)}) copy-start(bf16[128,768]{1,0:T(8,128)(2,1)} %get-tuple-element.69) | copy-start | bytes 589828

commit v3 on v2

--- a/solution.py
+++ b/solution.py
@@ -164,6 +164,11 @@
 
 
 BLOCK = 128
+MIB = 1024 * 1024
+ATTEND_VMEM = 26 * MIB
+BACK_VMEM = 26 * MIB
+FEED_VMEM = 26 * MIB
+COMM_VMEM = 16 * MIB
 
 
 def dot_nn(a, b):
@@ -224,7 +229,6 @@
     w_ref,
     mix_ref,
     table_ref,
-    x_ref,
     segc_ref,
     place_ref,
     wide_ref,
@@ -232,7 +236,7 @@
     held_ref,
 ):
     at = Place()
-    full_len = x_ref.shape[0]
+    full_len = xs_ref.shape[0] * xs_ref.shape[1]
     buckets = table_ref.shape[0]
     blocks = full_len // BLOCK
     span = buckets // 2
@@ -259,7 +263,6 @@
         table_ref[part * table_rows : (part + 1) * table_rows] = jnp.concatenate(
             [piece[shard_rows:] for piece in whole], axis=1
         )
-        x_ref[part * BLOCK : (part + 1) * BLOCK] = xs_ref[part]
         own_seg = vecs_ref[part, 9:10].astype(jnp.float32)
         segc_ref[part * BLOCK : (part + 1) * BLOCK] = jnp.broadcast_to(own_seg, (BLOCK, BLOCK)).T
     seg_row = jnp.concatenate(
@@ -268,7 +271,8 @@
     bias = jnp.concatenate(
         [chip_columns(vecs_ref, at.chip, i, at.core) for i in range(3)], axis=1
     )
-    proj = (dot_nn(x_ref[...], w_ref[...]) + bias).astype(jnp.bfloat16)
+    tokens_all = xs_ref[...].reshape(full_len, xs_ref.shape[2])
+    proj = (dot_nn(tokens_all, w_ref[...]) + bias).astype(jnp.bfloat16)
     rel = (dot_nn(table_ref[...], w_ref[:, : 2 * group]) + bias[:, : 2 * group]).astype(
         jnp.bfloat16
     )
@@ -364,14 +368,13 @@
         in_specs=[pl.BlockSpec(memory_space=pltpu.VMEM)] * 4,
         out_specs=[pl.BlockSpec(memory_space=pltpu.VMEM)] * 10,
         scratch_shapes=[
-            pltpu.VMEM((full_len, width), low),
             pltpu.VMEM((full_len, BLOCK), wide),
             pltpu.VMEM((2, pad_blocks, BLOCK, band_width), wide),
             pltpu.VMEM((BLOCK, full_len + buckets), wide),
             pltpu.VMEM((2, 2, 16, full_len), wide),
             pltpu.VMEM((2, full_len, DH), low),
         ],
-        compiler_params=pltpu.CompilerParams(vmem_limit_bytes=60 * 1024 * 1024),
+        compiler_params=pltpu.CompilerParams(vmem_limit_bytes=ATTEND_VMEM),
         name="attend",
     )(xs, qkvs, mts, vecs)
 
@@ -383,18 +386,11 @@
     qrev_ref,
     krev_ref,
     p_ref,
-    ctx_ref,
-    w_ref,
     mix_ref,
-    table_ref,
-    xs_ref,
     attn_ref,
-    in_ref,
-    dw_ref,
-    tab_ref,
-    mixpart_ref,
+    dcat_ref,
+    rel_ref,
     sum_ref,
-    x_ref,
     heads_ref,
     wide_ref,
     low_ref,
@@ -419,22 +415,11 @@
         ref[...] = jnp.zeros_like(ref)
     at = Place()
     group = 2 * DH
-    width = x_ref.shape[1]
     first_row = pl.multiple_of((3 * at.chip + at.core) * DH, DH)
     mix_rows = mix_ref[pl.ds(first_row, group)]
-    mix_part = jnp.zeros((group, width), jnp.float32)
-    for part in range(at.tokens):
-        x_ref[part * BLOCK : (part + 1) * BLOCK] = xs_ref[part]
-        low_part = attn_ref[part]
-        mix_part = mix_part + dot_tn(ctx_ref[part], low_part)
-        dctx = dot_nt(low_part, mix_rows).astype(jnp.bfloat16)
-        for slot in range(2):
-            heads_ref[slot, part * BLOCK : (part + 1) * BLOCK] = dctx[
-                :, slot * DH : (slot + 1) * DH
-            ]
-    columns = width // at.batches
-    for row in range(at.batches):
-        mixpart_ref[row] = mix_part[:, row * columns : (row + 1) * columns].astype(jnp.bfloat16)
+    dctx = dot_nt(attn_ref[...].reshape(full_len, attn_ref.shape[2]), mix_rows)
+    for slot in range(2):
+        heads_ref[slot] = dctx[:, slot * DH : (slot + 1) * DH].astype(jnp.bfloat16)
     first = at.core * (blocks // 2)
     turn = turn_matrix(BLOCK)
     place8 = lax.broadcasted_iota(jnp.int32, (8, full_len), 0)
@@ -521,47 +506,32 @@
         parts_r[slot] = dqr_out
         parts_r[2 + slot] = dkr_out
     dcat = jnp.concatenate(parts_q + parts_k + parts_v, axis=1)
-    in_part = dot_nt(dcat, w_ref[...]).astype(jnp.bfloat16)
-    for part in range(at.tokens):
-        in_ref[part // 2, part % 2] = in_part[part * BLOCK : (part + 1) * BLOCK]
+    dcat_ref[...] = dcat
     rel = jnp.concatenate(parts_r, axis=1)
-    rel_low = dot_nn(turn_matrix(buckets), rel.astype(jnp.bfloat16)).astype(jnp.bfloat16)
-    dw = dot_tn(x_ref[...], dcat)
-    dw_rel = dot_tn(table_ref[...], rel_low)
-    dw = jnp.concatenate([dw[:, : 2 * group] + dw_rel, dw[:, 2 * group :]], axis=1)
-    dw_low = dw.astype(jnp.bfloat16)
-    for row in range(at.batches):
-        rows = slice(row * columns, (row + 1) * columns)
-        dw_ref[row] = dw_low[rows]
-        tab_ref[row] = dot_nt(rel_low, w_ref[rows, : 2 * group]).astype(jnp.bfloat16)
+    rel_ref[...] = dot_nn(turn_matrix(buckets), rel.astype(jnp.bfloat16)).astype(jnp.bfloat16)
     rel_sum = jnp.sum(rel, axis=0, keepdims=True)
     rel_sum = jnp.concatenate([rel_sum, jnp.zeros((1, 2 * DH), jnp.float32)], axis=1)
     sums = jnp.sum(dcat.astype(jnp.float32), axis=0, keepdims=True) + rel_sum
     sum_ref[...] = jnp.broadcast_to(sums, sum_ref.shape)
 
 
-def attend_back(q, k, v, qrev, krev, probs, ctx, w_cat, m_mix, table, xs, attn_all):
+def attend_back(q, k, v, qrev, krev, probs, m_mix, attn_all):
     full_len = q.shape[1]
-    buckets, width = table.shape
+    buckets = qrev.shape[1]
     blocks = full_len // BLOCK
-    tokens, batches = lax.axis_size("seq"), lax.axis_size("batch")
-    columns = width // batches
     band_width = buckets + BLOCK
     low, wide = jnp.bfloat16, jnp.float32
     pad_blocks = blocks + band_width // BLOCK - 1
     return pl.pallas_call(
         attend_back_kernel,
         out_shape=(
-            jax.ShapeDtypeStruct((tokens // 2, 2, BLOCK, width), low),
-            jax.ShapeDtypeStruct((batches, columns, 6 * DH), low),
-            jax.ShapeDtypeStruct((batches, buckets, columns), low),
-            jax.ShapeDtypeStruct((batches, 2 * DH, columns), low),
+            jax.ShapeDtypeStruct((full_len, 6 * DH), low),
+            jax.ShapeDtypeStruct((buckets, 4 * DH), low),
             jax.ShapeDtypeStruct((8, 6 * DH), wide),
         ),
-        in_specs=[pl.BlockSpec(memory_space=pltpu.VMEM)] * 12,
-        out_specs=[pl.BlockSpec(memory_space=pltpu.VMEM)] * 5,
+        in_specs=[pl.BlockSpec(memory_space=pltpu.VMEM)] * 8,
+        out_specs=[pl.BlockSpec(memory_space=pltpu.VMEM)] * 3,
         scratch_shapes=[
-            pltpu.VMEM((full_len, width), low),
             pltpu.VMEM((2, full_len, DH), low),
             pltpu.VMEM((BLOCK, full_len + buckets), wide),
             pltpu.VMEM((BLOCK, full_len + buckets), low),
@@ -573,9 +543,9 @@
             pltpu.VMEM((2, DH, buckets), wide),
             pltpu.VMEM((2, DH, buckets), wide),
         ],
-        compiler_params=pltpu.CompilerParams(vmem_limit_bytes=60 * 1024 * 1024),
+        compiler_params=pltpu.CompilerParams(vmem_limit_bytes=BACK_VMEM),
         name="attend_back",
-    )(q, k, v, qrev, krev, probs, ctx, w_cat, m_mix, table, xs, attn_all)
+    )(q, k, v, qrev, krev, probs, m_mix, attn_all)
 
 
 MESH = pl.DeviceIdType.MESH
@@ -687,15 +657,15 @@
     ]
 
 
-def comm_call(kernel, name, ident, out_shapes, inputs, sends, locals_count, scratch=()):
+def comm_call(kernel, name, ident, out_shapes, inputs, sends, locals_count, scratch=(), spec=VMEM_SPEC):
     return pl.pallas_call(
         kernel,
         out_shape=tuple(out_shapes),
-        in_specs=[VMEM_SPEC] * len(inputs),
-        out_specs=tuple([ANY_SPEC] * len(out_shapes)),
+        in_specs=[spec] * len(inputs),
+        out_specs=tuple([VMEM_SPEC] * len(out_shapes)),
         scratch_shapes=list(scratch) + wire_scratch(sends, locals_count),
         compiler_params=pltpu.CompilerParams(
-            collective_id=ident, has_side_effects=True, vmem_limit_bytes=40 * 1024 * 1024
+            collective_id=ident, has_side_effects=True, vmem_limit_bytes=COMM_VMEM
         ),
         name=name,
     )(*inputs)
@@ -837,7 +807,7 @@
     )
     sends = 3 + 4 * (chips - 1) + 4 + 2 * batches - 1 + 2 * (batches - 1) + 1 + 2 * (chips - 1)
     inputs = (x, w_query, w_key, w_value, w_mix, rel_table, vec, up, down)
-    return comm_call(gather_kernel, "gather_inputs", 0, outs, inputs, sends, 7)
+    return comm_call(gather_kernel, "gather_inputs", 0, outs, inputs, sends, 7, spec=ANY_SPEC)
 
 
 def norm_parts(values):
@@ -1071,19 +1041,19 @@
         feed_kernel,
         out_shape=outs,
         in_specs=[VMEM_SPEC] * len(inputs),
-        out_specs=(VMEM_SPEC,) * 3 + (ANY_SPEC,) * 4,
+        out_specs=(VMEM_SPEC,) * len(outs),
         scratch_shapes=list(scratch) + wire_scratch(sends, 5),
         compiler_params=pltpu.CompilerParams(
-            collective_id=ident, has_side_effects=True, vmem_limit_bytes=60 * 1024 * 1024
+            collective_id=ident, has_side_effects=True, vmem_limit_bytes=FEED_VMEM
         ),
         name="feed_forward",
     )(*inputs)
 
 
 def settle_kernel(
-    in_ref, vec_ref, col_ref, dw_ref, tab_ref, mix_ref,
+    vec_ref, col_ref, dcat_ref, rel_ref, w_ref, xs_ref, table_ref, ctx_ref, attn_ref,
     ins_ref, vec_all_ref, cols_ref, dw_all_ref, tab_all_ref, mix_all_ref,
-    half_ref, sum_ref, vecs_ref, vec_low_ref, dws_ref, dw_low_ref, tabs_ref, tab_low_ref,
+    in_ref, dw_ref, tab_ref, mix_ref, half_ref, sum_ref, vecs_ref, vec_low_ref, dws_ref, dw_low_ref, tabs_ref, tab_low_ref,
     mixs_ref, mix_low_ref, *sems,
 ):
     at = Place()
@@ -1105,19 +1075,19 @@
     pl.semaphore_wait(barrier, len(peers) + 2 * off_diagonal.astype(jnp.int32))
 
     dw_sends, tab_sends, mix_sends, vec_sends, last, own = [], [], [], [], [], []
-    for k in range(1, at.batches):
-        row, peer = at.along_rows(k)
-        dw_sends.append(wires.send(dw_ref.at[row], dws_ref.at[k - 1], peer))
-    halves = [
-        wires.send(in_ref.at[chip, 1 - c], half_ref.at[chip], at.partner())
-        for chip in range(at.chips)
-    ]
-    for k in range(1, at.batches):
-        row, peer = at.along_rows(k)
-        tab_sends.append(wires.send(tab_ref.at[row], tabs_ref.at[k - 1], peer))
-    for k in range(1, at.batches):
-        row, peer = at.along_rows(k)
-        mix_sends.append(wires.send(mix_ref.at[row], mixs_ref.at[k - 1], peer))
+    width = w_ref.shape[0]
+    columns = width // at.batches
+    full_len = dcat_ref.shape[0]
+    group = 2 * DH
+
+    def input_part(chip, core):
+        start = pl.multiple_of((2 * chip + core) * BLOCK, BLOCK)
+        in_ref[chip, core] = dot_nt(dcat_ref[pl.ds(start, BLOCK)], w_ref[...]).astype(low)
+
+    halves = []
+    for chip in range(at.chips):
+        input_part(chip, 1 - c)
+        halves.append(wires.send(in_ref.at[chip, 1 - c], half_ref.at[chip], at.partner()))
     for k in range(1, at.tokens):
         part, peer = at.along_seq(k)
         vec_sends.append(wires.send(vec_ref.at[part], vecs_ref.at[k - 1], peer))
@@ -1125,6 +1095,39 @@
     for k in range(1, 2 * at.batches):
         last.append(wires.send(col_ref, cols_ref.at[mine], at.along_plane(k)[2]))
     own.append(wires.local(col_ref, cols_ref.at[mine]))
+
+    for chip in range(at.chips):
+        input_part(chip, c)
+        halves[chip].wait_recv()
+        sum_ref[chip] = (in_ref[chip, c].astype(wide) + half_ref[chip].astype(wide)).astype(low)
+    for k in range(1, at.chips):
+        chip, peer = at.along_chips(k)
+        last.append(wires.send(sum_ref.at[chip], ins_ref.at[z], peer))
+    own.append(wires.local(sum_ref.at[z], ins_ref.at[z]))
+
+    whole = xs_ref[...].reshape(full_len, width)
+    dw = dot_tn(whole, dcat_ref[...])
+    dw_rel = dot_tn(table_ref[...], rel_ref[...])
+    dw = jnp.concatenate([dw[:, : 2 * group] + dw_rel, dw[:, 2 * group :]], axis=1)
+    for row in range(at.batches):
+        dw_ref[row] = dw[row * columns : (row + 1) * columns].astype(low)
+    for k in range(1, at.batches):
+        row, peer = at.along_rows(k)
+        dw_sends.append(wires.send(dw_ref.at[row], dws_ref.at[k - 1], peer))
+    for row in range(at.batches):
+        rows = slice(row * columns, (row + 1) * columns)
+        tab_ref[row] = dot_nt(rel_ref[...], w_ref[rows, : 2 * group]).astype(low)
+    for k in range(1, at.batches):
+        row, peer = at.along_rows(k)
+        tab_sends.append(wires.send(tab_ref.at[row], tabs_ref.at[k - 1], peer))
+    mix = dot_tn(
+        ctx_ref[...].reshape(full_len, group), attn_ref[...].reshape(full_len, width)
+    )
+    for row in range(at.batches):
+        mix_ref[row] = mix[:, row * columns : (row + 1) * columns].astype(low)
+    for k in range(1, at.batches):
+        row, peer = at.along_rows(k)
+        mix_sends.append(wires.send(mix_ref.at[row], mixs_ref.at[k - 1], peer))
 
     total = dw_ref[b].astype(wide)
     for k in range(1, at.batches):
@@ -1158,14 +1161,6 @@
 
     last.append(wires.send(dw_low_ref.at[1 - c], dw_all_ref.at[c], cross))
 
-    for chip in range(at.chips):
-        halves[chip].wait_recv()
-        sum_ref[chip] = (in_ref[chip, c].astype(wide) + half_ref[chip].astype(wide)).astype(low)
-    for k in range(1, at.chips):
-        chip, peer = at.along_chips(k)
-        last.append(wires.send(sum_ref.at[chip], ins_ref.at[z], peer))
-    own.append(wires.local(sum_ref.at[z], ins_ref.at[z]))
-
     total = tab_ref[b].astype(wide)
     for k in range(1, at.batches):
         tab_sends[k - 1].wait_recv()
@@ -1210,16 +1205,18 @@
         stay.wait()
 
 
-def settle_grads(in_part, vec, cols, dw, tab, mix, ident):
+def settle_grads(vec, cols, dcat, rel, w_cat, xs, table, ctx, attn_all, ident):
     tokens, batches = lax.axis_size("seq"), lax.axis_size("batch")
     chips = tokens // 2
     low, wide = jnp.bfloat16, jnp.float32
-    half = (chips,) + in_part.shape[2:]
-    columns, group = dw.shape[1:]
-    buckets, table_cols = tab.shape[1:]
+    local_len, width = xs.shape[1:]
+    columns, group = width // batches, dcat.shape[1]
+    buckets = table.shape[0]
+    half = (chips, local_len, width)
     dw_pieces = (2, columns // 2, group)
-    tab_pieces = (tokens, buckets // tokens, table_cols)
-    mix_piece = mix.shape[1:]
+    tab_pieces = (tokens, buckets // tokens, columns)
+    mix_piece = (2 * DH, columns)
+    dw_piece, tab_piece = (columns, group), (buckets, columns)
     outs = (
         jax.ShapeDtypeStruct(half, low),
         jax.ShapeDtypeStruct((batches,) + vec.shape[1:], wide),
@@ -1229,13 +1226,17 @@
         jax.ShapeDtypeStruct((2,) + mix_piece, low),
     )
     scratch = (
+        pltpu.VMEM((chips, 2, local_len, width), low),
+        pltpu.VMEM((batches,) + dw_piece, low),
+        pltpu.VMEM((batches,) + tab_piece, low),
+        pltpu.VMEM((batches,) + mix_piece, low),
         pltpu.VMEM(half, low),
         pltpu.VMEM(half, low),
         pltpu.VMEM((tokens - 1,) + vec.shape[1:], wide),
         pltpu.VMEM(vec.shape[1:], wide),
-        pltpu.VMEM((batches - 1,) + dw.shape[1:], low),
+        pltpu.VMEM((batches - 1,) + dw_piece, low),
         pltpu.VMEM(dw_pieces, low),
-        pltpu.VMEM((batches - 1,) + tab.shape[1:], low),
+        pltpu.VMEM((batches - 1,) + tab_piece, low),
         pltpu.VMEM(tab_pieces, low),
         pltpu.VMEM((batches - 1,) + mix_piece, low),
         pltpu.VMEM(mix_piece, low),
@@ -1244,7 +1245,7 @@
         3 * (batches - 1) + chips + tokens - 1 + 2 * batches - 1
         + 2 + chips - 1 + tokens - 1 + 1 + batches - 1
     )
-    inputs = (in_part, vec, cols, dw, tab, mix)
+    inputs = (vec, cols, dcat, rel, w_cat, xs, table, ctx, attn_all)
     return comm_call(settle_kernel, "settle_grads", ident, outs, inputs, sends, 6, scratch=scratch)
 
 
@@ -1305,7 +1306,7 @@
         out_shape=tuple(jax.ShapeDtypeStruct(shape, jnp.float32) for shape in shapes),
         in_specs=[VMEM_SPEC] * len(inputs),
         out_specs=(VMEM_SPEC,) * len(shapes),
-        compiler_params=pltpu.CompilerParams(vmem_limit_bytes=40 * 1024 * 1024),
+        compiler_params=pltpu.CompilerParams(vmem_limit_bytes=COMM_VMEM),
         name="finish",
     )(*inputs)
 
@@ -1348,11 +1349,9 @@
     output, pre_grad, sums, attn_all, ups, downs, upbs = feed_forward(
         ctx, x, m_mix, vecs, w_up, w_down, up2, down2, out_grad[0], 1
     )
-    in_part, dw_part, tab_part, mix_part, cols = attend_back(
-        q, k, v, qrev, krev, probs, ctx, w_cat, m_mix, table, xs, attn_all
-    )
+    dcat, rel_grad, cols = attend_back(q, k, v, qrev, krev, probs, m_mix, attn_all)
     ins, vec_all, cols_all, dw_all, tab_all, mix_all = settle_grads(
-        in_part, sums, cols, dw_part, tab_part, mix_part, 2
+        sums, cols, dcat, rel_grad, w_cat, xs, table, ctx, attn_all, 2
     )
     shard = (shard_rows, shard_cols)
     shapes = (

time: 291 us -> 261 us (0.90)
  Pallas kernels: 267 us -> 248 us
  local copies, waits for them, and re-layouts: 19.9 us -> 8.57 us
    unnamed x52 -> x26, local copies, waits for them, and re-layouts: 19.9 us -> 8.57 us
    pallas_call x3, Pallas kernels: 128 us -> 118 us  [the longest x2 92.5 us: comm_call(): pl.pallas_call(kernel, out_shape=tuple(out_shapes), in_specs=[spec] * len...]
    pallas_call x1, Pallas kernels: 28.8 us -> 23.4 us  [attend(): pl.pallas_call(attend_kernel, out_shape=(jax.ShapeDtypeStruct((2, full_le...]
where the time goes in v3:
time: 261 us; the launch traced here: 260 us
  Pallas kernels  248 us (95%)
  local copies, waits for them, and re-layouts  8.57 us (3%)
  other arithmetic  2.69 us (1%)
    pallas_call x1, Pallas kernels, feed_forward(): pl.pallas_call(feed_kernel, out_shape=outs, in_specs=[VMEM_SPEC] * len(in...  106 us
    pallas_call x2, Pallas kernels, comm_call(): pl.pallas_call(kernel, out_shape=tuple(out_shapes), in_specs=[spec] * len...  92.5 us
    pallas_call x1, Pallas kernels, attend_back(): pl.pallas_call(attend_back_kernel, out_shape=(jax.ShapeDtypeStruct((full_...  25.3 us
    pallas_call x1, Pallas kernels, attend(): pl.pallas_call(attend_kernel, out_shape=(jax.ShapeDtypeStruct((2, full_le...  23.4 us
    unnamed x26, local copies, waits for them, and re-layouts  8.57 us

profile of v3, /device:TPU:0, one launch (start us, length us, event | category | flops | bytes accessed | tf_op | source)
XLA Modules:
  0.0 260.3 jit_solution(1819036611545892243)
XLA Ops:
  0.6 0.7 convert_element_type.7
  1.3 0.7 fusion.9
  2.0 0.7 fusion.11.vec_ref
  2.7 0.0 copy-start
  2.7 1.1 copy-done
  3.8 0.0 copy-start.2
  3.8 1.1 copy-done.2
  4.9 0.0 copy-start.4
  4.9 0.9 copy-done.4
  5.8 0.0 copy-start.7
  5.8 0.8 copy-done.7
  6.6 0.8 copy-done.8
  7.4 0.8 copy-done.9
  8.2 0.8 copy-done.10
  9.0 0.8 copy-done.11
  9.7 48.9 %gather_inputs.1 = (bf16[8,128,768]{2,1,0:T(8,128)(2,1)S(1)}, bf16[8,3,96,192]{3,2,1,0:T(8,128)(2,1)S(1)}, bf16[2,4,4,160,192]{4,3,2,1,0:T(8,128)(2,1)S(1)}, bf1...) custom-call(bf16[128,768]{1,0:T(8,128)(2,1)S(1)} %bitcast.7, ...), custom_call_target="tpu_custom_call" | custom-call | tf_op jit(solution)/shard_map/gather_inputs/pallas_call | solution.py:661
  58.7 0.0 copy-start.1
  58.7 0.0 copy-start.3
  58.7 0.0 copy-start.5
  58.7 0.0 copy-start.6
  58.7 23.4 %attend.1 = (bf16[2,1024,64]{2,1,0:T(8,128)(2,1)S(1)}, bf16[2,1024,64]{2,1,0:T(8,128)(2,1)S(1)}, bf16[2,1024,64]{2,1,0:T(8,128)(2,1)S(1)}, bf16[2,512,64]{2,1,0:...) custom-call(bf16[8,128,768]{2,1,0:T(8,128)(2,1)S(1)} %get-tuple-elem, ...), custom_call_target="tpu_custom_call" | custom-call | tf_op jit(solution)/shard_map/attend/pallas_call | solution.py:354
  82.1 0.0 copy-done.1
  82.1 0.0 copy-done.3
  82.1 0.0 copy-done.5
  82.1 0.0 copy-done.6
  82.1 105.6 %feed_forward.1 = (bf16[128,768]{1,0:T(8,128)(2,1)S(1)}, f32[128,768]{1,0:T(8,128)S(1)}, f32[8,8,128]{2,1,0:T(8,128)S(1)}, bf16[8,128,768]{2,1,0:T(8,128)(2,1)S(...) custom-call(bf16[8,128,128]{2,1,0:T(8,128)(2,1)S(1)} %get-tuple-element.63.ctx_ref,, ...), custom_call_target="tpu_custom_call" | custom-call | tf_op jit(solution)/shard_map/feed_forward/pallas_call | solution.py:1040
  187.7 25.3 %attend_back.1 = (bf16[1024,384]{1,0:T(8,128)(2,1)S(1)}, bf16[512,256]{1,0:T(8,128)(2,1)S(1)}, f32[8,384]{1,0:T(8,128)S(1)}) custom-call(bf16[2,1024,64]{2,1,0:T(8,128)(2,1)S(1)} %get-tuple-element.70.q_ref, bf16[2,1024,64]{2,1,0:T(8,128)(2,1)S(1)} %get-tuple-element.71.k_ref, bf16[2,1024,64]{2,1,0:T(8,128)(2,1)S(1)} %get-tuple-element.72.v_ref, ...), custom_call_target="tpu_custom_call" | custom-call | tf_op jit(solution)/shard_map/attend_back/pallas_call | solution.py:525
  213.0 43.6 %settle_grads.1 = (bf16[4,128,768]{2,1,0:T(8,128)(2,1)S(1)}, f32[4,8,128]{2,1,0:T(8,128)S(1)}, f32[8,8,384]{2,1,0:T(8,128)S(1)}, bf16[2,96,384]{2,1,0:T(8,128)(2...) custom-call(f32[8,8,128]{2,1,0:T(8,128)S(1)} %get-tuple-element.69.vec_ref, ...), custom_call_target="tpu_custom_call" | custom-call | tf_op jit(solution)/shard_map/settle_grads/pallas_call | solution.py:661
  256.6 1.5 finish.1
  258.1 0.6 reduce
  258.7 0.9 copy.29
  259.6 0.7 copy.31
  (4 shorter events, 0.0 us)
Async XLA Ops:
  2.7 1.1 copy-start
  3.8 1.1 copy-start.2
  4.9 0.9 copy-start.4
  5.8 0.8 copy-start.7
  6.6 0.8 copy-start.8
  7.4 0.8 copy-start.9
  8.2 0.8 copy-start.10
  9.0 0.8 copy-start.11
  58.7 23.4 %copy-start.1 = (bf16[768,384]{1,0:T(8,128)(2,1)S(1)}, bf16[768,384]{1,0:T(8,128)(2,1)}, u32[]{:S(2)}) copy-start(bf16[768,384]{1,0:T(8,128)(2,1)} %up_ref.3) | copy-start | bytes 1769476
  58.7 23.4 %copy-start.3 = (bf16[384,768]{1,0:T(8,128)(2,1)S(1)}, bf16[384,768]{1,0:T(8,128)(2,1)}, u32[]{:S(2)}) copy-start(bf16[384,768]{1,0:T(8,128)(2,1)} %down_ref.3) | copy-start | bytes 1769476
  58.7 23.4 %copy-start.5 = (bf16[1,128,768]{2,1,0:T(8,128)(2,1)S(1)}, bf16[1,128,768]{2,1,0:T(8,128)(2,1)}, u32[]{:S(2)}) copy-start(bf16[1,128,768]{2,1,0:T(8,128)(2,1)} %param.15) | copy-start | bytes 589828
  58.7 23.4 %copy-start.6 = (bf16[1,128,768]{2,1,0:T(8,128)(2,1)S(1)}, bf16[1,128,768]{2,1,0:T(8,128)(2,1)}, u32[]{:S(2)}) copy-start(bf16[1,128,768]{2,1,0:T(8,128)(2,1)} %param.29) | copy-start | bytes 589828

commit v4 on v3

--- a/solution.py
+++ b/solution.py
@@ -217,7 +217,7 @@
 def attend_kernel(
     xs_ref,
     qkvs_ref,
-    mts_ref,
+    tables_ref,
     vecs_ref,
     q_ref,
     k_ref,
@@ -227,7 +227,6 @@
     p_ref,
     ctx_ref,
     w_ref,
-    mix_ref,
     table_ref,
     segc_ref,
     place_ref,
@@ -247,8 +246,8 @@
     scale = 1.0 / math.sqrt(3.0 * DH)
     units = p_ref.shape[0]
     shard_rows = qkvs_ref.shape[2]
-    table_rows = mts_ref.shape[3] - shard_rows
-    batches = mts_ref.shape[1]
+    table_rows = tables_ref.shape[3]
+    batches = tables_ref.shape[1]
     for part in range(at.tokens):
         pieces = []
         for i in range(3):
@@ -256,12 +255,8 @@
             pieces.append(jnp.where(at.core == 0, piece[:, :group], piece[:, DH:]))
         w_ref[part * shard_rows : (part + 1) * shard_rows] = jnp.concatenate(pieces, axis=1)
         core, chip = part % 2, part // 2
-        whole = [mts_ref[core, row, chip] for row in range(batches)]
-        mix_ref[part * shard_rows : (part + 1) * shard_rows] = jnp.concatenate(
-            [piece[:shard_rows] for piece in whole], axis=1
-        )
         table_ref[part * table_rows : (part + 1) * table_rows] = jnp.concatenate(
-            [piece[shard_rows:] for piece in whole], axis=1
+            [tables_ref[core, row, chip] for row in range(batches)], axis=1
         )
         own_seg = vecs_ref[part, 9:10].astype(jnp.float32)
         segc_ref[part * BLOCK : (part + 1) * BLOCK] = jnp.broadcast_to(own_seg, (BLOCK, BLOCK)).T
@@ -341,11 +336,10 @@
         ctx_ref[part] = jnp.concatenate([held_ref[0, rows], held_ref[1, rows]], axis=1)
 
 
-def attend(xs, qkvs, mts, vecs):
+def attend(xs, qkvs, tables, vecs):
     tokens, local_len, width = xs.shape
     full_len = tokens * local_len
-    shard_rows = qkvs.shape[2]
-    buckets = tokens * (mts.shape[3] - shard_rows)
+    buckets = tokens * tables.shape[3]
     blocks = full_len // BLOCK
     units = 3 * blocks // 2
     band_width = buckets + BLOCK
@@ -362,11 +356,10 @@
             jax.ShapeDtypeStruct((units, BLOCK, full_len), low),
             jax.ShapeDtypeStruct((tokens, local_len, 2 * DH), low),
             jax.ShapeDtypeStruct((width, 6 * DH), low),
-            jax.ShapeDtypeStruct((width, width), low),
             jax.ShapeDtypeStruct((buckets, width), low),
         ),
         in_specs=[pl.BlockSpec(memory_space=pltpu.VMEM)] * 4,
-        out_specs=[pl.BlockSpec(memory_space=pltpu.VMEM)] * 10,
+        out_specs=[pl.BlockSpec(memory_space=pltpu.VMEM)] * 9,
         scratch_shapes=[
             pltpu.VMEM((full_len, BLOCK), wide),
             pltpu.VMEM((2, pad_blocks, BLOCK, band_width), wide),
@@ -376,7 +369,7 @@
         ],
         compiler_params=pltpu.CompilerParams(vmem_limit_bytes=ATTEND_VMEM),
         name="attend",
-    )(xs, qkvs, mts, vecs)
+    )(xs, qkvs, tables, vecs)
 
 
 def attend_back_kernel(
@@ -550,7 +543,8 @@
 
 MESH = pl.DeviceIdType.MESH
 VMEM_SPEC = pl.BlockSpec(memory_space=pltpu.VMEM)
-ANY_SPEC = pl.BlockSpec(memory_space=pl.ANY)
+HBM_SPEC = pl.BlockSpec(memory_space=pltpu.HBM)
+CHUNKS = 2
 
 
 class Place:
@@ -675,17 +669,205 @@
     return jax.ShapeDtypeStruct(tuple(lead) + tuple(array.shape), array.dtype)
 
 
+def pick(values, index):
+    out = jnp.int32(values[0])
+    for i in range(1, len(values)):
+        out = jnp.where(index == i, jnp.int32(values[i]), out)
+    return out
+
+
+def arrival_order(at):
+    chips = range(at.chips)
+    lists = [sorted((j for j in chips if j != z), key=lambda j: (abs(j - z), j)) for z in chips]
+    return [pick([lists[z][t] for z in chips], at.chip) for t in range(at.chips - 1)]
+
+
+def return_order(at):
+    chips = range(at.chips)
+
+    def away(j, z):
+        end = at.chips - 1 if j < z else 0
+        return (abs(j - end) + abs(end - z), j)
+
+    lists = [sorted((j for j in chips if j != z), key=lambda j: away(j, z)) for z in chips]
+    return [pick([lists[z][t] for z in chips], at.chip) for t in range(at.chips - 1)]
+
+
+def goes_on(at, j):
+    above = jnp.logical_and(j < at.chip, at.chip < at.chips - 1)
+    below = jnp.logical_and(j > at.chip, at.chip > 0)
+    return jnp.logical_or(above, below)
+
+
+def line_peer(at, step):
+    return (at.row, 2 * (at.chip + step) + at.core)
+
+
+class LineGather:
+    def __init__(self, at, buf, slot, sems, own=None):
+        self.at, self.buf, self.slot, self.own = at, buf, slot, own
+        self.send_sems, self.recv_sems = sems
+        self.rows = buf.shape[1] // CHUNKS
+
+    def copy(self, j, h, step, k, own=False):
+        window = pl.ds(h * self.rows, self.rows)
+        home = self.buf.at[self.slot(j), window]
+        src = self.own.at[window] if own and self.own is not None else home
+        return pltpu.make_async_remote_copy(
+            src_ref=src,
+            dst_ref=home,
+            send_sem=self.send_sems.at[k * CHUNKS + h],
+            recv_sem=self.recv_sems.at[j * CHUNKS + h],
+            device_id=line_peer(self.at, step),
+            device_id_type=MESH,
+        )
+
+    def own_each(self, act):
+        z, n = self.at.chip, self.at.chips
+        for h in range(CHUNKS):
+
+            @pl.when(z < n - 1)
+            def _():
+                act(self.copy(z, h, 1, z, own=True))
+
+            @pl.when(z > 0)
+            def _():
+                act(self.copy(z, h, -1, n, own=True))
+
+    def start(self):
+        self.own_each(lambda copy: copy.start())
+
+    def arrive(self, j):
+        step = jnp.where(j < self.at.chip, 1, -1)
+        for h in range(CHUNKS):
+            self.copy(j, h, -step, j).wait_recv()
+
+            @pl.when(goes_on(self.at, j))
+            def _():
+                self.copy(j, h, step, j).start()
+
+    def drain(self, order):
+        self.own_each(lambda copy: copy.wait_send())
+        for j in order:
+            step = jnp.where(j < self.at.chip, 1, -1)
+
+            @pl.when(goes_on(self.at, j))
+            def _():
+                for h in range(CHUNKS):
+                    self.copy(j, h, step, j).wait_send()
+
+
+class LineReduce:
+    def __init__(self, at, part, got, sems):
+        self.at, self.part, self.got = at, part, got
+        self.send_sems, self.recv_sems = sems
+        self.rows = part.shape[1] // CHUNKS
+
+    def copy(self, j, h):
+        z, n = self.at.chip, self.at.chips
+        window = pl.ds(h * self.rows, self.rows)
+        slot = jnp.where(z + 1 == j, n, j)
+        return pltpu.make_async_remote_copy(
+            src_ref=self.part.at[j, window],
+            dst_ref=self.got.at[slot, window],
+            send_sem=self.send_sems.at[j * CHUNKS + h],
+            recv_sem=self.recv_sems.at[slot * CHUNKS + h],
+            device_id=line_peer(self.at, jnp.where(j < z, -1, 1)),
+            device_id_type=MESH,
+        )
+
+    def landed(self, slot, h, step):
+        window = pl.ds(h * self.rows, self.rows)
+        return pltpu.make_async_remote_copy(
+            src_ref=self.got.at[slot, window],
+            dst_ref=self.got.at[slot, window],
+            send_sem=self.send_sems.at[h],
+            recv_sem=self.recv_sems.at[slot * CHUNKS + h],
+            device_id=line_peer(self.at, step),
+            device_id_type=MESH,
+        )
+
+    def send(self, j):
+        for h in range(CHUNKS):
+            self.copy(j, h).start()
+
+    def send_last(self, j):
+        @pl.when(jnp.logical_not(goes_on(self.at, j)))
+        def _():
+            self.send(j)
+
+    def pass_on(self, order):
+        z, n = self.at.chip, self.at.chips
+        wide = jnp.float32
+
+        @pl.when(jnp.logical_and(z > 0, z < n - 1))
+        def _():
+            for j in order:
+                step = jnp.where(j < z, 1, -1)
+                for h in range(CHUNKS):
+                    self.landed(j, h, step).wait_recv()
+                    window = pl.ds(h * self.rows, self.rows)
+                    total = self.part[j, window].astype(wide) + self.got[j, window].astype(wide)
+                    self.part[j, window] = total.astype(self.part.dtype)
+                    self.copy(j, h).start()
+
+    def clear(self):
+        z, n = self.at.chip, self.at.chips
+
+        @pl.when(z == n - 1)
+        def _():
+            self.got[z] = jnp.zeros(self.got.shape[1:], self.got.dtype)
+
+        @pl.when(z == 0)
+        def _():
+            self.got[n] = jnp.zeros(self.got.shape[1:], self.got.dtype)
+
+    def collect(self):
+        z, n = self.at.chip, self.at.chips
+        for h in range(CHUNKS):
+
+            @pl.when(z < n - 1)
+            def _():
+                self.landed(z, h, 1).wait_recv()
+
+            @pl.when(z > 0)
+            def _():
+                self.landed(n, h, -1).wait_recv()
+
+        return self.got[z].astype(jnp.float32) + self.got[n].astype(jnp.float32)
+
+    def drain(self, order):
+        for j in order:
+            for h in range(CHUNKS):
+                self.copy(j, h).wait_send()
+
+
+def gather_sems(chips):
+    return [
+        pltpu.SemaphoreType.DMA(((chips + 1) * CHUNKS,)),
+        pltpu.SemaphoreType.DMA((chips * CHUNKS,)),
+    ]
+
+
+def reduce_sems(chips):
+    return [
+        pltpu.SemaphoreType.DMA((chips * CHUNKS,)),
+        pltpu.SemaphoreType.DMA(((chips + 1) * CHUNKS,)),
+    ]
+
+
 def gather_kernel(
     x_ref, wq_ref, wk_ref, wv_ref, mix_ref, table_ref, vec_ref, up_ref, down_ref,
-    xs_ref, qkvs_ref, mts_ref, vecs_ref, up2_ref, down2_ref, *sems,
+    xs_ref, qkvs_ref, mixs_ref, tables_ref, vecs_ref, up2_ref, down2_ref,
+    line_send, line_recv, *sems,
 ):
     at = Place()
     wires = Wires(*sems)
     b, s, z, c = at.row, at.part, at.chip, at.core
     off_diagonal = b != z
     turned = (z, 2 * b + c)
+    peers = at.seq_peers() + at.row_peers()
     barrier = pltpu.get_barrier_semaphore()
-    peers = at.chip_peers() + at.plane_peers()
     for peer in peers:
         pl.semaphore_signal(barrier, inc=1, device_id=peer, device_id_type=MESH)
 
@@ -722,31 +904,26 @@
         for stay in stays:
             stay.start()
 
-    rows = mix_ref.shape[0]
-    table_rows = table_ref.shape[0]
-    mix_home = mts_ref.at[c, b, z, pl.ds(0, rows)]
-    table_home = mts_ref.at[c, b, z, pl.ds(rows, table_rows)]
-    mt_sends = []
-    for k in range(1, at.chips):
-        peer = at.along_chips(k)[1]
-        mt_sends.append(wires.send(mix_ref, mix_home, peer))
-        mt_sends.append(wires.send(table_ref, table_home, peer))
-    x_sends, vec_sends = [], []
-    for k in range(1, at.chips):
-        peer = at.along_chips(k)[1]
-        x_sends.append(wires.send(x_ref, xs_ref.at[s], peer))
-        vec_sends.append(wires.send(vec_ref, vecs_ref.at[s], peer))
+    table_home = tables_ref.at[c, b, z]
+    table_sends = [
+        wires.send(table_ref, table_home, at.along_chips(k)[1]) for k in range(1, at.chips)
+    ]
+    kept = wires.local(table_ref, table_home)
+    line = LineGather(at, xs_ref, lambda j: 2 * j + c, (line_send, line_recv), own=x_ref)
+    line.start()
+    last = [wires.send(vec_ref, vecs_ref.at[s], at.along_seq(k)[1]) for k in range(1, at.tokens)]
+    last += [
+        wires.send(mix_ref, mixs_ref.at[z], at.along_chips(k)[1]) for k in range(1, at.chips)
+    ]
+    last += [
+        wires.send(x_ref, xs_ref.at[s], at.partner()),
+        wires.send(up_ref, up2_ref, at.partner()),
+        wires.send(down_ref, down2_ref, at.partner()),
+    ]
     own = [
         wires.local(x_ref, xs_ref.at[s]),
-        wires.local(mix_ref, mix_home),
-        wires.local(table_ref, table_home),
+        wires.local(mix_ref, mixs_ref.at[z]),
         wires.local(vec_ref, vecs_ref.at[s]),
-    ]
-    last = [
-        wires.send(x_ref, xs_ref.at[s], at.partner()),
-        wires.send(vec_ref, vecs_ref.at[s], at.partner()),
-        wires.send(up_ref, up2_ref, at.partner()),
-        wires.send(down_ref, down2_ref, at.partner()),
     ]
 
     @pl.when(off_diagonal)
@@ -759,31 +936,40 @@
         for stay in stays:
             stay.wait()
 
-    for k in range(1, 2 * at.batches):
-        peer = at.along_plane(k)[2]
-        last.append(wires.send(qkvs_ref.at[2 * b + c], qkvs_ref.at[2 * b + c], peer))
-    for copy in mt_sends:
+    mine = qkvs_ref.at[2 * b + c]
+    qkv_sends = [wires.send(mine, mine, at.along_rows(k)[1]) for k in range(1, at.batches)]
+    last.append(wires.send(mine, mine, at.partner()))
+    for copy in table_sends:
+        copy.wait_recv()
+    kept.wait()
+    mine = tables_ref.at[c, b]
+    row_sends = [wires.send(mine, mine, at.along_rows(k)[1]) for k in range(1, at.batches)]
+    last.append(wires.send(mine, mine, at.partner()))
+    order = arrival_order(at)
+
+    def arrived(j):
+        line.arrive(j)
+        home = xs_ref.at[2 * j + c]
+        last.append(wires.send(home, home, at.partner()))
+
+    for j in order[:2]:
+        arrived(j)
+    for k in range(1, at.batches):
+        qkv_sends[k - 1].wait_recv()
+        home = qkvs_ref.at[2 * at.from_rows(k) + c]
+        last.append(wires.send(home, home, at.partner()))
+    for k in range(1, at.batches):
+        row_sends[k - 1].wait_recv()
+        home = tables_ref.at[c, at.from_rows(k)]
+        last.append(wires.send(home, home, at.partner()))
+    for j in order[2:]:
+        arrived(j)
+    for copy in last:
         copy.wait_recv()
     for copy in own:
         copy.wait()
-    row_sends = []
-    for k in range(1, at.batches):
-        peer = at.along_rows(k)[1]
-        row_sends.append(wires.send(mts_ref.at[c, b], mts_ref.at[c, b], peer))
-    last.append(wires.send(mts_ref.at[c, b], mts_ref.at[c, b], at.partner()))
-    for k in range(1, at.batches):
-        row = at.from_rows(k)
-        row_sends[k - 1].wait_recv()
-        last.append(wires.send(mts_ref.at[c, row], mts_ref.at[c, row], at.partner()))
-    for k in range(1, at.chips):
-        index = 2 * at.from_chips(k) + c
-        x_sends[k - 1].wait_recv()
-        last.append(wires.send(xs_ref.at[index], xs_ref.at[index], at.partner()))
-        vec_sends[k - 1].wait_recv()
-        last.append(wires.send(vecs_ref.at[index], vecs_ref.at[index], at.partner()))
-    for copy in last:
-        copy.wait_recv()
     wires.finish()
+    line.drain(order)
 
     @pl.when(off_diagonal)
     def _():
@@ -794,20 +980,28 @@
 def gather_inputs(x, w_query, w_key, w_value, w_mix, rel_table, vec, up, down):
     tokens, batches = lax.axis_size("seq"), lax.axis_size("batch")
     chips = tokens // 2
-    rows, columns = w_mix.shape
     outs = (
         like(x, tokens),
         like(w_query, tokens, 3),
-        jax.ShapeDtypeStruct(
-            (2, batches, chips, rows + rel_table.shape[0], columns), w_mix.dtype
-        ),
+        like(w_mix, chips),
+        like(rel_table, 2, batches, chips),
         like(vec, tokens),
         like(up),
         like(down),
     )
-    sends = 3 + 4 * (chips - 1) + 4 + 2 * batches - 1 + 2 * (batches - 1) + 1 + 2 * (chips - 1)
+    sends = 3 + 2 * (chips - 1) + tokens - 1 + 3 + 4 * (batches - 1) + 2 + chips - 1
     inputs = (x, w_query, w_key, w_value, w_mix, rel_table, vec, up, down)
-    return comm_call(gather_kernel, "gather_inputs", 0, outs, inputs, sends, 7, spec=ANY_SPEC)
+    return comm_call(
+        gather_kernel,
+        "gather_inputs",
+        0,
+        outs,
+        inputs,
+        sends,
+        7,
+        scratch=gather_sems(chips),
+        spec=HBM_SPEC,
+    )
 
 
 def norm_parts(values):
@@ -825,23 +1019,46 @@
     return scale * (inner - mean - unit * slope)
 
 
+def line_pass(gather, reduce, order, work):
+    def finish(j):
+        work(j)
+        reduce.send_last(j)
+
+    gather.arrive(order[0])
+    gather.arrive(order[1])
+    finish(order[0])
+    gather.arrive(order[2])
+    finish(order[1])
+    finish(order[2])
+
+
 def feed_kernel(
-    ctx_ref, x_ref, mix_ref, vecs_ref, up_ref, down_ref, up2_ref, down2_ref, out_grad_ref,
-    output_ref, pre_grad_ref, sums_ref, attn_ref, ups_ref, downs_ref, upbs_ref,
-    got_ref, hid_ref, act_ref, slope_ref, part_ref, ffn_ref, grad_ref, inner_ref,
-    back_ref, backs_ref, low_ref, upg_ref, downg_ref, upb_ref, vec_ref, *sems,
+    ctx_ref, x_ref, mixs_ref, vecs_ref, up_ref, down_ref, up2_ref, down2_ref, out_grad_ref,
+    output_ref, pre_grad_ref, sums_ref, attn_ref, mix_ref, ups_ref, downs_ref, upbs_ref,
+    got_ref, mixall_ref, hid_ref, act_ref, slope_ref, part_ref, ffn_ref, grad_ref, inner_ref,
+    back_ref, backs_ref, up_away_ref, down_away_ref, upb_away_ref,
+    up_got_ref, down_got_ref, upb_got_ref, upg_ref, downg_ref, upb_ref, vec_ref,
+    hid_send, hid_recv, ffn_send, ffn_recv, grad_send, grad_recv, back_send, back_recv,
+    attn_send, attn_recv, *sems,
 ):
     at = Place()
     wires = Wires(*sems)
     low, wide = jnp.bfloat16, jnp.float32
-    s, z, c = at.part, at.chip, at.core
-    meet(at.seq_peers() + at.cross_row_peers())
+    b, s, z, c = at.row, at.part, at.chip, at.core
+    order, returns = arrival_order(at), return_order(at)
+    meet(at.seq_peers() + at.row_peers())
     last, own = [], []
     swaps = []
     for k in range(1, at.tokens):
         part, peer = at.along_seq(k)
         swaps.append(wires.send(ctx_ref.at[part], got_ref.at[s], peer))
     kept = wires.local(ctx_ref.at[s], got_ref.at[s])
+    mix_sends = [
+        wires.send(mixs_ref, mixall_ref.at[c, b], at.along_rows(k)[1])
+        for k in range(1, at.batches)
+    ]
+    mix_lasts = [wires.send(mixs_ref, mixall_ref.at[c, b], at.partner())]
+    mix_kept = wires.local(mixs_ref, mixall_ref.at[c, b])
     lanes = x_ref.shape[1] // at.tokens
     hidden_here = up_ref.shape[1]
     vec_ref[...] = jnp.concatenate(
@@ -858,6 +1075,18 @@
         + [vecs_ref[partner, 10 + i : 11 + i].astype(wide) for i in range(up_rows)],
         axis=1,
     )
+    for k in range(1, at.batches):
+        mix_sends[k - 1].wait_recv()
+        home = mixall_ref.at[c, at.from_rows(k)]
+        mix_lasts.append(wires.send(home, home, at.partner()))
+    for copy in mix_lasts:
+        copy.wait_recv()
+    mix_kept.wait()
+    shard_rows = mixs_ref.shape[1]
+    for part in range(at.tokens):
+        mix_ref[part * shard_rows : (part + 1) * shard_rows] = jnp.concatenate(
+            [mixall_ref[part % 2, row, part // 2] for row in range(at.batches)], axis=1
+        )
     for copy in swaps:
         copy.wait_recv()
     kept.wait()
@@ -871,15 +1100,12 @@
     unit1, scale1 = norm_parts(pre_norm)
     hidden = unit1 * gain1 + shift1
     hid_ref[z] = hidden.astype(low)
-    spread = [
-        wires.send(hid_ref.at[z], hid_ref.at[z], at.along_chips(k)[1]) for k in range(1, at.chips)
-    ]
-
-    ffn_sends = []
-    for k in range(at.chips):
-        chip = at.from_chips(k)
-        if k:
-            spread[k - 1].wait_recv()
+    hid_line = LineGather(at, hid_ref, lambda j: j, (hid_send, hid_recv))
+    ffn_line = LineReduce(at, part_ref, ffn_ref, (ffn_send, ffn_recv))
+    hid_line.start()
+    ffn_line.clear()
+
+    def ffn(chip):
         rows = hid_ref[chip]
         inner = jnp.concatenate(
             [dot_nn(rows, up_ref[...]), dot_nn(rows, up2_ref[...])], axis=1
@@ -895,32 +1121,26 @@
             dot_nn(act[:, :hidden_here], down_ref[...])
             + dot_nn(act[:, hidden_here:], down2_ref[...])
         ).astype(low)
-        if k:
-            peer = (at.row, 2 * chip + c)
-            ffn_sends.append(wires.send(part_ref.at[chip], ffn_ref.at[at.chips - 1 - k], peer))
-    total = part_ref[z].astype(wide)
-    for k in range(1, at.chips):
-        ffn_sends[k - 1].wait_recv()
-        total = total + ffn_ref[at.chips - 1 - k].astype(wide)
+
+    ffn(z)
+    line_pass(hid_line, ffn_line, order, ffn)
+    ffn_line.pass_on(returns)
+    total = part_ref[z].astype(wide) + ffn_line.collect()
     mixed = hidden + total + bias_down
     unit2, scale2 = norm_parts(mixed)
     output_ref[...] = (unit2 * gain2 + shift2).astype(low)
     out_grad = out_grad_ref[...].astype(wide)
     mixed_grad = norm_back(out_grad, gain2, unit2, scale2)
     grad_ref[z] = mixed_grad.astype(low)
-    spread = [
-        wires.send(grad_ref.at[z], grad_ref.at[z], at.along_chips(k)[1])
-        for k in range(1, at.chips)
-    ]
+    grad_line = LineGather(at, grad_ref, lambda j: j, (grad_send, grad_recv))
+    back_line = LineReduce(at, back_ref, backs_ref, (back_send, back_recv))
+    grad_line.start()
+    back_line.clear()
     gain2_grad = jnp.sum(out_grad * unit2, axis=0, keepdims=True)
     shift2_grad = jnp.sum(out_grad, axis=0, keepdims=True)
     downb_grad = jnp.sum(mixed_grad, axis=0, keepdims=True)
 
-    back_sends = []
-    for k in range(at.chips):
-        chip = at.from_chips(k)
-        if k:
-            spread[k - 1].wait_recv()
+    def back(chip):
         rows = grad_ref[chip]
         act_grad = jnp.concatenate(
             [dot_nt(rows, down_ref[...]), dot_nt(rows, down2_ref[...])], axis=1
@@ -931,49 +1151,53 @@
             dot_nt(inner_low[:, :hidden_here], up_ref[...])
             + dot_nt(inner_low[:, hidden_here:], up2_ref[...])
         ).astype(low)
-        if k:
-            peer = (at.row, 2 * chip + c)
-            back_sends.append(wires.send(back_ref.at[chip], backs_ref.at[at.chips - 1 - k], peer))
-
+
+    back(z)
+    line_pass(grad_line, back_line, order, back)
     width = x_ref.shape[1]
     columns = width // at.batches
     inner_all = inner_ref[...].reshape(at.chips * BLOCK, 2 * hidden_here)
     act_all = act_ref[...].reshape(at.chips * BLOCK, 2 * hidden_here)
     hid_all = hid_ref[...].reshape(at.chips * BLOCK, width)
     grad_all = grad_ref[...].reshape(at.chips * BLOCK, width)
-    up_grad = dot_tn(hid_all, inner_all).astype(low)
-    down_grad = dot_tn(act_all, grad_all).astype(low)
+    near, away = slice(0, hidden_here), slice(hidden_here, 2 * hidden_here)
+    up_away_ref[...] = dot_tn(hid_all, inner_all[:, away]).astype(low)
+    down_grad = dot_tn(act_all, grad_all)
+    for row in range(at.batches):
+        piece = slice(row * columns, (row + 1) * columns)
+        down_away_ref[row] = down_grad[away, piece].astype(low)
     upb_grad = jnp.sum(inner_all.astype(wide), axis=0, keepdims=True)
-    for d in range(2):
-        half = slice(d * hidden_here, (d + 1) * hidden_here)
-        upb_ref[d] = jnp.broadcast_to(upb_grad[:, half], upb_ref.shape[1:])
-        for row in range(at.batches):
-            piece = slice(row * columns, (row + 1) * columns)
-            upg_ref[d, row] = up_grad[piece, half]
-            downg_ref[d, row] = down_grad[half, piece]
-    mine = 2 * at.row + c
-    for k in range(1, 2 * at.batches):
-        row, core, peer = at.along_plane(k)
-        other = lax.rem(core + c, 2)
-        last.append(wires.send(upg_ref.at[other, row], ups_ref.at[mine], peer))
-        last.append(wires.send(downg_ref.at[other, row], downs_ref.at[mine], peer))
-        last.append(wires.send(upb_ref.at[other], upbs_ref.at[mine], peer))
-    own.append(wires.local(upg_ref.at[0, at.row], ups_ref.at[mine]))
-    own.append(wires.local(downg_ref.at[0, at.row], downs_ref.at[mine]))
-    own.append(wires.local(upb_ref.at[0], upbs_ref.at[mine]))
-
-    total = back_ref[z].astype(wide)
-    for k in range(1, at.chips):
-        back_sends[k - 1].wait_recv()
-        total = total + backs_ref[at.chips - 1 - k].astype(wide)
+    upb_away_ref[...] = jnp.broadcast_to(upb_grad[:, away], upb_away_ref.shape)
+    halves = [
+        wires.send(up_away_ref, up_got_ref, at.partner()),
+        wires.send(down_away_ref, down_got_ref, at.partner()),
+        wires.send(upb_away_ref, upb_got_ref, at.partner()),
+    ]
+    back_line.pass_on(returns)
+    up_own = dot_tn(hid_all, inner_all[:, near])
+    for copy in halves:
+        copy.wait_recv()
+    upb_ref[...] = jnp.broadcast_to(upb_grad[:, near], upb_ref.shape) + upb_got_ref[...]
+    up_sum = (up_own + up_got_ref[...].astype(wide)).astype(low)
+    for row in range(at.batches):
+        upg_ref[row] = up_sum[row * columns : (row + 1) * columns]
+        piece = slice(row * columns, (row + 1) * columns)
+        downg_ref[row] = (down_grad[near, piece] + down_got_ref[row].astype(wide)).astype(low)
+    for k in range(1, at.batches):
+        row, peer = at.along_rows(k)
+        last.append(wires.send(upg_ref.at[row], ups_ref.at[b], peer))
+        last.append(wires.send(downg_ref.at[row], downs_ref.at[b], peer))
+        last.append(wires.send(upb_ref, upbs_ref.at[b], peer))
+    own.append(wires.local(upg_ref.at[b], ups_ref.at[b]))
+    own.append(wires.local(downg_ref.at[b], downs_ref.at[b]))
+    own.append(wires.local(upb_ref, upbs_ref.at[b]))
+    total = back_ref[z].astype(wide) + back_line.collect()
     hidden_grad = mixed_grad + total
     pre_grad = norm_back(hidden_grad, gain1, unit1, scale1)
-    low_ref[...] = pre_grad.astype(low)
-    spread = [
-        wires.send(low_ref, attn_ref.at[s], at.along_chips(k)[1]) for k in range(1, at.chips)
-    ]
-    last.append(wires.send(low_ref, attn_ref.at[s], at.partner()))
-    own.append(wires.local(low_ref, attn_ref.at[s]))
+    attn_ref[s] = pre_grad.astype(low)
+    attn_line = LineGather(at, attn_ref, lambda j: 2 * j + c, (attn_send, attn_recv))
+    attn_line.start()
+    last.append(wires.send(attn_ref.at[s], attn_ref.at[s], at.partner()))
     pre_grad_ref[...] = pre_grad
     gain1_grad = jnp.sum(hidden_grad * unit1, axis=0, keepdims=True)
     shift1_grad = jnp.sum(hidden_grad, axis=0, keepdims=True)
@@ -988,18 +1212,20 @@
         sums_ref[part] = jnp.concatenate(
             [sums[:, part * lanes : (part + 1) * lanes], spare], axis=1
         )
-    for k in range(1, at.chips):
-        index = 2 * at.from_chips(k) + c
-        spread[k - 1].wait_recv()
-        last.append(wires.send(attn_ref.at[index], attn_ref.at[index], at.partner()))
+    for j in order:
+        attn_line.arrive(j)
+        home = attn_ref.at[2 * j + c]
+        last.append(wires.send(home, home, at.partner()))
     for copy in last:
         copy.wait_recv()
     for copy in own:
         copy.wait()
     wires.finish()
-
-
-def feed_forward(ctx, x, m_mix, vecs, up, down, up2, down2, out_grad, ident):
+    for line in (hid_line, ffn_line, grad_line, back_line, attn_line):
+        line.drain(order)
+
+
+def feed_forward(ctx, x, mixs, vecs, up, down, up2, down2, out_grad, ident):
     tokens, batches = lax.axis_size("seq"), lax.axis_size("batch")
     chips = tokens // 2
     width = x.shape[1]
@@ -1011,38 +1237,48 @@
         jax.ShapeDtypeStruct(x.shape, wide),
         jax.ShapeDtypeStruct((tokens, 8, BLOCK), wide),
         jax.ShapeDtypeStruct((tokens,) + x.shape, low),
-        jax.ShapeDtypeStruct((2 * batches, columns, hidden_here), low),
-        jax.ShapeDtypeStruct((2 * batches, hidden_here, columns), low),
-        jax.ShapeDtypeStruct((2 * batches, 8, hidden_here), wide),
+        jax.ShapeDtypeStruct((width, width), low),
+        jax.ShapeDtypeStruct((batches, columns, hidden_here), low),
+        jax.ShapeDtypeStruct((batches, hidden_here, columns), low),
+        jax.ShapeDtypeStruct((batches, 8, hidden_here), wide),
     )
     block = (chips,) + x.shape
     wide_block = (chips, x.shape[0], 2 * hidden_here)
-    others = (chips - 1,) + x.shape
-    scratch = (
+    slots = (chips + 1,) + x.shape
+    up_half, bias_half = (width, hidden_here), (8, hidden_here)
+    down_half = (batches, hidden_here, columns)
+    scratch = [
         pltpu.VMEM(ctx.shape, low),
+        pltpu.VMEM((2, batches) + mixs.shape, low),
         pltpu.VMEM(block, low),
         pltpu.VMEM(wide_block, low),
         pltpu.VMEM(wide_block, wide),
         pltpu.VMEM(block, low),
-        pltpu.VMEM(others, low),
+        pltpu.VMEM(slots, low),
         pltpu.VMEM(block, low),
         pltpu.VMEM(wide_block, low),
         pltpu.VMEM(block, low),
-        pltpu.VMEM(others, low),
-        pltpu.VMEM(x.shape, low),
-        pltpu.VMEM((2, batches, columns, hidden_here), low),
-        pltpu.VMEM((2, batches, hidden_here, columns), low),
-        pltpu.VMEM((2, 8, hidden_here), wide),
+        pltpu.VMEM(slots, low),
+        pltpu.VMEM(up_half, low),
+        pltpu.VMEM(down_half, low),
+        pltpu.VMEM(bias_half, wide),
+        pltpu.VMEM(up_half, low),
+        pltpu.VMEM(down_half, low),
+        pltpu.VMEM(bias_half, wide),
+        pltpu.VMEM((batches, columns, hidden_here), low),
+        pltpu.VMEM((batches, hidden_here, columns), low),
+        pltpu.VMEM(bias_half, wide),
         pltpu.VMEM((16, width), wide),
-    )
-    inputs = (ctx, x, m_mix, vecs, up, down, up2, down2, out_grad)
-    sends = tokens - 1 + 4 * (chips - 1) + 3 * (2 * batches - 1) + 2 * (chips - 1) + 1
+    ]
+    scratch += (gather_sems(chips) + reduce_sems(chips)) * 2 + gather_sems(chips)
+    inputs = (ctx, x, mixs, vecs, up, down, up2, down2, out_grad)
+    sends = tokens - 1 + 2 * batches - 1 + 3 + 3 * (batches - 1) + chips
     return pl.pallas_call(
         feed_kernel,
         out_shape=outs,
         in_specs=[VMEM_SPEC] * len(inputs),
         out_specs=(VMEM_SPEC,) * len(outs),
-        scratch_shapes=list(scratch) + wire_scratch(sends, 5),
+        scratch_shapes=scratch + wire_scratch(sends, 5),
         compiler_params=pltpu.CompilerParams(
             collective_id=ident, has_side_effects=True, vmem_limit_bytes=FEED_VMEM
         ),
@@ -1320,7 +1556,7 @@
         and tokens == 2 * batches
         and width == 3 * DH * batches
         and (table_shard.shape[0] * tokens) % (4 * BLOCK) == 0
-        and tokens % 4 == 0
+        and tokens == 8
         and 10 + hidden_here // BLOCK <= 16
         and hidden_here % BLOCK == 0
     )
@@ -1342,12 +1578,12 @@
         [pack, segment_ids.astype(low), up_bias.reshape(hidden_here // BLOCK, BLOCK)], axis=0
     )
     pack = jnp.pad(pack, ((0, 16 - pack.shape[0]), (0, 0)))
-    xs, qkvs, mts, vecs, up2, down2 = gather_inputs(
+    xs, qkvs, mixs, tables, vecs, up2, down2 = gather_inputs(
         x, w_query, w_key, w_value, w_mix, rel_table, pack, w_up, w_down
     )
-    q, k, v, qrev, krev, probs, ctx, w_cat, m_mix, table = attend(xs, qkvs, mts, vecs)
-    output, pre_grad, sums, attn_all, ups, downs, upbs = feed_forward(
-        ctx, x, m_mix, vecs, w_up, w_down, up2, down2, out_grad[0], 1
+    q, k, v, qrev, krev, probs, ctx, w_cat, table = attend(xs, qkvs, tables, vecs)
+    output, pre_grad, sums, attn_all, m_mix, ups, downs, upbs = feed_forward(
+        ctx, x, mixs, vecs, w_up, w_down, up2, down2, out_grad[0], 1
     )
     dcat, rel_grad, cols = attend_back(q, k, v, qrev, krev, probs, m_mix, attn_all)
     ins, vec_all, cols_all, dw_all, tab_all, mix_all = settle_grads(

time: 261 us -> 237 us (0.908)
  Pallas kernels: 248 us -> 225 us
    pallas_call x2, Pallas kernels: 92.5 us -> 77.8 us  [comm_call(): pl.pallas_call(kernel, out_shape=tuple(out_shapes), in_specs=[spec] * len...]
    pallas_call x1, Pallas kernels: 106 us -> 97 us  [feed_forward(): pl.pallas_call(feed_kernel, out_shape=outs, in_specs=[VMEM_SPEC] * len(in...]
where the time goes in v4:
time: 237 us
  Pallas kernels  225 us (95%)
  local copies, waits for them, and re-layouts  8.57 us (4%)
  other arithmetic  2.69 us (1%)
    pallas_call x1, Pallas kernels, feed_forward(): pl.pallas_call(feed_kernel, out_shape=outs, in_specs=[VMEM_SPEC] * len(in...  97 us
    pallas_call x2, Pallas kernels, comm_call(): pl.pallas_call(kernel, out_shape=tuple(out_shapes), in_specs=[spec] * len...  77.8 us
    pallas_call x1, Pallas kernels, attend_back(): pl.pallas_call(attend_back_kernel, out_shape=(jax.ShapeDtypeStruct((full_...  25.3 us
    pallas_call x1, Pallas kernels, attend(): pl.pallas_call(attend_kernel, out_shape=(jax.ShapeDtypeStruct((2, full_le...  23.4 us
    unnamed x26, local copies, waits for them, and re-layouts  8.57 us

profile of v4, /device:TPU:0, one launch (start us, length us, event | category | flops | bytes accessed | tf_op | source)
XLA Modules:
  0.0 236.7 jit_solution(5804270871950267565)
XLA Ops:
  0.6 0.7 convert_element_type.7
  1.3 0.7 fusion.9
  2.0 0.7 fusion.11.vec_ref
  2.7 0.0 copy-start
  2.7 1.1 copy-done
  3.8 0.0 copy-start.2
  3.8 1.1 copy-done.2
  4.9 0.0 copy-start.4
  4.9 0.9 copy-done.4
  5.8 0.0 copy-start.7
  5.8 0.8 copy-done.7
  6.6 0.8 copy-done.8
  7.4 0.8 copy-done.9
  8.2 0.8 copy-done.10
  9.0 0.8 copy-done.11
  9.7 36.5 %gather_inputs.1 = (bf16[8,128,768]{2,1,0:T(8,128)(2,1)S(1)}, bf16[8,3,96,192]{3,2,1,0:T(8,128)(2,1)S(1)}, bf16[4,96,192]{2,1,0:T(8,128)(2,1)S(1)}, bf16[2,4,4,6...) custom-call(bf16[128,768]{1,0:T(8,128)(2,1)S(1)} %bitcast.7, ...), custom_call_target="tpu_custom_call" | custom-call | tf_op jit(solution)/shard_map/gather_inputs/pallas_call | solution.py:655
  46.2 0.0 copy-start.1
  46.2 0.0 copy-start.3
  46.2 0.0 copy-start.5
  46.3 0.0 copy-start.6
  46.3 23.4 %attend.1 = (bf16[2,1024,64]{2,1,0:T(8,128)(2,1)S(1)}, bf16[2,1024,64]{2,1,0:T(8,128)(2,1)S(1)}, bf16[2,1024,64]{2,1,0:T(8,128)(2,1)S(1)}, bf16[2,512,64]{2,1,0:...) custom-call(bf16[8,128,768]{2,1,0:T(8,128)(2,1)S(1)} %get-tuple-elem, ...), custom_call_target="tpu_custom_call" | custom-call | tf_op jit(solution)/shard_map/attend/pallas_call | solution.py:348
  69.7 0.0 copy-done.1
  69.7 0.0 copy-done.3
  69.7 0.0 copy-done.5
  69.7 0.0 copy-done.6
  69.8 97.0 %feed_forward.1 = (bf16[128,768]{1,0:T(8,128)(2,1)S(1)}, f32[128,768]{1,0:T(8,128)S(1)}, f32[8,8,128]{2,1,0:T(8,128)S(1)}, bf16[8,128,768]{2,1,0:T(8,128)(2,1)S(...) custom-call(bf16[8,128,128]{2,1,0:T(8,128)(2,1)S(1)} %get-tuple-elem, ...), custom_call_target="tpu_custom_call" | custom-call | tf_op jit(solution)/shard_map/feed_forward/pallas_call | solution.py:1276
  166.8 25.3 %attend_back.1 = (bf16[1024,384]{1,0:T(8,128)(2,1)S(1)}, bf16[512,256]{1,0:T(8,128)(2,1)S(1)}, f32[8,384]{1,0:T(8,128)S(1)}) custom-call(bf16[2,1024,64]{2,1,0:T(8,128)(2,1)S(1)} %get-tuple-element.71.q_ref, bf16[2,1024,64]{2,1,0:T(8,128)(2,1)S(1)} %get-tuple-element.72.k_ref, bf16[2,1024,64]{2,1,0:T(8,128)(2,1)S(1)} %get-tuple-element.73.v_ref, ...), custom_call_target="tpu_custom_call" | custom-call | tf_op jit(solution)/shard_map/attend_back/pallas_call | solution.py:518
  192.1 41.3 %settle_grads.1 = (bf16[4,128,768]{2,1,0:T(8,128)(2,1)S(1)}, f32[4,8,128]{2,1,0:T(8,128)S(1)}, f32[8,8,384]{2,1,0:T(8,128)S(1)}, bf16[2,96,384]{2,1,0:T(8,128)(2...) custom-call(f32[8,8,128]{2,1,0:T(8,128)S(1)} %get-tuple-element.70.vec_ref, ...), custom_call_target="tpu_custom_call" | custom-call | tf_op jit(solution)/shard_map/settle_grads/pallas_call | solution.py:655
  233.4 1.2 finish.1
  234.6 0.6 reduce
  235.2 0.9 copy.29
  236.1 0.7 copy.31
  (4 shorter events, 0.0 us)
Async XLA Ops:
  2.7 1.1 copy-start
  3.8 1.1 copy-start.2
  4.9 0.9 copy-start.4
  5.8 0.8 copy-start.7
  6.6 0.8 copy-start.8
  7.4 0.8 copy-start.9
  8.2 0.8 copy-start.10
  9.0 0.8 copy-start.11
  46.2 23.5 %copy-start.1 = (bf16[768,384]{1,0:T(8,128)(2,1)S(1)}, bf16[768,384]{1,0:T(8,128)(2,1)}, u32[]{:S(2)}) copy-start(bf16[768,384]{1,0:T(8,128)(2,1)} %up_ref.3) | copy-start | bytes 1769476
  46.2 23.5 %copy-start.3 = (bf16[384,768]{1,0:T(8,128)(2,1)S(1)}, bf16[384,768]{1,0:T(8,128)(2,1)}, u32[]{:S(2)}) copy-start(bf16[384,768]{1,0:T(8,128)(2,1)} %down_ref.3) | copy-start | bytes 1769476
  46.2 23.5 %copy-start.5 = (bf16[1,128,768]{2,1,0:T(8,128)(2,1)S(1)}, bf16[1,128,768]{2,1,0:T(8,128)(2,1)}, u32[]{:S(2)}) copy-start(bf16[1,128,768]{2,1,0:T(8,128)(2,1)} %param.15) | copy-start | bytes 589828
  46.3 23.5 %copy-start.6 = (bf16[1,128,768]{2,1,0:T(8,128)(2,1)S(1)}, bf16[1,128,768]{2,1,0:T(8,128)(2,1)}, u32[]{:S(2)}) copy-start(bf16[1,128,768]{2,1,0:T(8,128)(2,1)} %param.29) | copy-start | bytes 589828

commit v5 on v4

--- a/solution.py
+++ b/solution.py
@@ -905,15 +905,16 @@
             stay.start()
 
     table_home = tables_ref.at[c, b, z]
+    mix_home = mixs_ref.at[c, b, z]
     table_sends = [
         wires.send(table_ref, table_home, at.along_chips(k)[1]) for k in range(1, at.chips)
     ]
-    kept = wires.local(table_ref, table_home)
+    kept = [wires.local(table_ref, table_home), wires.local(mix_ref, mix_home)]
     line = LineGather(at, xs_ref, lambda j: 2 * j + c, (line_send, line_recv), own=x_ref)
     line.start()
     last = [wires.send(vec_ref, vecs_ref.at[s], at.along_seq(k)[1]) for k in range(1, at.tokens)]
-    last += [
-        wires.send(mix_ref, mixs_ref.at[z], at.along_chips(k)[1]) for k in range(1, at.chips)
+    mix_sends = [
+        wires.send(mix_ref, mix_home, at.along_chips(k)[1]) for k in range(1, at.chips)
     ]
     last += [
         wires.send(x_ref, xs_ref.at[s], at.partner()),
@@ -922,7 +923,6 @@
     ]
     own = [
         wires.local(x_ref, xs_ref.at[s]),
-        wires.local(mix_ref, mixs_ref.at[z]),
         wires.local(vec_ref, vecs_ref.at[s]),
     ]
 
@@ -941,7 +941,8 @@
     last.append(wires.send(mine, mine, at.partner()))
     for copy in table_sends:
         copy.wait_recv()
-    kept.wait()
+    for copy in kept:
+        copy.wait()
     mine = tables_ref.at[c, b]
     row_sends = [wires.send(mine, mine, at.along_rows(k)[1]) for k in range(1, at.batches)]
     last.append(wires.send(mine, mine, at.partner()))
@@ -952,8 +953,13 @@
         home = xs_ref.at[2 * j + c]
         last.append(wires.send(home, home, at.partner()))
 
-    for j in order[:2]:
-        arrived(j)
+    arrived(order[0])
+    for copy in mix_sends:
+        copy.wait_recv()
+    mine = mixs_ref.at[c, b]
+    mix_rows = [wires.send(mine, mine, at.along_rows(k)[1]) for k in range(1, at.batches)]
+    last.append(wires.send(mine, mine, at.partner()))
+    arrived(order[1])
     for k in range(1, at.batches):
         qkv_sends[k - 1].wait_recv()
         home = qkvs_ref.at[2 * at.from_rows(k) + c]
@@ -964,6 +970,10 @@
         last.append(wires.send(home, home, at.partner()))
     for j in order[2:]:
         arrived(j)
+    for k in range(1, at.batches):
+        mix_rows[k - 1].wait_recv()
+        home = mixs_ref.at[c, at.from_rows(k)]
+        last.append(wires.send(home, home, at.partner()))
     for copy in last:
         copy.wait_recv()
     for copy in own:
@@ -983,13 +993,13 @@
     outs = (
         like(x, tokens),
         like(w_query, tokens, 3),
-        like(w_mix, chips),
+        like(w_mix, 2, batches, chips),
         like(rel_table, 2, batches, chips),
         like(vec, tokens),
         like(up),
         like(down),
     )
-    sends = 3 + 2 * (chips - 1) + tokens - 1 + 3 + 4 * (batches - 1) + 2 + chips - 1
+    sends = 3 + 2 * (chips - 1) + tokens - 1 + 3 + 6 * (batches - 1) + 3 + chips - 1
     inputs = (x, w_query, w_key, w_value, w_mix, rel_table, vec, up, down)
     return comm_call(
         gather_kernel,
@@ -1024,18 +1034,15 @@
         work(j)
         reduce.send_last(j)
 
-    gather.arrive(order[0])
-    gather.arrive(order[1])
-    finish(order[0])
-    gather.arrive(order[2])
-    finish(order[1])
-    finish(order[2])
+    for j in order:
+        gather.arrive(j)
+        finish(j)
 
 
 def feed_kernel(
     ctx_ref, x_ref, mixs_ref, vecs_ref, up_ref, down_ref, up2_ref, down2_ref, out_grad_ref,
     output_ref, pre_grad_ref, sums_ref, attn_ref, mix_ref, ups_ref, downs_ref, upbs_ref,
-    got_ref, mixall_ref, hid_ref, act_ref, slope_ref, part_ref, ffn_ref, grad_ref, inner_ref,
+    got_ref, hid_ref, act_ref, slope_ref, part_ref, ffn_ref, grad_ref, inner_ref,
     back_ref, backs_ref, up_away_ref, down_away_ref, upb_away_ref,
     up_got_ref, down_got_ref, upb_got_ref, upg_ref, downg_ref, upb_ref, vec_ref,
     hid_send, hid_recv, ffn_send, ffn_recv, grad_send, grad_recv, back_send, back_recv,
@@ -1053,12 +1060,6 @@
         part, peer = at.along_seq(k)
         swaps.append(wires.send(ctx_ref.at[part], got_ref.at[s], peer))
     kept = wires.local(ctx_ref.at[s], got_ref.at[s])
-    mix_sends = [
-        wires.send(mixs_ref, mixall_ref.at[c, b], at.along_rows(k)[1])
-        for k in range(1, at.batches)
-    ]
-    mix_lasts = [wires.send(mixs_ref, mixall_ref.at[c, b], at.partner())]
-    mix_kept = wires.local(mixs_ref, mixall_ref.at[c, b])
     lanes = x_ref.shape[1] // at.tokens
     hidden_here = up_ref.shape[1]
     vec_ref[...] = jnp.concatenate(
@@ -1075,17 +1076,10 @@
         + [vecs_ref[partner, 10 + i : 11 + i].astype(wide) for i in range(up_rows)],
         axis=1,
     )
-    for k in range(1, at.batches):
-        mix_sends[k - 1].wait_recv()
-        home = mixall_ref.at[c, at.from_rows(k)]
-        mix_lasts.append(wires.send(home, home, at.partner()))
-    for copy in mix_lasts:
-        copy.wait_recv()
-    mix_kept.wait()
-    shard_rows = mixs_ref.shape[1]
+    shard_rows = mixs_ref.shape[3]
     for part in range(at.tokens):
         mix_ref[part * shard_rows : (part + 1) * shard_rows] = jnp.concatenate(
-            [mixall_ref[part % 2, row, part // 2] for row in range(at.batches)], axis=1
+            [mixs_ref[part % 2, row, part // 2] for row in range(at.batches)], axis=1
         )
     for copy in swaps:
         copy.wait_recv()
@@ -1161,11 +1155,10 @@
     hid_all = hid_ref[...].reshape(at.chips * BLOCK, width)
     grad_all = grad_ref[...].reshape(at.chips * BLOCK, width)
     near, away = slice(0, hidden_here), slice(hidden_here, 2 * hidden_here)
-    up_away_ref[...] = dot_tn(hid_all, inner_all[:, away]).astype(low)
-    down_grad = dot_tn(act_all, grad_all)
-    for row in range(at.batches):
-        piece = slice(row * columns, (row + 1) * columns)
-        down_away_ref[row] = down_grad[away, piece].astype(low)
+    up_grad = dot_tn(hid_all, inner_all)
+    up_away_ref[...] = up_grad[:, away].astype(low)
+    down_grad = dot_tn(grad_all, act_all)
+    down_away_ref[...] = down_grad[:, away].astype(low)
     upb_grad = jnp.sum(inner_all.astype(wide), axis=0, keepdims=True)
     upb_away_ref[...] = jnp.broadcast_to(upb_grad[:, away], upb_away_ref.shape)
     halves = [
@@ -1174,15 +1167,14 @@
         wires.send(upb_away_ref, upb_got_ref, at.partner()),
     ]
     back_line.pass_on(returns)
-    up_own = dot_tn(hid_all, inner_all[:, near])
     for copy in halves:
         copy.wait_recv()
     upb_ref[...] = jnp.broadcast_to(upb_grad[:, near], upb_ref.shape) + upb_got_ref[...]
-    up_sum = (up_own + up_got_ref[...].astype(wide)).astype(low)
+    up_sum = (up_grad[:, near] + up_got_ref[...].astype(wide)).astype(low)
+    down_sum = (down_grad[:, near] + down_got_ref[...].astype(wide)).astype(low)
     for row in range(at.batches):
         upg_ref[row] = up_sum[row * columns : (row + 1) * columns]
-        piece = slice(row * columns, (row + 1) * columns)
-        downg_ref[row] = (down_grad[near, piece] + down_got_ref[row].astype(wide)).astype(low)
+        downg_ref[row] = down_sum[row * columns : (row + 1) * columns]
     for k in range(1, at.batches):
         row, peer = at.along_rows(k)
         last.append(wires.send(upg_ref.at[row], ups_ref.at[b], peer))
@@ -1239,17 +1231,16 @@
         jax.ShapeDtypeStruct((tokens,) + x.shape, low),
         jax.ShapeDtypeStruct((width, width), low),
         jax.ShapeDtypeStruct((batches, columns, hidden_here), low),
-        jax.ShapeDtypeStruct((batches, hidden_here, columns), low),
+        jax.ShapeDtypeStruct((batches, columns, hidden_here), low),
         jax.ShapeDtypeStruct((batches, 8, hidden_here), wide),
     )
     block = (chips,) + x.shape
     wide_block = (chips, x.shape[0], 2 * hidden_here)
     slots = (chips + 1,) + x.shape
     up_half, bias_half = (width, hidden_here), (8, hidden_here)
-    down_half = (batches, hidden_here, columns)
+    down_half = up_half
     scratch = [
         pltpu.VMEM(ctx.shape, low),
-        pltpu.VMEM((2, batches) + mixs.shape, low),
         pltpu.VMEM(block, low),
         pltpu.VMEM(wide_block, low),
         pltpu.VMEM(wide_block, wide),
@@ -1266,7 +1257,7 @@
         pltpu.VMEM(down_half, low),
         pltpu.VMEM(bias_half, wide),
         pltpu.VMEM((batches, columns, hidden_here), low),
-        pltpu.VMEM((batches, hidden_here, columns), low),
+        pltpu.VMEM((batches, columns, hidden_here), low),
         pltpu.VMEM(bias_half, wide),
         pltpu.VMEM((16, width), wide),
     ]
@@ -1487,8 +1478,8 @@
 
 def finish_kernel(
     pre_ref, ins_ref, vecs_ref, cols_ref, dws_ref, tabs_ref, mixs_ref, ups_ref, downs_ref,
-    upbs_ref,
-    input_ref, dq_ref, dk_ref, dv_ref, mix_ref, table_ref, bias_ref, gain_ref, shift_ref,
+    upbs_ref, last_ref,
+    output_ref, input_ref, dq_ref, dk_ref, dv_ref, mix_ref, table_ref, bias_ref, gain_ref, shift_ref,
     up_ref, upb_ref, down_ref, downb_ref,
 ):
     at = Place()
@@ -1500,6 +1491,7 @@
             out = out + ref[k].astype(wide)
         return out
 
+    output_ref[...] = last_ref[...]
     input_ref[...] = pre_ref[...] + total(ins_ref)
     up_ref[...] = total(ups_ref)
     down_ref[...] = total(downs_ref)
@@ -1539,9 +1531,10 @@
     inputs = (pre_grad,) + tuple(parts)
     return pl.pallas_call(
         finish_kernel,
-        out_shape=tuple(jax.ShapeDtypeStruct(shape, jnp.float32) for shape in shapes),
+        out_shape=(like(parts[-1]),)
+        + tuple(jax.ShapeDtypeStruct(shape, jnp.float32) for shape in shapes),
         in_specs=[VMEM_SPEC] * len(inputs),
-        out_specs=(VMEM_SPEC,) * len(shapes),
+        out_specs=(VMEM_SPEC,) * (len(shapes) + 1),
         compiler_params=pltpu.CompilerParams(vmem_limit_bytes=COMM_VMEM),
         name="finish",
     )(*inputs)
@@ -1578,8 +1571,9 @@
         [pack, segment_ids.astype(low), up_bias.reshape(hidden_here // BLOCK, BLOCK)], axis=0
     )
     pack = jnp.pad(pack, ((0, 16 - pack.shape[0]), (0, 0)))
+    weights = (w_query, w_key, w_value, w_mix, rel_table, pack, w_up, w_down)
     xs, qkvs, mixs, tables, vecs, up2, down2 = gather_inputs(
-        x, w_query, w_key, w_value, w_mix, rel_table, pack, w_up, w_down
+        *[pltpu.with_memory_space_constraint(a, pltpu.HBM) for a in (x,) + weights]
     )
     q, k, v, qrev, krev, probs, ctx, w_cat, table = attend(xs, qkvs, tables, vecs)
     output, pre_grad, sums, attn_all, m_mix, ups, downs, upbs = feed_forward(
@@ -1593,17 +1587,18 @@
     shapes = (
         x.shape, shard, shard, shard, shard, rel_table.shape, (4, lanes), (2, lanes), (2, lanes),
         (width // lax.axis_size("batch"), hidden_here), (1, hidden_here),
-        (hidden_here, width // lax.axis_size("batch")), (1, lanes),
+        (width // lax.axis_size("batch"), hidden_here), (1, lanes),
     )
     grads = finish(
         pre_grad,
-        (ins, vec_all, cols_all, dw_all, tab_all, mix_all, ups, downs, upbs),
+        (ins, vec_all, cols_all, dw_all, tab_all, mix_all, ups, downs, upbs, output),
         shapes,
     )
-    input_grad, dq, dk, dv, dmix, dtable, dbias, dgain, dshift, dup, dupb, ddown, ddownb = grads
+    output, input_grad, dq, dk, dv, dmix, dtable = grads[:7]
+    dbias, dgain, dshift, dup, dupb, ddown, ddownb = grads[7:]
     return (
         output[None], input_grad[None], dq, dk, dv, dmix, dtable, dbias, dgain, dshift,
-        dup, dupb[0], ddown, ddownb[0],
+        dup, dupb.reshape(hidden_here), ddown.T, ddownb.reshape(lanes),
     )
 
 

time: 237 us -> 222 us (0.937)
  local copies, waits for them, and re-layouts: 8.57 us -> 0.03 us
  Pallas kernels: 225 us -> 218 us
    pallas_call x1, Pallas kernels: 97 us -> 85.1 us  [feed_forward(): pl.pallas_call(feed_kernel, out_shape=outs, in_specs=[VMEM_SPEC] * len(in...]
    unnamed x26 -> x8, local copies, waits for them, and re-layouts: 8.57 us -> 0.03 us
    pallas_call x2, Pallas kernels: 77.8 us -> 82.3 us  [comm_call(): pl.pallas_call(kernel, out_shape=tuple(out_shapes), in_specs=[spec] * len...]
where the time goes in v5:
time: 222 us
  Pallas kernels  218 us (98%)
  other arithmetic  3.28 us (1%)
    pallas_call x1, Pallas kernels, feed_forward(): pl.pallas_call(feed_kernel, out_shape=outs, in_specs=[VMEM_SPEC] * len(in...  85.1 us
    pallas_call x2, Pallas kernels, comm_call(): pl.pallas_call(kernel, out_shape=tuple(out_shapes), in_specs=[spec] * len...  82.3 us
    pallas_call x1, Pallas kernels, attend_back(): pl.pallas_call(attend_back_kernel, out_shape=(jax.ShapeDtypeStruct((full_...  25.3 us
    pallas_call x1, Pallas kernels, attend(): pl.pallas_call(attend_kernel, out_shape=(jax.ShapeDtypeStruct((2, full_le...  23.5 us

profile of v5, /device:TPU:0, one launch (start us, length us, event | category | flops | bytes accessed | tf_op | source)
XLA Modules:
  0.0 221.6 jit_solution(11517069552256393215)
XLA Ops:
  0.6 0.7 convert_element_type.7
  1.3 0.7 fusion.9
  2.0 1.3 fusion.11.vec_ref
  3.3 42.5 %gather_inputs.1 = (bf16[8,128,768]{2,1,0:T(8,128)(2,1)S(1)}, bf16[8,3,96,192]{3,2,1,0:T(8,128)(2,1)S(1)}, bf16[2,4,4,96,192]{4,3,2,1,0:T(8,128)(2,1)S(1)}, bf16...) custom-call(bf16[128,768]{1,0:T(8,128)(2,1)} %bitcast.8, ...), custom_call_target="tpu_custom_call" | custom-call | tf_op jit(solution)/shard_map/gather_inputs/pallas_call | solution.py:655
  45.8 0.0 copy-start
  45.9 0.0 copy-start.1
  45.9 0.0 copy-start.2
  45.9 0.0 copy-start.3
  45.9 23.5 %attend.1 = (bf16[2,1024,64]{2,1,0:T(8,128)(2,1)S(1)}, bf16[2,1024,64]{2,1,0:T(8,128)(2,1)S(1)}, bf16[2,1024,64]{2,1,0:T(8,128)(2,1)S(1)}, bf16[2,512,64]{2,1,0:...) custom-call(bf16[8,128,768]{2,1,0:T(8,128)(2,1)S(1)} %get-tuple-elem, ...), custom_call_target="tpu_custom_call" | custom-call | tf_op jit(solution)/shard_map/attend/pallas_call | solution.py:348
  69.4 0.0 copy-done
  69.4 0.0 copy-done.1
  69.4 0.0 copy-done.2
  69.4 0.0 copy-done.3
  69.4 85.1 %feed_forward.1 = (bf16[128,768]{1,0:T(8,128)(2,1)S(1)}, f32[128,768]{1,0:T(8,128)S(1)}, f32[8,8,128]{2,1,0:T(8,128)S(1)}, bf16[8,128,768]{2,1,0:T(8,128)(2,1)S(...) custom-call(bf16[8,128,128]{2,1,0:T(8,128)(2,1)S(1)} %get-tuple-elem, ...), custom_call_target="tpu_custom_call" | custom-call | tf_op jit(solution)/shard_map/feed_forward/pallas_call | solution.py:1267
  154.5 25.3 %attend_back.1 = (bf16[1024,384]{1,0:T(8,128)(2,1)S(1)}, bf16[512,256]{1,0:T(8,128)(2,1)S(1)}, f32[8,384]{1,0:T(8,128)S(1)}) custom-call(bf16[2,1024,64]{2,1,0:T(8,128)(2,1)S(1)} %get-tuple-element.71.q_ref, bf16[2,1024,64]{2,1,0:T(8,128)(2,1)S(1)} %get-tuple-element.72.k_ref, bf16[2,1024,64]{2,1,0:T(8,128)(2,1)S(1)} %get-tuple-element.73.v_ref, ...), custom_call_target="tpu_custom_call" | custom-call | tf_op jit(solution)/shard_map/attend_back/pallas_call | solution.py:518
  179.8 39.8 %settle_grads.1 = (bf16[4,128,768]{2,1,0:T(8,128)(2,1)S(1)}, f32[4,8,128]{2,1,0:T(8,128)S(1)}, f32[8,8,384]{2,1,0:T(8,128)S(1)}, bf16[2,96,384]{2,1,0:T(8,128)(2...) custom-call(f32[8,8,128]{2,1,0:T(8,128)S(1)} %get-tuple-element.70.vec_ref, ...), custom_call_target="tpu_custom_call" | custom-call | tf_op jit(solution)/shard_map/settle_grads/pallas_call | solution.py:655
  219.6 1.4 finish.1
  221.0 0.6 reduce
Async XLA Ops:
  45.8 23.5 %copy-start = (bf16[768,384]{1,0:T(8,128)(2,1)S(1)}, bf16[768,384]{1,0:T(8,128)(2,1)}, u32[]{:S(2)}) copy-start(bf16[768,384]{1,0:T(8,128)(2,1)} %up_ref.3) | copy-start | bytes 1769476
  45.9 23.5 %copy-start.1 = (bf16[384,768]{1,0:T(8,128)(2,1)S(1)}, bf16[384,768]{1,0:T(8,128)(2,1)}, u32[]{:S(2)}) copy-start(bf16[384,768]{1,0:T(8,128)(2,1)} %down_ref.3) | copy-start | bytes 1769476
  45.9 23.5 %copy-start.2 = (bf16[1,128,768]{2,1,0:T(8,128)(2,1)S(1)}, bf16[1,128,768]{2,1,0:T(8,128)(2,1)}, u32[]{:S(2)}) copy-start(bf16[1,128,768]{2,1,0:T(8,128)(2,1)} %param.15) | copy-start | bytes 589828
  45.9 23.5 %copy-start.3 = (bf16[1,128,768]{2,1,0:T(8,128)(2,1)S(1)}, bf16[1,128,768]{2,1,0:T(8,128)(2,1)}, u32[]{:S(2)}) copy-start(bf16[1,128,768]{2,1,0:T(8,128)(2,1)} %param.29) | copy-start | bytes 589828

commit v6 on v5

--- a/solution.py
+++ b/solution.py
@@ -596,6 +596,15 @@
     def cross_row_peers(self):
         return self.row_peers() + self.cross_peers()
 
+    def all_peers(self):
+        peers = []
+        for i in range(self.batches):
+            row = lax.rem(self.row + i, self.batches)
+            for j in range(self.tokens):
+                if i or j:
+                    peers.append((row, lax.rem(self.part + j, self.tokens)))
+        return peers
+
     def seq_peers(self):
         return [self.along_seq(k)[1] for k in range(1, self.tokens)]
 
@@ -690,6 +699,12 @@
         return (abs(j - end) + abs(end - z), j)
 
     lists = [sorted((j for j in chips if j != z), key=lambda j: away(j, z)) for z in chips]
+    return [pick([lists[z][t] for z in chips], at.chip) for t in range(at.chips - 1)]
+
+
+def far_order(at):
+    chips = range(at.chips)
+    lists = [sorted((j for j in chips if j != z), key=lambda j: (-abs(j - z), j)) for z in chips]
     return [pick([lists[z][t] for z in chips], at.chip) for t in range(at.chips - 1)]
 
 
@@ -1280,8 +1295,9 @@
 def settle_kernel(
     vec_ref, col_ref, dcat_ref, rel_ref, w_ref, xs_ref, table_ref, ctx_ref, attn_ref,
     ins_ref, vec_all_ref, cols_ref, dw_all_ref, tab_all_ref, mix_all_ref,
-    in_ref, dw_ref, tab_ref, mix_ref, half_ref, sum_ref, vecs_ref, vec_low_ref, dws_ref, dw_low_ref, tabs_ref, tab_low_ref,
-    mixs_ref, mix_low_ref, *sems,
+    in_ref, dw_ref, tab_ref, mix_ref, half_ref, sum_ref, got_ref, vecs_ref, vec_low_ref,
+    dws_ref, dw_low_ref, rels_ref, rel_low_ref, mixs_ref, mix_low_ref,
+    line_send, line_recv, tab_send, tab_recv, *sems,
 ):
     at = Place()
     wires = Wires(*sems)
@@ -1289,32 +1305,40 @@
     b, s, z, c = at.row, at.part, at.chip, at.core
     off_diagonal = b != z
     same, cross = (z, 2 * b + c), (z, 2 * b + 1 - c)
-    peers = at.seq_peers() + at.cross_row_peers()
-    barrier = pltpu.get_barrier_semaphore()
-    for peer in peers:
-        pl.semaphore_signal(barrier, inc=1, device_id=peer, device_id_type=MESH)
-
-    @pl.when(off_diagonal)
-    def _():
-        pl.semaphore_signal(barrier, inc=1, device_id=same, device_id_type=MESH)
-        pl.semaphore_signal(barrier, inc=1, device_id=cross, device_id_type=MESH)
-
-    pl.semaphore_wait(barrier, len(peers) + 2 * off_diagonal.astype(jnp.int32))
-
-    dw_sends, tab_sends, mix_sends, vec_sends, last, own = [], [], [], [], [], []
+    meet(at.all_peers())
     width = w_ref.shape[0]
     columns = width // at.batches
     full_len = dcat_ref.shape[0]
     group = 2 * DH
+    buckets = table_ref.shape[0]
+    bucket_rows = buckets // at.batches
+
+    dw_sends, mix_sends, vec_sends, rel_sends, last, own = [], [], [], [], [], []
+    for k in range(1, at.batches):
+        row, peer = at.along_rows(k)
+        rows = pl.ds(pl.multiple_of(row * bucket_rows, bucket_rows), bucket_rows)
+        rel_sends.append(wires.send(rel_ref.at[rows], rels_ref.at[k - 1], peer))
 
     def input_part(chip, core):
         start = pl.multiple_of((2 * chip + core) * BLOCK, BLOCK)
         in_ref[chip, core] = dot_nt(dcat_ref[pl.ds(start, BLOCK)], w_ref[...]).astype(low)
 
+    order = far_order(at)
+    places = order + [z]
     halves = []
-    for chip in range(at.chips):
+    for chip in places:
         input_part(chip, 1 - c)
         halves.append(wires.send(in_ref.at[chip, 1 - c], half_ref.at[chip], at.partner()))
+    line = LineReduce(at, sum_ref, got_ref, (line_send, line_recv))
+    line.clear()
+    for i, chip in enumerate(places):
+        input_part(chip, c)
+        halves[i].wait_recv()
+        total = in_ref[chip, c].astype(wide) + half_ref[chip].astype(wide)
+        sum_ref[chip] = total.astype(low)
+        if i < len(order):
+            line.send_last(chip)
+
     for k in range(1, at.tokens):
         part, peer = at.along_seq(k)
         vec_sends.append(wires.send(vec_ref.at[part], vecs_ref.at[k - 1], peer))
@@ -1322,15 +1346,6 @@
     for k in range(1, 2 * at.batches):
         last.append(wires.send(col_ref, cols_ref.at[mine], at.along_plane(k)[2]))
     own.append(wires.local(col_ref, cols_ref.at[mine]))
-
-    for chip in range(at.chips):
-        input_part(chip, c)
-        halves[chip].wait_recv()
-        sum_ref[chip] = (in_ref[chip, c].astype(wide) + half_ref[chip].astype(wide)).astype(low)
-    for k in range(1, at.chips):
-        chip, peer = at.along_chips(k)
-        last.append(wires.send(sum_ref.at[chip], ins_ref.at[z], peer))
-    own.append(wires.local(sum_ref.at[z], ins_ref.at[z]))
 
     whole = xs_ref[...].reshape(full_len, width)
     dw = dot_tn(whole, dcat_ref[...])
@@ -1341,12 +1356,49 @@
     for k in range(1, at.batches):
         row, peer = at.along_rows(k)
         dw_sends.append(wires.send(dw_ref.at[row], dws_ref.at[k - 1], peer))
+    line.pass_on(order)
+
+    rows = pl.ds(pl.multiple_of(b * bucket_rows, bucket_rows), bucket_rows)
+    total = rel_ref[rows].astype(wide)
+    for k in range(1, at.batches):
+        rel_sends[k - 1].wait_recv()
+        total = total + rels_ref[k - 1].astype(wide)
+    rel_low_ref[...] = total.astype(low)
+    table_rows = bucket_rows // 2
     for row in range(at.batches):
-        rows = slice(row * columns, (row + 1) * columns)
-        tab_ref[row] = dot_nt(rel_ref[...], w_ref[rows, : 2 * group]).astype(low)
-    for k in range(1, at.batches):
-        row, peer = at.along_rows(k)
-        tab_sends.append(wires.send(tab_ref.at[row], tabs_ref.at[k - 1], peer))
+        piece = dot_nt(rel_low_ref[...], w_ref[row * columns : (row + 1) * columns, : 2 * group])
+        for core in range(2):
+            tab_ref[core, row] = piece[core * table_rows : (core + 1) * table_rows].astype(low)
+
+    def tab_copy(k, d):
+        row = lax.rem(b + k, at.batches)
+        core = jnp.where(d == 0, c, 1 - c)
+        return pltpu.make_async_remote_copy(
+            src_ref=tab_ref.at[core, row],
+            dst_ref=tab_all_ref.at[s],
+            send_sem=tab_send.at[2 * k + d],
+            recv_sem=tab_recv.at[s],
+            device_id=(row, 2 * b + core),
+            device_id_type=MESH,
+        )
+
+    tab_stay = pltpu.make_async_copy(
+        tab_ref.at[c, b], tab_all_ref.at[s], sems[2].at[wires.used[1]]
+    )
+    wires.used[1] += 1
+    for k in range(at.batches):
+        for d in range(2):
+            if k or d:
+                tab_copy(k, d).start()
+
+    @pl.when(off_diagonal)
+    def _():
+        tab_copy(0, 0).start()
+
+    @pl.when(jnp.logical_not(off_diagonal))
+    def _():
+        tab_stay.start()
+
     mix = dot_tn(
         ctx_ref[...].reshape(full_len, group), attn_ref[...].reshape(full_len, width)
     )
@@ -1355,6 +1407,15 @@
     for k in range(1, at.batches):
         row, peer = at.along_rows(k)
         mix_sends.append(wires.send(mix_ref.at[row], mixs_ref.at[k - 1], peer))
+
+    total = vec_ref[s]
+    for k in range(1, at.tokens):
+        vec_sends[k - 1].wait_recv()
+        total = total + vecs_ref[k - 1]
+    vec_low_ref[...] = total
+    for k in range(1, at.batches):
+        last.append(wires.send(vec_low_ref, vec_all_ref.at[b], at.along_rows(k)[1]))
+    own.append(wires.local(vec_low_ref, vec_all_ref.at[b]))
 
     total = dw_ref[b].astype(wide)
     for k in range(1, at.batches):
@@ -1388,18 +1449,6 @@
 
     last.append(wires.send(dw_low_ref.at[1 - c], dw_all_ref.at[c], cross))
 
-    total = tab_ref[b].astype(wide)
-    for k in range(1, at.batches):
-        tab_sends[k - 1].wait_recv()
-        total = total + tabs_ref[k - 1].astype(wide)
-    table_rows = tab_low_ref.shape[1]
-    for part in range(at.tokens):
-        tab_low_ref[part] = total[part * table_rows : (part + 1) * table_rows].astype(low)
-    for k in range(1, at.tokens):
-        part, peer = at.along_seq(k)
-        last.append(wires.send(tab_low_ref.at[part], tab_all_ref.at[s], peer))
-    own.append(wires.local(tab_low_ref.at[s], tab_all_ref.at[s]))
-
     total = mix_ref[b].astype(wide)
     for k in range(1, at.batches):
         mix_sends[k - 1].wait_recv()
@@ -1408,27 +1457,40 @@
     last.append(wires.send(mix_low_ref, mix_all_ref.at[c], at.partner()))
     own.append(wires.local(mix_low_ref, mix_all_ref.at[c]))
 
-    total = vec_ref[s]
-    for k in range(1, at.tokens):
-        vec_sends[k - 1].wait_recv()
-        total = total + vecs_ref[k - 1]
-    vec_low_ref[...] = total
-    for k in range(1, at.batches):
-        last.append(wires.send(vec_low_ref, vec_all_ref.at[b], at.along_rows(k)[1]))
-    own.append(wires.local(vec_low_ref, vec_all_ref.at[b]))
-
+    ins_ref[...] = sum_ref[z].astype(wide) + line.collect()
     for copy in last:
         copy.wait_recv()
     for copy in own:
         copy.wait()
     wires.finish()
+    line.drain(order)
+    for part in range(at.tokens):
+        landed = pltpu.make_async_remote_copy(
+            src_ref=tab_all_ref.at[part],
+            dst_ref=tab_all_ref.at[part],
+            send_sem=tab_send.at[0],
+            recv_sem=tab_recv.at[part],
+            device_id=at.partner(),
+            device_id_type=MESH,
+        )
+
+        @pl.when(jnp.logical_or(off_diagonal, s != part))
+        def _():
+            landed.wait_recv()
+
+    for k in range(at.batches):
+        for d in range(2):
+            if k or d:
+                tab_copy(k, d).wait_send()
 
     @pl.when(off_diagonal)
     def _():
+        tab_copy(0, 0).wait_send()
         move.wait()
 
     @pl.when(jnp.logical_not(off_diagonal))
     def _():
+        tab_stay.wait()
         stay.wait()
 
 
@@ -1441,37 +1503,36 @@
     buckets = table.shape[0]
     half = (chips, local_len, width)
     dw_pieces = (2, columns // 2, group)
-    tab_pieces = (tokens, buckets // tokens, columns)
     mix_piece = (2 * DH, columns)
-    dw_piece, tab_piece = (columns, group), (buckets, columns)
+    dw_piece, rel_piece = (columns, group), (buckets // batches, rel.shape[1])
     outs = (
-        jax.ShapeDtypeStruct(half, low),
+        jax.ShapeDtypeStruct((local_len, width), wide),
         jax.ShapeDtypeStruct((batches,) + vec.shape[1:], wide),
         like(cols, 2 * batches),
         jax.ShapeDtypeStruct(dw_pieces, low),
-        jax.ShapeDtypeStruct(tab_pieces, low),
+        jax.ShapeDtypeStruct((tokens, buckets // tokens, columns), low),
         jax.ShapeDtypeStruct((2,) + mix_piece, low),
     )
-    scratch = (
+    scratch = [
         pltpu.VMEM((chips, 2, local_len, width), low),
         pltpu.VMEM((batches,) + dw_piece, low),
-        pltpu.VMEM((batches,) + tab_piece, low),
+        pltpu.VMEM((2, batches, buckets // tokens, columns), low),
         pltpu.VMEM((batches,) + mix_piece, low),
         pltpu.VMEM(half, low),
         pltpu.VMEM(half, low),
+        pltpu.VMEM((chips + 1, local_len, width), low),
         pltpu.VMEM((tokens - 1,) + vec.shape[1:], wide),
         pltpu.VMEM(vec.shape[1:], wide),
         pltpu.VMEM((batches - 1,) + dw_piece, low),
         pltpu.VMEM(dw_pieces, low),
-        pltpu.VMEM((batches - 1,) + tab_piece, low),
-        pltpu.VMEM(tab_pieces, low),
+        pltpu.VMEM((batches - 1,) + rel_piece, low),
+        pltpu.VMEM(rel_piece, low),
         pltpu.VMEM((batches - 1,) + mix_piece, low),
         pltpu.VMEM(mix_piece, low),
-    )
-    sends = (
-        3 * (batches - 1) + chips + tokens - 1 + 2 * batches - 1
-        + 2 + chips - 1 + tokens - 1 + 1 + batches - 1
-    )
+    ]
+    scratch += reduce_sems(chips)
+    scratch += [pltpu.SemaphoreType.DMA((2 * batches,)), pltpu.SemaphoreType.DMA((tokens,))]
+    sends = 4 * (batches - 1) + chips + tokens - 1 + 2 * batches - 1 + 3
     inputs = (vec, cols, dcat, rel, w_cat, xs, table, ctx, attn_all)
     return comm_call(settle_kernel, "settle_grads", ident, outs, inputs, sends, 6, scratch=scratch)
 
@@ -1492,7 +1553,7 @@
         return out
 
     output_ref[...] = last_ref[...]
-    input_ref[...] = pre_ref[...] + total(ins_ref)
+    input_ref[...] = pre_ref[...] + ins_ref[...]
     up_ref[...] = total(ups_ref)
     down_ref[...] = total(downs_ref)
     upb_ref[...] = total(upbs_ref)[0:1]

time: 222 us -> 228 us (1.027)
  Pallas kernels: 218 us -> 223 us
    pallas_call x2, Pallas kernels: 82.3 us -> 87.8 us  [comm_call(): pl.pallas_call(kernel, out_shape=tuple(out_shapes), in_specs=[spec] * len...]
where the time goes in v6:
time: 228 us; the launch traced here: 227 us
  Pallas kernels  223 us (98%)
  other arithmetic  3.28 us (1%)
    pallas_call x2, Pallas kernels, comm_call(): pl.pallas_call(kernel, out_shape=tuple(out_shapes), in_specs=[spec] * len...  87.8 us
    pallas_call x1, Pallas kernels, feed_forward(): pl.pallas_call(feed_kernel, out_shape=outs, in_specs=[VMEM_SPEC] * len(in...  85.1 us
    pallas_call x1, Pallas kernels, attend_back(): pl.pallas_call(attend_back_kernel, out_shape=(jax.ShapeDtypeStruct((full_...  25.3 us
    pallas_call x1, Pallas kernels, attend(): pl.pallas_call(attend_kernel, out_shape=(jax.ShapeDtypeStruct((2, full_le...  23.5 us

profile of v6, /device:TPU:0, one launch (start us, length us, event | category | flops | bytes accessed | tf_op | source)
XLA Modules:
  0.0 227.0 jit_solution(6322715119462287566)
XLA Ops:
  0.6 0.7 convert_element_type.7
  1.3 0.7 fusion.9
  2.0 1.3 fusion.11.vec_ref
  3.3 42.5 %gather_inputs.1 = (bf16[8,128,768]{2,1,0:T(8,128)(2,1)S(1)}, bf16[8,3,96,192]{3,2,1,0:T(8,128)(2,1)S(1)}, bf16[2,4,4,96,192]{4,3,2,1,0:T(8,128)(2,1)S(1)}, bf16...) custom-call(bf16[128,768]{1,0:T(8,128)(2,1)} %bitcast.8, ...), custom_call_target="tpu_custom_call" | custom-call | tf_op jit(solution)/shard_map/gather_inputs/pallas_call | solution.py:664
  45.8 0.0 copy-start
  45.9 0.0 copy-start.1
  45.9 0.0 copy-start.2
  45.9 0.0 copy-start.3
  45.9 23.5 %attend.1 = (bf16[2,1024,64]{2,1,0:T(8,128)(2,1)S(1)}, bf16[2,1024,64]{2,1,0:T(8,128)(2,1)S(1)}, bf16[2,1024,64]{2,1,0:T(8,128)(2,1)S(1)}, bf16[2,512,64]{2,1,0:...) custom-call(bf16[8,128,768]{2,1,0:T(8,128)(2,1)S(1)} %get-tuple-elem, ...), custom_call_target="tpu_custom_call" | custom-call | tf_op jit(solution)/shard_map/attend/pallas_call | solution.py:348
  69.4 0.0 copy-done
  69.4 0.0 copy-done.1
  69.4 0.0 copy-done.2
  69.4 0.0 copy-done.3
  69.4 85.1 %feed_forward.1 = (bf16[128,768]{1,0:T(8,128)(2,1)S(1)}, f32[128,768]{1,0:T(8,128)S(1)}, f32[8,8,128]{2,1,0:T(8,128)S(1)}, bf16[8,128,768]{2,1,0:T(8,128)(2,1)S(...) custom-call(bf16[8,128,128]{2,1,0:T(8,128)(2,1)S(1)} %get-tuple-elem, ...), custom_call_target="tpu_custom_call" | custom-call | tf_op jit(solution)/shard_map/feed_forward/pallas_call | solution.py:1282
  154.5 25.3 %attend_back.1 = (bf16[1024,384]{1,0:T(8,128)(2,1)S(1)}, bf16[512,256]{1,0:T(8,128)(2,1)S(1)}, f32[8,384]{1,0:T(8,128)S(1)}) custom-call(bf16[2,1024,64]{2,1,0:T(8,128)(2,1)S(1)} %get-tuple-element.71.q_ref, bf16[2,1024,64]{2,1,0:T(8,128)(2,1)S(1)} %get-tuple-element.72.k_ref, bf16[2,1024,64]{2,1,0:T(8,128)(2,1)S(1)} %get-tuple-element.73.v_ref, ...), custom_call_target="tpu_custom_call" | custom-call | tf_op jit(solution)/shard_map/attend_back/pallas_call | solution.py:518
  179.8 45.3 %settle_grads.1 = (f32[128,768]{1,0:T(8,128)S(1)}, f32[4,8,128]{2,1,0:T(8,128)S(1)}, f32[8,8,384]{2,1,0:T(8,128)S(1)}, bf16[2,96,384]{2,1,0:T(8,128)(2,1)S(1)}, ...) custom-call(f32[8,8,128]{2,1,0:T(8,128)S(1)} %get-tuple-element.70.vec_ref, ...), custom_call_target="tpu_custom_call" | custom-call | tf_op jit(solution)/shard_map/settle_grads/pallas_call | solution.py:664
  225.1 1.3 finish.1
  226.4 0.6 reduce
Async XLA Ops:
  45.8 23.5 %copy-start = (bf16[768,384]{1,0:T(8,128)(2,1)S(1)}, bf16[768,384]{1,0:T(8,128)(2,1)}, u32[]{:S(2)}) copy-start(bf16[768,384]{1,0:T(8,128)(2,1)} %up_ref.3) | copy-start | bytes 1769476
  45.9 23.5 %copy-start.1 = (bf16[384,768]{1,0:T(8,128)(2,1)S(1)}, bf16[384,768]{1,0:T(8,128)(2,1)}, u32[]{:S(2)}) copy-start(bf16[384,768]{1,0:T(8,128)(2,1)} %down_ref.3) | copy-start | bytes 1769476
  45.9 23.5 %copy-start.2 = (bf16[1,128,768]{2,1,0:T(8,128)(2,1)S(1)}, bf16[1,128,768]{2,1,0:T(8,128)(2,1)}, u32[]{:S(2)}) copy-start(bf16[1,128,768]{2,1,0:T(8,128)(2,1)} %param.15) | copy-start | bytes 589828
  45.9 23.5 %copy-start.3 = (bf16[1,128,768]{2,1,0:T(8,128)(2,1)S(1)}, bf16[1,128,768]{2,1,0:T(8,128)(2,1)}, u32[]{:S(2)}) copy-start(bf16[1,128,768]{2,1,0:T(8,128)(2,1)} %param.29) | copy-start | bytes 589828

commit v7 on v6

--- a/solution.py
+++ b/solution.py
@@ -167,7 +167,7 @@
 MIB = 1024 * 1024
 ATTEND_VMEM = 26 * MIB
 BACK_VMEM = 26 * MIB
-FEED_VMEM = 26 * MIB
+FEED_VMEM = 40 * MIB
 COMM_VMEM = 16 * MIB
 
 
@@ -233,6 +233,8 @@
     wide_ref,
     ends_ref,
     held_ref,
+    ready,
+    leave,
 ):
     at = Place()
     full_len = xs_ref.shape[0] * xs_ref.shape[1]
@@ -299,11 +301,17 @@
         lax.fori_loop(0, blocks, key_block, 0)
 
     first = at.core * (blocks // 2)
+    ready()
 
     def unit(u, carry):
         g = u + first
         slot = g // blocks
         qb = g % blocks
+
+        @pl.when(u > 0)
+        def _():
+            leave(u - 1)
+
         start = pl.multiple_of(qb * BLOCK, BLOCK)
         rows = q_ref[slot, pl.ds(start, BLOCK)]
         own = dot_nt(rows, krev_ref[slot])
@@ -334,42 +342,7 @@
     for part in range(at.tokens):
         rows = slice(part * BLOCK, (part + 1) * BLOCK)
         ctx_ref[part] = jnp.concatenate([held_ref[0, rows], held_ref[1, rows]], axis=1)
-
-
-def attend(xs, qkvs, tables, vecs):
-    tokens, local_len, width = xs.shape
-    full_len = tokens * local_len
-    buckets = tokens * tables.shape[3]
-    blocks = full_len // BLOCK
-    units = 3 * blocks // 2
-    band_width = buckets + BLOCK
-    low, wide = jnp.bfloat16, jnp.float32
-    pad_blocks = blocks + band_width // BLOCK - 1
-    return pl.pallas_call(
-        attend_kernel,
-        out_shape=(
-            jax.ShapeDtypeStruct((2, full_len, DH), low),
-            jax.ShapeDtypeStruct((2, full_len, DH), low),
-            jax.ShapeDtypeStruct((2, full_len, DH), low),
-            jax.ShapeDtypeStruct((2, buckets, DH), low),
-            jax.ShapeDtypeStruct((2, buckets, DH), low),
-            jax.ShapeDtypeStruct((units, BLOCK, full_len), low),
-            jax.ShapeDtypeStruct((tokens, local_len, 2 * DH), low),
-            jax.ShapeDtypeStruct((width, 6 * DH), low),
-            jax.ShapeDtypeStruct((buckets, width), low),
-        ),
-        in_specs=[pl.BlockSpec(memory_space=pltpu.VMEM)] * 4,
-        out_specs=[pl.BlockSpec(memory_space=pltpu.VMEM)] * 9,
-        scratch_shapes=[
-            pltpu.VMEM((full_len, BLOCK), wide),
-            pltpu.VMEM((2, pad_blocks, BLOCK, band_width), wide),
-            pltpu.VMEM((BLOCK, full_len + buckets), wide),
-            pltpu.VMEM((2, 2, 16, full_len), wide),
-            pltpu.VMEM((2, full_len, DH), low),
-        ],
-        compiler_params=pltpu.CompilerParams(vmem_limit_bytes=ATTEND_VMEM),
-        name="attend",
-    )(xs, qkvs, tables, vecs)
+    leave(units - 1)
 
 
 def attend_back_kernel(
@@ -1055,26 +1028,62 @@
 
 
 def feed_kernel(
-    ctx_ref, x_ref, mixs_ref, vecs_ref, up_ref, down_ref, up2_ref, down2_ref, out_grad_ref,
+    xs_ref, qkvs_ref, tables_ref, x_ref, mixs_ref, vecs_ref, up_ref, down_ref, up2_ref,
+    down2_ref, out_grad_ref,
+    q_ref, k_ref, v_ref, qrev_ref, krev_ref, p_ref, ctx_ref, w_ref, table_ref,
     output_ref, pre_grad_ref, sums_ref, attn_ref, mix_ref, ups_ref, downs_ref, upbs_ref,
+    segc_ref, place_ref, wide_ref, ends_ref, held_ref,
     got_ref, hid_ref, act_ref, slope_ref, part_ref, ffn_ref, grad_ref, inner_ref,
     back_ref, backs_ref, up_away_ref, down_away_ref, upb_away_ref,
     up_got_ref, down_got_ref, upb_got_ref, upg_ref, downg_ref, upb_ref, vec_ref,
     hid_send, hid_recv, ffn_send, ffn_recv, grad_send, grad_recv, back_send, back_recv,
-    attn_send, attn_recv, *sems,
+    attn_send, attn_recv, ctx_send, ctx_recv, *sems,
 ):
     at = Place()
     wires = Wires(*sems)
     low, wide = jnp.bfloat16, jnp.float32
     b, s, z, c = at.row, at.part, at.chip, at.core
     order, returns = arrival_order(at), return_order(at)
-    meet(at.seq_peers() + at.row_peers())
+    peers = at.seq_peers() + at.row_peers()
+    barrier = pltpu.get_barrier_semaphore()
+    for peer in peers:
+        pl.semaphore_signal(barrier, inc=1, device_id=peer, device_id_type=MESH)
     last, own = [], []
-    swaps = []
-    for k in range(1, at.tokens):
-        part, peer = at.along_seq(k)
-        swaps.append(wires.send(ctx_ref.at[part], got_ref.at[s], peer))
-    kept = wires.local(ctx_ref.at[s], got_ref.at[s])
+    blocks = at.tokens
+    units = p_ref.shape[0]
+
+    def context_copy(u):
+        g = u + c * (blocks // 2)
+        slot, qb = g // blocks, g % blocks
+        rows = pl.ds(pl.multiple_of(qb * BLOCK, BLOCK), BLOCK)
+        head = 3 * z + c + slot
+        src, dst = held_ref.at[slot, rows], got_ref.at[head]
+        remote = pltpu.make_async_remote_copy(
+            src_ref=src,
+            dst_ref=dst,
+            send_sem=ctx_send.at[u],
+            recv_sem=ctx_recv.at[head],
+            device_id=(b, qb),
+            device_id_type=MESH,
+        )
+        return qb != s, remote, pltpu.make_async_copy(src, dst, ctx_recv.at[head])
+
+    def leave(u):
+        away, remote, here = context_copy(u)
+
+        @pl.when(away)
+        def _():
+            remote.start()
+
+        @pl.when(jnp.logical_not(away))
+        def _():
+            here.start()
+
+    attend_kernel(
+        xs_ref, qkvs_ref, tables_ref, vecs_ref, q_ref, k_ref, v_ref, qrev_ref, krev_ref, p_ref,
+        ctx_ref, w_ref, table_ref, segc_ref, place_ref, wide_ref, ends_ref, held_ref,
+        lambda: pl.semaphore_wait(barrier, len(peers)), leave,
+    )
     lanes = x_ref.shape[1] // at.tokens
     hidden_here = up_ref.shape[1]
     vec_ref[...] = jnp.concatenate(
@@ -1096,14 +1105,9 @@
         mix_ref[part * shard_rows : (part + 1) * shard_rows] = jnp.concatenate(
             [mixs_ref[part % 2, row, part // 2] for row in range(at.batches)], axis=1
         )
-    for copy in swaps:
-        copy.wait_recv()
-    kept.wait()
-    pieces = []
-    for chip in range(at.chips):
-        left, right = got_ref[2 * chip], got_ref[2 * chip + 1]
-        middle = left[:, DH:].astype(wide) + right[:, :DH].astype(wide)
-        pieces += [left[:, :DH], middle.astype(low), right[:, DH:]]
+    for head in range(3 * at.chips):
+        pltpu.make_async_copy(got_ref.at[head], got_ref.at[head], ctx_recv.at[head]).wait()
+    pieces = [got_ref[head] for head in range(3 * at.chips)]
     context = jnp.concatenate(pieces, axis=1)
     pre_norm = x_ref[...].astype(wide) + dot_nn(context, mix_ref[...]) + bias3
     unit1, scale1 = norm_parts(pre_norm)
@@ -1231,15 +1235,41 @@
     for line in (hid_line, ffn_line, grad_line, back_line, attn_line):
         line.drain(order)
 
-
-def feed_forward(ctx, x, mixs, vecs, up, down, up2, down2, out_grad, ident):
+    def left(u, carry):
+        away, remote, _ = context_copy(u)
+
+        @pl.when(away)
+        def _():
+            remote.wait_send()
+
+        return carry
+
+    lax.fori_loop(0, units, left, 0)
+
+
+def feed_forward(xs, qkvs, tables, x, mixs, vecs, up, down, up2, down2, out_grad, ident):
     tokens, batches = lax.axis_size("seq"), lax.axis_size("batch")
     chips = tokens // 2
-    width = x.shape[1]
+    local_len, width = x.shape
+    full_len = tokens * local_len
     columns = width // batches
     hidden_here = up.shape[1]
+    buckets = tokens * tables.shape[3]
+    blocks = full_len // BLOCK
+    units = 3 * blocks // 2
+    band_width = buckets + BLOCK
+    pad_blocks = blocks + band_width // BLOCK - 1
     low, wide = jnp.bfloat16, jnp.float32
     outs = (
+        jax.ShapeDtypeStruct((2, full_len, DH), low),
+        jax.ShapeDtypeStruct((2, full_len, DH), low),
+        jax.ShapeDtypeStruct((2, full_len, DH), low),
+        jax.ShapeDtypeStruct((2, buckets, DH), low),
+        jax.ShapeDtypeStruct((2, buckets, DH), low),
+        jax.ShapeDtypeStruct((units, BLOCK, full_len), low),
+        jax.ShapeDtypeStruct((tokens, local_len, 2 * DH), low),
+        jax.ShapeDtypeStruct((width, 6 * DH), low),
+        jax.ShapeDtypeStruct((buckets, width), low),
         jax.ShapeDtypeStruct(x.shape, low),
         jax.ShapeDtypeStruct(x.shape, wide),
         jax.ShapeDtypeStruct((tokens, 8, BLOCK), wide),
@@ -1255,7 +1285,12 @@
     up_half, bias_half = (width, hidden_here), (8, hidden_here)
     down_half = up_half
     scratch = [
-        pltpu.VMEM(ctx.shape, low),
+        pltpu.VMEM((full_len, BLOCK), wide),
+        pltpu.VMEM((2, pad_blocks, BLOCK, band_width), wide),
+        pltpu.VMEM((BLOCK, full_len + buckets), wide),
+        pltpu.VMEM((2, 2, 16, full_len), wide),
+        pltpu.VMEM((2, full_len, DH), low),
+        pltpu.VMEM((3 * chips, local_len, DH), low),
         pltpu.VMEM(block, low),
         pltpu.VMEM(wide_block, low),
         pltpu.VMEM(wide_block, wide),
@@ -1277,8 +1312,9 @@
         pltpu.VMEM((16, width), wide),
     ]
     scratch += (gather_sems(chips) + reduce_sems(chips)) * 2 + gather_sems(chips)
-    inputs = (ctx, x, mixs, vecs, up, down, up2, down2, out_grad)
-    sends = tokens - 1 + 2 * batches - 1 + 3 + 3 * (batches - 1) + chips
+    scratch += [pltpu.SemaphoreType.DMA((units,)), pltpu.SemaphoreType.DMA((3 * chips,))]
+    inputs = (xs, qkvs, tables, x, mixs, vecs, up, down, up2, down2, out_grad)
+    sends = 3 + 3 * (batches - 1) + chips
     return pl.pallas_call(
         feed_kernel,
         out_shape=outs,
@@ -1319,6 +1355,14 @@
         rows = pl.ds(pl.multiple_of(row * bucket_rows, bucket_rows), bucket_rows)
         rel_sends.append(wires.send(rel_ref.at[rows], rels_ref.at[k - 1], peer))
 
+    for k in range(1, at.tokens):
+        part, peer = at.along_seq(k)
+        vec_sends.append(wires.send(vec_ref.at[part], vecs_ref.at[k - 1], peer))
+    mine = 2 * b + c
+    for k in range(1, 2 * at.batches):
+        last.append(wires.send(col_ref, cols_ref.at[mine], at.along_plane(k)[2]))
+    own.append(wires.local(col_ref, cols_ref.at[mine]))
+
     def input_part(chip, core):
         start = pl.multiple_of((2 * chip + core) * BLOCK, BLOCK)
         in_ref[chip, core] = dot_nt(dcat_ref[pl.ds(start, BLOCK)], w_ref[...]).astype(low)
@@ -1339,14 +1383,6 @@
         if i < len(order):
             line.send_last(chip)
 
-    for k in range(1, at.tokens):
-        part, peer = at.along_seq(k)
-        vec_sends.append(wires.send(vec_ref.at[part], vecs_ref.at[k - 1], peer))
-    mine = 2 * b + c
-    for k in range(1, 2 * at.batches):
-        last.append(wires.send(col_ref, cols_ref.at[mine], at.along_plane(k)[2]))
-    own.append(wires.local(col_ref, cols_ref.at[mine]))
-
     whole = xs_ref[...].reshape(full_len, width)
     dw = dot_tn(whole, dcat_ref[...])
     dw_rel = dot_tn(table_ref[...], rel_ref[...])
@@ -1356,7 +1392,6 @@
     for k in range(1, at.batches):
         row, peer = at.along_rows(k)
         dw_sends.append(wires.send(dw_ref.at[row], dws_ref.at[k - 1], peer))
-    line.pass_on(order)
 
     rows = pl.ds(pl.multiple_of(b * bucket_rows, bucket_rows), bucket_rows)
     total = rel_ref[rows].astype(wide)
@@ -1399,6 +1434,7 @@
     def _():
         tab_stay.start()
 
+    line.pass_on(order[:1])
     mix = dot_tn(
         ctx_ref[...].reshape(full_len, group), attn_ref[...].reshape(full_len, width)
     )
@@ -1408,15 +1444,7 @@
         row, peer = at.along_rows(k)
         mix_sends.append(wires.send(mix_ref.at[row], mixs_ref.at[k - 1], peer))
 
-    total = vec_ref[s]
-    for k in range(1, at.tokens):
-        vec_sends[k - 1].wait_recv()
-        total = total + vecs_ref[k - 1]
-    vec_low_ref[...] = total
-    for k in range(1, at.batches):
-        last.append(wires.send(vec_low_ref, vec_all_ref.at[b], at.along_rows(k)[1]))
-    own.append(wires.local(vec_low_ref, vec_all_ref.at[b]))
-
+    line.pass_on(order[1:2])
     total = dw_ref[b].astype(wide)
     for k in range(1, at.batches):
         dw_sends[k - 1].wait_recv()
@@ -1449,6 +1477,7 @@
 
     last.append(wires.send(dw_low_ref.at[1 - c], dw_all_ref.at[c], cross))
 
+    line.pass_on(order[2:])
     total = mix_ref[b].astype(wide)
     for k in range(1, at.batches):
         mix_sends[k - 1].wait_recv()
@@ -1456,6 +1485,15 @@
     mix_low_ref[...] = total.astype(low)
     last.append(wires.send(mix_low_ref, mix_all_ref.at[c], at.partner()))
     own.append(wires.local(mix_low_ref, mix_all_ref.at[c]))
+
+    total = vec_ref[s]
+    for k in range(1, at.tokens):
+        vec_sends[k - 1].wait_recv()
+        total = total + vecs_ref[k - 1]
+    vec_low_ref[...] = total
+    for k in range(1, at.batches):
+        last.append(wires.send(vec_low_ref, vec_all_ref.at[b], at.along_rows(k)[1]))
+    own.append(wires.local(vec_low_ref, vec_all_ref.at[b]))
 
     ins_ref[...] = sum_ref[z].astype(wide) + line.collect()
     for copy in last:
@@ -1636,10 +1674,11 @@
     xs, qkvs, mixs, tables, vecs, up2, down2 = gather_inputs(
         *[pltpu.with_memory_space_constraint(a, pltpu.HBM) for a in (x,) + weights]
     )
-    q, k, v, qrev, krev, probs, ctx, w_cat, table = attend(xs, qkvs, tables, vecs)
-    output, pre_grad, sums, attn_all, m_mix, ups, downs, upbs = feed_forward(
-        ctx, x, mixs, vecs, w_up, w_down, up2, down2, out_grad[0], 1
-    )
+    forward = feed_forward(
+        xs, qkvs, tables, x, mixs, vecs, w_up, w_down, up2, down2, out_grad[0], 1
+    )
+    q, k, v, qrev, krev, probs, ctx, w_cat, table = forward[:9]
+    output, pre_grad, sums, attn_all, m_mix, ups, downs, upbs = forward[9:]
     dcat, rel_grad, cols = attend_back(q, k, v, qrev, krev, probs, m_mix, attn_all)
     ins, vec_all, cols_all, dw_all, tab_all, mix_all = settle_grads(
         sums, cols, dcat, rel_grad, w_cat, xs, table, ctx, attn_all, 2

time: 228 us -> 225 us (0.987)
  Pallas kernels: 223 us -> 216 us
  local copies, waits for them, and re-layouts: 0.03 us -> 4.23 us
    pallas_call x1, Pallas kernels: 85.1 us -> 109 us  [feed_forward(): pl.pallas_call(feed_kernel, out_shape=outs, in_specs=[VMEM_SPEC] * len(in...]
    pallas_call x1 -> x0, Pallas kernels: 23.5 us -> none  [attend(): pl.pallas_call(attend_kernel, out_shape=(jax.ShapeDtypeStruct((2, full_le...]
    pallas_call x2, Pallas kernels: 87.8 us -> 80.2 us  [comm_call(): pl.pallas_call(kernel, out_shape=tuple(out_shapes), in_specs=[spec] * len...]
    unnamed x8 -> x16, local copies, waits for them, and re-layouts: 0.03 us -> 4.23 us
where the time goes in v7:
time: 225 us; the launch traced here: 224 us
  Pallas kernels  216 us (96%)
  local copies, waits for them, and re-layouts  4.23 us (2%)
  other arithmetic  3.39 us (2%)
    pallas_call x1, Pallas kernels, feed_forward(): pl.pallas_call(feed_kernel, out_shape=outs, in_specs=[VMEM_SPEC] * len(in...  109 us
    pallas_call x2, Pallas kernels, comm_call(): pl.pallas_call(kernel, out_shape=tuple(out_shapes), in_specs=[spec] * len...  80.2 us
    pallas_call x1, Pallas kernels, attend_back(): pl.pallas_call(attend_back_kernel, out_shape=(jax.ShapeDtypeStruct((full_...  25.3 us

profile of v7, /device:TPU:0, one launch (start us, length us, event | category | flops | bytes accessed | tf_op | source)
XLA Modules:
  0.0 223.9 jit_solution(16244009438254293105)
XLA Ops:
  0.6 0.0 copy-start.4
  0.7 0.0 copy-start.3
  0.7 0.0 copy-start.7
  0.7 0.0 copy-start.6
  0.7 0.8 convert_element_type.7
  1.5 0.7 fusion.9
  2.2 1.3 fusion.11.vec_ref
  3.5 42.5 %gather_inputs.1 = (bf16[8,128,768]{2,1,0:T(8,128)(2,1)S(1)}, bf16[8,3,96,192]{3,2,1,0:T(8,128)(2,1)S(1)}, bf16[2,4,4,96,192]{4,3,2,1,0:T(8,128)(2,1)S(1)}, bf16...) custom-call(bf16[128,768]{1,0:T(8,128)(2,1)} %bitcast.8, ...), custom_call_target="tpu_custom_call" | custom-call | tf_op jit(solution)/shard_map/gather_inputs/pallas_call | solution.py:637
  46.0 0.0 copy-start
  46.0 1.1 copy-done
  47.2 0.0 copy-start.5
  47.2 1.2 copy-done.5
  48.3 0.0 copy-done.4
  48.3 0.0 copy-done.3
  48.3 0.0 copy-done.7
  48.3 0.0 copy-done.6
  48.3 108.7 %feed_forward.1 = (bf16[2,1024,64]{2,1,0:T(8,128)(2,1)S(1)}, bf16[2,1024,64]{2,1,0:T(8,128)(2,1)S(1)}, bf16[2,1024,64]{2,1,0:T(8,128)(2,1)S(1)}, bf16[2,512,64]{...) custom-call(bf16[8,128,768]{2,1,0:T(8,128)(2,1)} %copy-done, ...), custom_call_target="tpu_custom_call" | custom-call | tf_op jit(solution)/shard_map/feed_forward/pallas_call | solution.py:1318
  157.1 0.0 copy-start.2
  157.1 1.9 copy-done.2
  159.0 0.0 copy-start.1
  159.0 25.3 %attend_back.1 = (bf16[1024,384]{1,0:T(8,128)(2,1)S(1)}, bf16[512,256]{1,0:T(8,128)(2,1)S(1)}, f32[8,384]{1,0:T(8,128)S(1)}) custom-call(bf16[2,1024,64]{2,1,0:T(8,128)(2,1)S(1)} %get-tuple-element.70.q_ref, bf16[2,1024,64]{2,1,0:T(8,128)(2,1)S(1)} %get-tuple-element.71.k_ref, bf16[2,1024,64]{2,1,0:T(8,128)(2,1)S(1)} %get-tuple-element.72.v_ref, ...), custom_call_target="tpu_custom_call" | custom-call | tf_op jit(solution)/shard_map/attend_back/pallas_call | solution.py:491
  184.2 0.0 copy-done.1
  184.3 37.7 %settle_grads.1 = (f32[128,768]{1,0:T(8,128)S(1)}, f32[4,8,128]{2,1,0:T(8,128)S(1)}, f32[8,8,384]{2,1,0:T(8,128)S(1)}, bf16[2,96,384]{2,1,0:T(8,128)(2,1)S(1)}, ...) custom-call(f32[8,8,128]{2,1,0:T(8,128)S(1)} %get-tuple-element.69.vec_ref, ...), custom_call_target="tpu_custom_call" | custom-call | tf_op jit(solution)/shard_map/settle_grads/pallas_call | solution.py:637
  221.9 1.3 finish.1
  223.3 0.6 reduce
Async XLA Ops:
  0.6 47.7 %copy-start.4 = (bf16[384,768]{1,0:T(8,128)(2,1)S(1)}, bf16[384,768]{1,0:T(8,128)(2,1)}, u32[]{:S(2)}) copy-start(bf16[384,768]{1,0:T(8,128)(2,1)} %down_ref.3) | copy-start | bytes 1769476
  0.7 47.7 %copy-start.3 = (bf16[768,384]{1,0:T(8,128)(2,1)S(1)}, bf16[768,384]{1,0:T(8,128)(2,1)}, u32[]{:S(2)}) copy-start(bf16[768,384]{1,0:T(8,128)(2,1)} %up_ref.3) | copy-start | bytes 1769476
  0.7 47.7 %copy-start.7 = (bf16[1,128,768]{2,1,0:T(8,128)(2,1)S(1)}, bf16[1,128,768]{2,1,0:T(8,128)(2,1)}, u32[]{:S(2)}) copy-start(bf16[1,128,768]{2,1,0:T(8,128)(2,1)} %param.29) | copy-start | bytes 589828
  0.7 47.7 %copy-start.6 = (bf16[1,128,768]{2,1,0:T(8,128)(2,1)S(1)}, bf16[1,128,768]{2,1,0:T(8,128)(2,1)}, u32[]{:S(2)}) copy-start(bf16[1,128,768]{2,1,0:T(8,128)(2,1)} %param.15) | copy-start | bytes 589828
  46.0 1.2 copy-start
  47.2 1.2 copy-start.5
  157.1 1.9 copy-start.2
  159.0 25.3 %copy-start.1 = (bf16[8,128,768]{2,1,0:T(8,128)(2,1)S(1)}, bf16[8,128,768]{2,1,0:T(8,128)(2,1)}, u32[]{:S(2)}) copy-start(bf16[8,128,768]{2,1,0:T(8,128)(2,1)} %copy-done) | copy-start | bytes 4718596

commit v8 on v6

--- a/solution.py
+++ b/solution.py
@@ -296,7 +296,7 @@
                 ] = band[:, e * BLOCK : (e + 1) * BLOCK].T
             return carry
 
-        lax.fori_loop(0, blocks, key_block, 0)
+        lax.fori_loop(0, blocks, key_block, 0, unroll=8)
 
     first = at.core * (blocks // 2)
 
@@ -308,7 +308,7 @@
         rows = q_ref[slot, pl.ds(start, BLOCK)]
         own = dot_nt(rows, krev_ref[slot])
         band = skew_band(own) + place_ref[slot, qb + side]
-        wide_ref[:, pl.ds(start, band_width)] = band
+        wide_ref[u % 2, :, pl.ds(start, band_width)] = band
         content = dot_nt(rows, k_ref[slot])
         lane = lax.broadcasted_iota(jnp.int32, (BLOCK, full_len), 1)
         near = jnp.where(
@@ -317,7 +317,7 @@
             jnp.where(
                 lane >= start + band_width - span,
                 own[:, buckets - 1 :] + ends_ref[slot, 0, 0:1],
-                wide_ref[:, span : span + full_len],
+                wide_ref[u % 2, :, span : span + full_len],
             ),
         )
         same = segc_ref[pl.ds(start, BLOCK), 0:1] == seg_row
@@ -330,7 +330,7 @@
         held_ref[slot, pl.ds(start, BLOCK)] = dot_nn(probs, v_ref[slot]).astype(jnp.bfloat16)
         return carry
 
-    lax.fori_loop(0, units, unit, 0)
+    lax.fori_loop(0, units, unit, 0, unroll=4)
     for part in range(at.tokens):
         rows = slice(part * BLOCK, (part + 1) * BLOCK)
         ctx_ref[part] = jnp.concatenate([held_ref[0, rows], held_ref[1, rows]], axis=1)
@@ -363,7 +363,7 @@
         scratch_shapes=[
             pltpu.VMEM((full_len, BLOCK), wide),
             pltpu.VMEM((2, pad_blocks, BLOCK, band_width), wide),
-            pltpu.VMEM((BLOCK, full_len + buckets), wide),
+            pltpu.VMEM((2, BLOCK, full_len + buckets), wide),
             pltpu.VMEM((2, 2, 16, full_len), wide),
             pltpu.VMEM((2, full_len, DH), low),
         ],
@@ -430,8 +430,8 @@
         inner = jnp.sum(wide_probs * prob_grad, axis=-1, keepdims=True)
         low_grad = (wide_probs * (prob_grad - inner)).astype(jnp.bfloat16)
         score_grad = low_grad.astype(jnp.float32)
-        wide_ref[:, span : span + full_len] = dot_nn(turn, low_grad)
-        low_ref[:, span : span + full_len] = low_grad
+        wide_ref[u % 2, :, span : span + full_len] = dot_nn(turn, low_grad)
+        low_ref[u % 2, :, span : span + full_len] = low_grad
         dvt_ref[slot] += dot_tn(grad, probs)
         dkt_ref[slot] += dot_tn(rows, low_grad)
         row = lax.broadcasted_iota(jnp.int32, (BLOCK, full_len), 0)
@@ -444,7 +444,7 @@
         far_right = jnp.sum(jnp.where(gap >= span, score_grad, 0.0), axis=0, keepdims=True)
         far_left = jnp.sum(jnp.where(gap < -span, score_grad, 0.0), axis=0, keepdims=True)
         far_ref[slot] += jnp.where(place8 == 0, far_right, jnp.where(place8 == 1, far_left, 0.0))
-        band = wide_ref[:, pl.ds(start, band_width)]
+        band = wide_ref[u % 2, :, pl.ds(start, band_width)]
         near = dot_nn(turn, skew_back(band, buckets).astype(jnp.bfloat16))
         bucket = lax.broadcasted_iota(jnp.int32, (BLOCK, buckets), 1)
         near = near + jnp.where(
@@ -458,10 +458,10 @@
             keys_at = pl.multiple_of(start + e * BLOCK, BLOCK)
             place_ref[
                 slot, qb + e, :, (band_blocks - 1 - e) * BLOCK : (band_blocks - e) * BLOCK
-            ] = dot_nt(turn, low_ref[:, pl.ds(keys_at, BLOCK)])
+            ] = dot_nt(turn, low_ref[u % 2, :, pl.ds(keys_at, BLOCK)])
         return carry
 
-    lax.fori_loop(0, units, unit, 0)
+    lax.fori_loop(0, units, unit, 0, unroll=4)
     parts_q, parts_k, parts_v = [], [], []
     parts_r = [None] * 4
     for slot in range(2):
@@ -486,7 +486,7 @@
             dq_ref[2 + slot, pl.ds(start, BLOCK)] = dot_nn(far, qrev_ref[slot])
             return carry
 
-        lax.fori_loop(0, blocks, key_side, 0)
+        lax.fori_loop(0, blocks, key_side, 0, unroll=8)
         parts_q.append((dq_ref[slot] * scale).astype(jnp.bfloat16))
         parts_k.append(((dq_ref[2 + slot] + whole_k) * scale).astype(jnp.bfloat16))
         parts_v.append(dvt_ref[slot].T.astype(jnp.bfloat16))
@@ -526,8 +526,8 @@
         out_specs=[pl.BlockSpec(memory_space=pltpu.VMEM)] * 3,
         scratch_shapes=[
             pltpu.VMEM((2, full_len, DH), low),
-            pltpu.VMEM((BLOCK, full_len + buckets), wide),
-            pltpu.VMEM((BLOCK, full_len + buckets), low),
+            pltpu.VMEM((2, BLOCK, full_len + buckets), wide),
+            pltpu.VMEM((2, BLOCK, full_len + buckets), low),
             pltpu.VMEM((2, pad_blocks, BLOCK, band_width), wide),
             pltpu.VMEM((4, full_len, DH), wide),
             pltpu.VMEM((2, DH, full_len), wide),
@@ -544,7 +544,7 @@
 MESH = pl.DeviceIdType.MESH
 VMEM_SPEC = pl.BlockSpec(memory_space=pltpu.VMEM)
 HBM_SPEC = pl.BlockSpec(memory_space=pltpu.HBM)
-CHUNKS = 2
+CHUNKS = 4
 
 
 class Place:
@@ -1319,6 +1319,14 @@
         rows = pl.ds(pl.multiple_of(row * bucket_rows, bucket_rows), bucket_rows)
         rel_sends.append(wires.send(rel_ref.at[rows], rels_ref.at[k - 1], peer))
 
+    for k in range(1, at.tokens):
+        part, peer = at.along_seq(k)
+        vec_sends.append(wires.send(vec_ref.at[part], vecs_ref.at[k - 1], peer))
+    mine = 2 * b + c
+    for k in range(1, 2 * at.batches):
+        last.append(wires.send(col_ref, cols_ref.at[mine], at.along_plane(k)[2]))
+    own.append(wires.local(col_ref, cols_ref.at[mine]))
+
     def input_part(chip, core):
         start = pl.multiple_of((2 * chip + core) * BLOCK, BLOCK)
         in_ref[chip, core] = dot_nt(dcat_ref[pl.ds(start, BLOCK)], w_ref[...]).astype(low)
@@ -1339,14 +1347,6 @@
         if i < len(order):
             line.send_last(chip)
 
-    for k in range(1, at.tokens):
-        part, peer = at.along_seq(k)
-        vec_sends.append(wires.send(vec_ref.at[part], vecs_ref.at[k - 1], peer))
-    mine = 2 * b + c
-    for k in range(1, 2 * at.batches):
-        last.append(wires.send(col_ref, cols_ref.at[mine], at.along_plane(k)[2]))
-    own.append(wires.local(col_ref, cols_ref.at[mine]))
-
     whole = xs_ref[...].reshape(full_len, width)
     dw = dot_tn(whole, dcat_ref[...])
     dw_rel = dot_tn(table_ref[...], rel_ref[...])
@@ -1356,7 +1356,6 @@
     for k in range(1, at.batches):
         row, peer = at.along_rows(k)
         dw_sends.append(wires.send(dw_ref.at[row], dws_ref.at[k - 1], peer))
-    line.pass_on(order)
 
     rows = pl.ds(pl.multiple_of(b * bucket_rows, bucket_rows), bucket_rows)
     total = rel_ref[rows].astype(wide)
@@ -1399,6 +1398,7 @@
     def _():
         tab_stay.start()
 
+    line.pass_on(order[:1])
     mix = dot_tn(
         ctx_ref[...].reshape(full_len, group), attn_ref[...].reshape(full_len, width)
     )
@@ -1408,15 +1408,7 @@
         row, peer = at.along_rows(k)
         mix_sends.append(wires.send(mix_ref.at[row], mixs_ref.at[k - 1], peer))
 
-    total = vec_ref[s]
-    for k in range(1, at.tokens):
-        vec_sends[k - 1].wait_recv()
-        total = total + vecs_ref[k - 1]
-    vec_low_ref[...] = total
-    for k in range(1, at.batches):
-        last.append(wires.send(vec_low_ref, vec_all_ref.at[b], at.along_rows(k)[1]))
-    own.append(wires.local(vec_low_ref, vec_all_ref.at[b]))
-
+    line.pass_on(order[1:2])
     total = dw_ref[b].astype(wide)
     for k in range(1, at.batches):
         dw_sends[k - 1].wait_recv()
@@ -1449,6 +1441,7 @@
 
     last.append(wires.send(dw_low_ref.at[1 - c], dw_all_ref.at[c], cross))
 
+    line.pass_on(order[2:])
     total = mix_ref[b].astype(wide)
     for k in range(1, at.batches):
         mix_sends[k - 1].wait_recv()
@@ -1456,6 +1449,15 @@
     mix_low_ref[...] = total.astype(low)
     last.append(wires.send(mix_low_ref, mix_all_ref.at[c], at.partner()))
     own.append(wires.local(mix_low_ref, mix_all_ref.at[c]))
+
+    total = vec_ref[s]
+    for k in range(1, at.tokens):
+        vec_sends[k - 1].wait_recv()
+        total = total + vecs_ref[k - 1]
+    vec_low_ref[...] = total
+    for k in range(1, at.batches):
+        last.append(wires.send(vec_low_ref, vec_all_ref.at[b], at.along_rows(k)[1]))
+    own.append(wires.local(vec_low_ref, vec_all_ref.at[b]))
 
     ins_ref[...] = sum_ref[z].astype(wide) + line.collect()
     for copy in last:

time: 228 us -> 207 us (0.908)
  Pallas kernels: 223 us -> 202 us
    pallas_call x2, Pallas kernels: 87.8 us -> 80.8 us  [comm_call(): pl.pallas_call(kernel, out_shape=tuple(out_shapes), in_specs=[spec] * len...]
    pallas_call x1, Pallas kernels: 23.5 us -> 17.6 us  [attend(): pl.pallas_call(attend_kernel, out_shape=(jax.ShapeDtypeStruct((2, full_le...]
    pallas_call x1, Pallas kernels: 25.3 us -> 19.8 us  [attend_back(): pl.pallas_call(attend_back_kernel, out_shape=(jax.ShapeDtypeStruct((full_...]
    pallas_call x1, Pallas kernels: 85.1 us -> 82.7 us  [feed_forward(): pl.pallas_call(feed_kernel, out_shape=outs, in_specs=[VMEM_SPEC] * len(in...]
where the time goes in v8:
time: 207 us; the launch traced here: 206 us
  Pallas kernels  202 us (98%)
  other arithmetic  3.28 us (2%)
    pallas_call x1, Pallas kernels, feed_forward(): pl.pallas_call(feed_kernel, out_shape=outs, in_specs=[VMEM_SPEC] * len(in...  82.7 us
    pallas_call x2, Pallas kernels, comm_call(): pl.pallas_call(kernel, out_shape=tuple(out_shapes), in_specs=[spec] * len...  80.8 us
    pallas_call x1, Pallas kernels, attend_back(): pl.pallas_call(attend_back_kernel, out_shape=(jax.ShapeDtypeStruct((full_...  19.8 us
    pallas_call x1, Pallas kernels, attend(): pl.pallas_call(attend_kernel, out_shape=(jax.ShapeDtypeStruct((2, full_le...  17.6 us

profile of v8, /device:TPU:0, one launch (start us, length us, event | category | flops | bytes accessed | tf_op | source)
XLA Modules:
  0.0 206.3 jit_solution(3759131570302030252)
XLA Ops:
  0.6 0.7 convert_element_type.7
  1.3 0.7 fusion.9
  2.0 1.3 fusion.11.vec_ref
  3.3 42.7 %gather_inputs.1 = (bf16[8,128,768]{2,1,0:T(8,128)(2,1)S(1)}, bf16[8,3,96,192]{3,2,1,0:T(8,128)(2,1)S(1)}, bf16[2,4,4,96,192]{4,3,2,1,0:T(8,128)(2,1)S(1)}, bf16...) custom-call(bf16[128,768]{1,0:T(8,128)(2,1)} %bitcast.8, ...), custom_call_target="tpu_custom_call" | custom-call | tf_op jit(solution)/shard_map/gather_inputs/pallas_call | solution.py:664
  46.0 0.0 copy-start
  46.0 0.0 copy-start.1
  46.0 0.0 copy-start.2
  46.0 0.0 copy-start.3
  46.1 17.6 %attend.1 = (bf16[2,1024,64]{2,1,0:T(8,128)(2,1)S(1)}, bf16[2,1024,64]{2,1,0:T(8,128)(2,1)S(1)}, bf16[2,1024,64]{2,1,0:T(8,128)(2,1)S(1)}, bf16[2,512,64]{2,1,0:...) custom-call(bf16[8,128,768]{2,1,0:T(8,128)(2,1)S(1)} %get-tuple-elem, ...), custom_call_target="tpu_custom_call" | custom-call | tf_op jit(solution)/shard_map/attend/pallas_call | solution.py:348
  63.6 0.0 copy-done
  63.6 0.0 copy-done.1
  63.6 0.0 copy-done.2
  63.7 0.0 copy-done.3
  63.7 82.7 %feed_forward.1 = (bf16[128,768]{1,0:T(8,128)(2,1)S(1)}, f32[128,768]{1,0:T(8,128)S(1)}, f32[8,8,128]{2,1,0:T(8,128)S(1)}, bf16[8,128,768]{2,1,0:T(8,128)(2,1)S(...) custom-call(bf16[8,128,128]{2,1,0:T(8,128)(2,1)S(1)} %get-tuple-elem, ...), custom_call_target="tpu_custom_call" | custom-call | tf_op jit(solution)/shard_map/feed_forward/pallas_call | solution.py:1282
  146.4 19.8 %attend_back.1 = (bf16[1024,384]{1,0:T(8,128)(2,1)S(1)}, bf16[512,256]{1,0:T(8,128)(2,1)S(1)}, f32[8,384]{1,0:T(8,128)S(1)}) custom-call(bf16[2,1024,64]{2,1,0:T(8,128)(2,1)S(1)} %get-tuple-element.71.q_ref, bf16[2,1024,64]{2,1,0:T(8,128)(2,1)S(1)} %get-tuple-element.72.k_ref, bf16[2,1024,64]{2,1,0:T(8,128)(2,1)S(1)} %get-tuple-element.73.v_ref, ...), custom_call_target="tpu_custom_call" | custom-call | tf_op jit(solution)/shard_map/attend_back/pallas_call | solution.py:518
  166.2 38.1 %settle_grads.1 = (f32[128,768]{1,0:T(8,128)S(1)}, f32[4,8,128]{2,1,0:T(8,128)S(1)}, f32[8,8,384]{2,1,0:T(8,128)S(1)}, bf16[2,96,384]{2,1,0:T(8,128)(2,1)S(1)}, ...) custom-call(f32[8,8,128]{2,1,0:T(8,128)S(1)} %get-tuple-element.70.vec_ref, ...), custom_call_target="tpu_custom_call" | custom-call | tf_op jit(solution)/shard_map/settle_grads/pallas_call | solution.py:664
  204.4 1.3 finish.1
  205.7 0.6 reduce
Async XLA Ops:
  46.0 17.6 %copy-start = (bf16[768,384]{1,0:T(8,128)(2,1)S(1)}, bf16[768,384]{1,0:T(8,128)(2,1)}, u32[]{:S(2)}) copy-start(bf16[768,384]{1,0:T(8,128)(2,1)} %up_ref.3) | copy-start | bytes 1769476
  46.0 17.6 %copy-start.1 = (bf16[384,768]{1,0:T(8,128)(2,1)S(1)}, bf16[384,768]{1,0:T(8,128)(2,1)}, u32[]{:S(2)}) copy-start(bf16[384,768]{1,0:T(8,128)(2,1)} %down_ref.3) | copy-start | bytes 1769476
  46.0 17.6 %copy-start.2 = (bf16[1,128,768]{2,1,0:T(8,128)(2,1)S(1)}, bf16[1,128,768]{2,1,0:T(8,128)(2,1)}, u32[]{:S(2)}) copy-start(bf16[1,128,768]{2,1,0:T(8,128)(2,1)} %param.15) | copy-start | bytes 589828
  46.0 17.6 %copy-start.3 = (bf16[1,128,768]{2,1,0:T(8,128)(2,1)S(1)}, bf16[1,128,768]{2,1,0:T(8,128)(2,1)}, u32[]{:S(2)}) copy-start(bf16[1,128,768]{2,1,0:T(8,128)(2,1)} %param.29) | copy-start | bytes 589828

commit v9 on v8

--- a/solution.py
+++ b/solution.py
@@ -166,7 +166,7 @@
 BLOCK = 128
 MIB = 1024 * 1024
 ATTEND_VMEM = 26 * MIB
-BACK_VMEM = 26 * MIB
+BACK_VMEM = 40 * MIB
 FEED_VMEM = 26 * MIB
 COMM_VMEM = 16 * MIB
 
@@ -508,39 +508,6 @@
     sum_ref[...] = jnp.broadcast_to(sums, sum_ref.shape)
 
 
-def attend_back(q, k, v, qrev, krev, probs, m_mix, attn_all):
-    full_len = q.shape[1]
-    buckets = qrev.shape[1]
-    blocks = full_len // BLOCK
-    band_width = buckets + BLOCK
-    low, wide = jnp.bfloat16, jnp.float32
-    pad_blocks = blocks + band_width // BLOCK - 1
-    return pl.pallas_call(
-        attend_back_kernel,
-        out_shape=(
-            jax.ShapeDtypeStruct((full_len, 6 * DH), low),
-            jax.ShapeDtypeStruct((buckets, 4 * DH), low),
-            jax.ShapeDtypeStruct((8, 6 * DH), wide),
-        ),
-        in_specs=[pl.BlockSpec(memory_space=pltpu.VMEM)] * 8,
-        out_specs=[pl.BlockSpec(memory_space=pltpu.VMEM)] * 3,
-        scratch_shapes=[
-            pltpu.VMEM((2, full_len, DH), low),
-            pltpu.VMEM((2, BLOCK, full_len + buckets), wide),
-            pltpu.VMEM((2, BLOCK, full_len + buckets), low),
-            pltpu.VMEM((2, pad_blocks, BLOCK, band_width), wide),
-            pltpu.VMEM((4, full_len, DH), wide),
-            pltpu.VMEM((2, DH, full_len), wide),
-            pltpu.VMEM((2, DH, full_len), wide),
-            pltpu.VMEM((2, 8, full_len), wide),
-            pltpu.VMEM((2, DH, buckets), wide),
-            pltpu.VMEM((2, DH, buckets), wide),
-        ],
-        compiler_params=pltpu.CompilerParams(vmem_limit_bytes=BACK_VMEM),
-        name="attend_back",
-    )(q, k, v, qrev, krev, probs, m_mix, attn_all)
-
-
 MESH = pl.DeviceIdType.MESH
 VMEM_SPEC = pl.BlockSpec(memory_space=pltpu.VMEM)
 HBM_SPEC = pl.BlockSpec(memory_space=pltpu.HBM)
@@ -660,7 +627,7 @@
     ]
 
 
-def comm_call(kernel, name, ident, out_shapes, inputs, sends, locals_count, scratch=(), spec=VMEM_SPEC):
+def comm_call(kernel, name, ident, out_shapes, inputs, sends, locals_count, scratch=(), spec=VMEM_SPEC, limit=None):
     return pl.pallas_call(
         kernel,
         out_shape=tuple(out_shapes),
@@ -668,7 +635,7 @@
         out_specs=tuple([VMEM_SPEC] * len(out_shapes)),
         scratch_shapes=list(scratch) + wire_scratch(sends, locals_count),
         compiler_params=pltpu.CompilerParams(
-            collective_id=ident, has_side_effects=True, vmem_limit_bytes=COMM_VMEM
+            collective_id=ident, has_side_effects=True, vmem_limit_bytes=limit or COMM_VMEM
         ),
         name=name,
     )(*inputs)
@@ -1044,21 +1011,20 @@
     return scale * (inner - mean - unit * slope)
 
 
-def line_pass(gather, reduce, order, work):
-    def finish(j):
+def line_pass(gather, reduce, order, work, after=None):
+    for j in order:
+        gather.arrive(j)
         work(j)
         reduce.send_last(j)
-
-    for j in order:
-        gather.arrive(j)
-        finish(j)
+        if after is not None:
+            after(j)
 
 
 def feed_kernel(
     ctx_ref, x_ref, mixs_ref, vecs_ref, up_ref, down_ref, up2_ref, down2_ref, out_grad_ref,
     output_ref, pre_grad_ref, sums_ref, attn_ref, mix_ref, ups_ref, downs_ref, upbs_ref,
     got_ref, hid_ref, act_ref, slope_ref, part_ref, ffn_ref, grad_ref, inner_ref,
-    back_ref, backs_ref, up_away_ref, down_away_ref, upb_away_ref,
+    back_ref, backs_ref, up_acc_ref, down_acc_ref, up_away_ref, down_away_ref, upb_away_ref,
     up_got_ref, down_got_ref, upb_got_ref, upg_ref, downg_ref, upb_ref, vec_ref,
     hid_send, hid_recv, ffn_send, ffn_recv, grad_send, grad_recv, back_send, back_recv,
     attn_send, attn_recv, *sems,
@@ -1161,19 +1127,20 @@
             + dot_nt(inner_low[:, hidden_here:], up2_ref[...])
         ).astype(low)
 
+    def weight_grads(chip):
+        up_acc_ref[...] += dot_tn(hid_ref[chip], inner_ref[chip])
+        down_acc_ref[...] += dot_tn(grad_ref[chip], act_ref[chip])
+
     back(z)
-    line_pass(grad_line, back_line, order, back)
+    up_acc_ref[...] = dot_tn(hid_ref[z], inner_ref[z])
+    down_acc_ref[...] = dot_tn(grad_ref[z], act_ref[z])
+    line_pass(grad_line, back_line, order, back, weight_grads)
     width = x_ref.shape[1]
     columns = width // at.batches
     inner_all = inner_ref[...].reshape(at.chips * BLOCK, 2 * hidden_here)
-    act_all = act_ref[...].reshape(at.chips * BLOCK, 2 * hidden_here)
-    hid_all = hid_ref[...].reshape(at.chips * BLOCK, width)
-    grad_all = grad_ref[...].reshape(at.chips * BLOCK, width)
     near, away = slice(0, hidden_here), slice(hidden_here, 2 * hidden_here)
-    up_grad = dot_tn(hid_all, inner_all)
-    up_away_ref[...] = up_grad[:, away].astype(low)
-    down_grad = dot_tn(grad_all, act_all)
-    down_away_ref[...] = down_grad[:, away].astype(low)
+    up_away_ref[...] = up_acc_ref[:, away].astype(low)
+    down_away_ref[...] = down_acc_ref[:, away].astype(low)
     upb_grad = jnp.sum(inner_all.astype(wide), axis=0, keepdims=True)
     upb_away_ref[...] = jnp.broadcast_to(upb_grad[:, away], upb_away_ref.shape)
     halves = [
@@ -1185,8 +1152,8 @@
     for copy in halves:
         copy.wait_recv()
     upb_ref[...] = jnp.broadcast_to(upb_grad[:, near], upb_ref.shape) + upb_got_ref[...]
-    up_sum = (up_grad[:, near] + up_got_ref[...].astype(wide)).astype(low)
-    down_sum = (down_grad[:, near] + down_got_ref[...].astype(wide)).astype(low)
+    up_sum = (up_acc_ref[:, near] + up_got_ref[...].astype(wide)).astype(low)
+    down_sum = (down_acc_ref[:, near] + down_got_ref[...].astype(wide)).astype(low)
     for row in range(at.batches):
         upg_ref[row] = up_sum[row * columns : (row + 1) * columns]
         downg_ref[row] = down_sum[row * columns : (row + 1) * columns]
@@ -1265,6 +1232,8 @@
         pltpu.VMEM(wide_block, low),
         pltpu.VMEM(block, low),
         pltpu.VMEM(slots, low),
+        pltpu.VMEM((width, 2 * hidden_here), wide),
+        pltpu.VMEM((width, 2 * hidden_here), wide),
         pltpu.VMEM(up_half, low),
         pltpu.VMEM(down_half, low),
         pltpu.VMEM(bias_half, wide),
@@ -1293,10 +1262,13 @@
 
 
 def settle_kernel(
-    vec_ref, col_ref, dcat_ref, rel_ref, w_ref, xs_ref, table_ref, ctx_ref, attn_ref,
+    q_ref, k_ref, v_ref, qrev_ref, krev_ref, p_ref, mix_all_rows_ref,
+    vec_ref, w_ref, xs_ref, table_ref, ctx_ref, attn_ref,
     ins_ref, vec_all_ref, cols_ref, dw_all_ref, tab_all_ref, mix_all_ref,
     in_ref, dw_ref, tab_ref, mix_ref, half_ref, sum_ref, got_ref, vecs_ref, vec_low_ref,
     dws_ref, dw_low_ref, rels_ref, rel_low_ref, mixs_ref, mix_low_ref,
+    dcat_ref, rel_ref, col_ref, heads_ref, wide_ref, low_ref, place_ref, dq_ref, dkt_ref,
+    dvt_ref, far_ref, dkr_ref, dqr_ref,
     line_send, line_recv, tab_send, tab_recv, *sems,
 ):
     at = Place()
@@ -1305,7 +1277,16 @@
     b, s, z, c = at.row, at.part, at.chip, at.core
     off_diagonal = b != z
     same, cross = (z, 2 * b + c), (z, 2 * b + 1 - c)
-    meet(at.all_peers())
+    peers = at.all_peers()
+    barrier = pltpu.get_barrier_semaphore()
+    for peer in peers:
+        pl.semaphore_signal(barrier, inc=1, device_id=peer, device_id_type=MESH)
+    attend_back_kernel(
+        q_ref, k_ref, v_ref, qrev_ref, krev_ref, p_ref, mix_all_rows_ref, attn_ref,
+        dcat_ref, rel_ref, col_ref, heads_ref, wide_ref, low_ref, place_ref, dq_ref, dkt_ref,
+        dvt_ref, far_ref, dkr_ref, dqr_ref,
+    )
+    pl.semaphore_wait(barrier, len(peers))
     width = w_ref.shape[0]
     columns = width // at.batches
     full_len = dcat_ref.shape[0]
@@ -1496,21 +1477,24 @@
         stay.wait()
 
 
-def settle_grads(vec, cols, dcat, rel, w_cat, xs, table, ctx, attn_all, ident):
+def settle_grads(q, k, v, qrev, krev, probs, m_mix, vec, w_cat, xs, table, ctx, attn_all, ident):
     tokens, batches = lax.axis_size("seq"), lax.axis_size("batch")
     chips = tokens // 2
     low, wide = jnp.bfloat16, jnp.float32
     local_len, width = xs.shape[1:]
-    columns, group = width // batches, dcat.shape[1]
+    columns, group = width // batches, 6 * DH
     buckets = table.shape[0]
+    full_len = tokens * local_len
+    band_width = buckets + BLOCK
+    pad_blocks = full_len // BLOCK + band_width // BLOCK - 1
     half = (chips, local_len, width)
     dw_pieces = (2, columns // 2, group)
     mix_piece = (2 * DH, columns)
-    dw_piece, rel_piece = (columns, group), (buckets // batches, rel.shape[1])
+    dw_piece, rel_piece = (columns, group), (buckets // batches, 4 * DH)
     outs = (
         jax.ShapeDtypeStruct((local_len, width), wide),
         jax.ShapeDtypeStruct((batches,) + vec.shape[1:], wide),
-        like(cols, 2 * batches),
+        jax.ShapeDtypeStruct((2 * batches, 8, group), wide),
         jax.ShapeDtypeStruct(dw_pieces, low),
         jax.ShapeDtypeStruct((tokens, buckets // tokens, columns), low),
         jax.ShapeDtypeStruct((2,) + mix_piece, low),
@@ -1531,12 +1515,35 @@
         pltpu.VMEM(rel_piece, low),
         pltpu.VMEM((batches - 1,) + mix_piece, low),
         pltpu.VMEM(mix_piece, low),
+        pltpu.VMEM((full_len, group), low),
+        pltpu.VMEM((buckets, 4 * DH), low),
+        pltpu.VMEM((8, group), wide),
+        pltpu.VMEM((2, full_len, DH), low),
+        pltpu.VMEM((2, BLOCK, full_len + buckets), wide),
+        pltpu.VMEM((2, BLOCK, full_len + buckets), low),
+        pltpu.VMEM((2, pad_blocks, BLOCK, band_width), wide),
+        pltpu.VMEM((4, full_len, DH), wide),
+        pltpu.VMEM((2, DH, full_len), wide),
+        pltpu.VMEM((2, DH, full_len), wide),
+        pltpu.VMEM((2, 8, full_len), wide),
+        pltpu.VMEM((2, DH, buckets), wide),
+        pltpu.VMEM((2, DH, buckets), wide),
     ]
     scratch += reduce_sems(chips)
     scratch += [pltpu.SemaphoreType.DMA((2 * batches,)), pltpu.SemaphoreType.DMA((tokens,))]
     sends = 4 * (batches - 1) + chips + tokens - 1 + 2 * batches - 1 + 3
-    inputs = (vec, cols, dcat, rel, w_cat, xs, table, ctx, attn_all)
-    return comm_call(settle_kernel, "settle_grads", ident, outs, inputs, sends, 6, scratch=scratch)
+    inputs = (q, k, v, qrev, krev, probs, m_mix, vec, w_cat, xs, table, ctx, attn_all)
+    return comm_call(
+        settle_kernel,
+        "settle_grads",
+        ident,
+        outs,
+        inputs,
+        sends,
+        6,
+        scratch=scratch,
+        limit=BACK_VMEM,
+    )
 
 
 def finish_kernel(
@@ -1642,9 +1649,8 @@
     output, pre_grad, sums, attn_all, m_mix, ups, downs, upbs = feed_forward(
         ctx, x, mixs, vecs, w_up, w_down, up2, down2, out_grad[0], 1
     )
-    dcat, rel_grad, cols = attend_back(q, k, v, qrev, krev, probs, m_mix, attn_all)
     ins, vec_all, cols_all, dw_all, tab_all, mix_all = settle_grads(
-        sums, cols, dcat, rel_grad, w_cat, xs, table, ctx, attn_all, 2
+        q, k, v, qrev, krev, probs, m_mix, sums, w_cat, xs, table, ctx, attn_all, 2
     )
     shard = (shard_rows, shard_cols)
     shapes = (

time: 207 us -> 204 us (0.986)
    pallas_call x1 -> x0, Pallas kernels: 19.8 us -> none  [attend_back(): pl.pallas_call(attend_back_kernel, out_shape=(jax.ShapeDtypeStruct((full_...]
    pallas_call x2, Pallas kernels: 80.8 us -> 97.9 us  [comm_call(): pl.pallas_call(kernel, out_shape=tuple(out_shapes), in_specs=[spec] * len...]
where the time goes in v9:
time: 204 us
  Pallas kernels  200 us (98%)
  other arithmetic  3.28 us (2%)
    pallas_call x2, Pallas kernels, comm_call(): pl.pallas_call(kernel, out_shape=tuple(out_shapes), in_specs=[spec] * len...  97.9 us
    pallas_call x1, Pallas kernels, feed_forward(): pl.pallas_call(feed_kernel, out_shape=outs, in_specs=[VMEM_SPEC] * len(in...  82.7 us
    pallas_call x1, Pallas kernels, attend(): pl.pallas_call(attend_kernel, out_shape=(jax.ShapeDtypeStruct((2, full_le...  17.6 us

profile of v9, /device:TPU:0, one launch (start us, length us, event | category | flops | bytes accessed | tf_op | source)
XLA Modules:
  0.0 203.6 jit_solution(15719793483627290869)
XLA Ops:
  0.6 0.7 convert_element_type.7
  1.3 0.7 fusion.9
  2.0 1.3 fusion.11.vec_ref
  3.3 42.7 %gather_inputs.1 = (bf16[8,128,768]{2,1,0:T(8,128)(2,1)S(1)}, bf16[8,3,96,192]{3,2,1,0:T(8,128)(2,1)S(1)}, bf16[2,4,4,96,192]{4,3,2,1,0:T(8,128)(2,1)S(1)}, bf16...) custom-call(bf16[128,768]{1,0:T(8,128)(2,1)} %bitcast.8, ...), custom_call_target="tpu_custom_call" | custom-call | tf_op jit(solution)/shard_map/gather_inputs/pallas_call | solution.py:631
  46.0 0.0 copy-start
  46.0 0.0 copy-start.1
  46.0 0.0 copy-start.2
  46.0 0.0 copy-start.3
  46.1 17.6 %attend.1 = (bf16[2,1024,64]{2,1,0:T(8,128)(2,1)S(1)}, bf16[2,1024,64]{2,1,0:T(8,128)(2,1)S(1)}, bf16[2,1024,64]{2,1,0:T(8,128)(2,1)S(1)}, bf16[2,512,64]{2,1,0:...) custom-call(bf16[8,128,768]{2,1,0:T(8,128)(2,1)S(1)} %get-tuple-elem, ...), custom_call_target="tpu_custom_call" | custom-call | tf_op jit(solution)/shard_map/attend/pallas_call | solution.py:348
  63.6 0.0 copy-done
  63.7 0.0 copy-done.1
  63.7 0.0 copy-done.2
  63.7 0.0 copy-done.3
  63.7 82.7 %feed_forward.1 = (bf16[128,768]{1,0:T(8,128)(2,1)S(1)}, f32[128,768]{1,0:T(8,128)S(1)}, f32[8,8,128]{2,1,0:T(8,128)S(1)}, bf16[8,128,768]{2,1,0:T(8,128)(2,1)S(...) custom-call(bf16[8,128,128]{2,1,0:T(8,128)(2,1)S(1)} %get-tuple-elem, ...), custom_call_target="tpu_custom_call" | custom-call | tf_op jit(solution)/shard_map/feed_forward/pallas_call | solution.py:1251
  146.4 55.2 %settle_grads.1 = (f32[128,768]{1,0:T(8,128)S(1)}, f32[4,8,128]{2,1,0:T(8,128)S(1)}, f32[8,8,384]{2,1,0:T(8,128)S(1)}, bf16[2,96,384]{2,1,0:T(8,128)(2,1)S(1)}, ...) custom-call(bf16[2,1024,64]{2,1,0:T(8,128)(2,1)S(1)} %get-tuple-element.67.q_ref, ...), custom_call_target="tpu_custom_call" | custom-call | tf_op jit(solution)/shard_map/settle_grads/pallas_call | solution.py:631
  201.6 1.3 finish.1
  203.0 0.6 reduce
Async XLA Ops:
  46.0 17.6 %copy-start = (bf16[768,384]{1,0:T(8,128)(2,1)S(1)}, bf16[768,384]{1,0:T(8,128)(2,1)}, u32[]{:S(2)}) copy-start(bf16[768,384]{1,0:T(8,128)(2,1)} %up_ref.3) | copy-start | bytes 1769476
  46.0 17.6 %copy-start.1 = (bf16[384,768]{1,0:T(8,128)(2,1)S(1)}, bf16[384,768]{1,0:T(8,128)(2,1)}, u32[]{:S(2)}) copy-start(bf16[384,768]{1,0:T(8,128)(2,1)} %down_ref.3) | copy-start | bytes 1769476
  46.0 17.6 %copy-start.2 = (bf16[1,128,768]{2,1,0:T(8,128)(2,1)S(1)}, bf16[1,128,768]{2,1,0:T(8,128)(2,1)}, u32[]{:S(2)}) copy-start(bf16[1,128,768]{2,1,0:T(8,128)(2,1)} %param.15) | copy-start | bytes 589828
  46.0 17.6 %copy-start.3 = (bf16[1,128,768]{2,1,0:T(8,128)(2,1)S(1)}, bf16[1,128,768]{2,1,0:T(8,128)(2,1)}, u32[]{:S(2)}) copy-start(bf16[1,128,768]{2,1,0:T(8,128)(2,1)} %param.29) | copy-start | bytes 589828

commit v10 on v9

--- a/solution.py
+++ b/solution.py
@@ -524,6 +524,9 @@
         self.chip = self.part // 2
         self.core = self.part % 2
 
+    def inside(self):
+        return jnp.logical_and(self.chip > 0, self.chip < self.chips - 1)
+
     def along_chips(self, k):
         chip = lax.rem(self.chip + k, self.chips)
         return chip, (self.row, 2 * chip + self.core)
@@ -719,14 +722,33 @@
     def start(self):
         self.own_each(lambda copy: copy.start())
 
-    def arrive(self, j):
+    def arrive_chunk(self, j, h):
         step = jnp.where(j < self.at.chip, 1, -1)
-        for h in range(CHUNKS):
-            self.copy(j, h, -step, j).wait_recv()
-
-            @pl.when(goes_on(self.at, j))
+        self.copy(j, h, -step, j).wait_recv()
+
+        @pl.when(goes_on(self.at, j))
+        def _():
+            self.copy(j, h, step, j).start()
+
+    def arrive(self, order, t):
+        if t == 0:
+
+            @pl.when(self.at.inside())
             def _():
-                self.copy(j, h, step, j).start()
+                for h in range(CHUNKS):
+                    self.arrive_chunk(order[0], h)
+                    self.arrive_chunk(order[1], h)
+
+        if t < 2:
+
+            @pl.when(jnp.logical_not(self.at.inside()))
+            def _():
+                for h in range(CHUNKS):
+                    self.arrive_chunk(order[t], h)
+
+        else:
+            for h in range(CHUNKS):
+                self.arrive_chunk(order[t], h)
 
     def drain(self, order):
         self.own_each(lambda copy: copy.wait_send())
@@ -778,20 +800,21 @@
         def _():
             self.send(j)
 
+    def pass_chunk(self, j, h):
+        wide = jnp.float32
+        step = jnp.where(j < self.at.chip, 1, -1)
+        self.landed(j, h, step).wait_recv()
+        window = pl.ds(h * self.rows, self.rows)
+        total = self.part[j, window].astype(wide) + self.got[j, window].astype(wide)
+        self.part[j, window] = total.astype(self.part.dtype)
+        self.copy(j, h).start()
+
     def pass_on(self, order):
-        z, n = self.at.chip, self.at.chips
-        wide = jnp.float32
-
-        @pl.when(jnp.logical_and(z > 0, z < n - 1))
+        @pl.when(self.at.inside())
         def _():
-            for j in order:
-                step = jnp.where(j < z, 1, -1)
-                for h in range(CHUNKS):
-                    self.landed(j, h, step).wait_recv()
-                    window = pl.ds(h * self.rows, self.rows)
-                    total = self.part[j, window].astype(wide) + self.got[j, window].astype(wide)
-                    self.part[j, window] = total.astype(self.part.dtype)
-                    self.copy(j, h).start()
+            for h in range(CHUNKS):
+                for j in order:
+                    self.pass_chunk(j, h)
 
     def clear(self):
         z, n = self.at.chip, self.at.chips
@@ -930,18 +953,18 @@
     last.append(wires.send(mine, mine, at.partner()))
     order = arrival_order(at)
 
-    def arrived(j):
-        line.arrive(j)
-        home = xs_ref.at[2 * j + c]
+    def arrived(t):
+        line.arrive(order, t)
+        home = xs_ref.at[2 * order[t] + c]
         last.append(wires.send(home, home, at.partner()))
 
-    arrived(order[0])
+    arrived(0)
     for copy in mix_sends:
         copy.wait_recv()
     mine = mixs_ref.at[c, b]
     mix_rows = [wires.send(mine, mine, at.along_rows(k)[1]) for k in range(1, at.batches)]
     last.append(wires.send(mine, mine, at.partner()))
-    arrived(order[1])
+    arrived(1)
     for k in range(1, at.batches):
         qkv_sends[k - 1].wait_recv()
         home = qkvs_ref.at[2 * at.from_rows(k) + c]
@@ -950,8 +973,8 @@
         row_sends[k - 1].wait_recv()
         home = tables_ref.at[c, at.from_rows(k)]
         last.append(wires.send(home, home, at.partner()))
-    for j in order[2:]:
-        arrived(j)
+    for t in range(2, at.chips - 1):
+        arrived(t)
     for k in range(1, at.batches):
         mix_rows[k - 1].wait_recv()
         home = mixs_ref.at[c, at.from_rows(k)]
@@ -1011,13 +1034,11 @@
     return scale * (inner - mean - unit * slope)
 
 
-def line_pass(gather, reduce, order, work, after=None):
-    for j in order:
-        gather.arrive(j)
+def line_pass(gather, reduce, order, work):
+    for t, j in enumerate(order):
+        gather.arrive(order, t)
         work(j)
         reduce.send_last(j)
-        if after is not None:
-            after(j)
 
 
 def feed_kernel(
@@ -1099,7 +1120,8 @@
 
     ffn(z)
     line_pass(hid_line, ffn_line, order, ffn)
-    ffn_line.pass_on(returns)
+    ffn_line.pass_on(returns[:1])
+    ffn_line.pass_on(returns[1:])
     total = part_ref[z].astype(wide) + ffn_line.collect()
     mixed = hidden + total + bias_down
     unit2, scale2 = norm_parts(mixed)
@@ -1134,7 +1156,11 @@
     back(z)
     up_acc_ref[...] = dot_tn(hid_ref[z], inner_ref[z])
     down_acc_ref[...] = dot_tn(grad_ref[z], act_ref[z])
-    line_pass(grad_line, back_line, order, back, weight_grads)
+    line_pass(grad_line, back_line, order, back)
+    back_line.pass_on(returns[:1])
+    back_line.pass_on(returns[1:])
+    for j in order:
+        weight_grads(j)
     width = x_ref.shape[1]
     columns = width // at.batches
     inner_all = inner_ref[...].reshape(at.chips * BLOCK, 2 * hidden_here)
@@ -1148,7 +1174,6 @@
         wires.send(down_away_ref, down_got_ref, at.partner()),
         wires.send(upb_away_ref, upb_got_ref, at.partner()),
     ]
-    back_line.pass_on(returns)
     for copy in halves:
         copy.wait_recv()
     upb_ref[...] = jnp.broadcast_to(upb_grad[:, near], upb_ref.shape) + upb_got_ref[...]
@@ -1186,8 +1211,8 @@
         sums_ref[part] = jnp.concatenate(
             [sums[:, part * lanes : (part + 1) * lanes], spare], axis=1
         )
-    for j in order:
-        attn_line.arrive(j)
+    for t, j in enumerate(order):
+        attn_line.arrive(order, t)
         home = attn_ref.at[2 * j + c]
         last.append(wires.send(home, home, at.partner()))
     for copy in last:
@@ -1389,7 +1414,7 @@
         row, peer = at.along_rows(k)
         mix_sends.append(wires.send(mix_ref.at[row], mixs_ref.at[k - 1], peer))
 
-    line.pass_on(order[1:2])
+    line.pass_on(order[1:])
     total = dw_ref[b].astype(wide)
     for k in range(1, at.batches):
         dw_sends[k - 1].wait_recv()
@@ -1422,7 +1447,6 @@
 
     last.append(wires.send(dw_low_ref.at[1 - c], dw_all_ref.at[c], cross))
 
-    line.pass_on(order[2:])
     total = mix_ref[b].astype(wide)
     for k in range(1, at.batches):
         mix_sends[k - 1].wait_recv()

time: 204 us -> 220 us (1.078)
  Pallas kernels: 200 us -> 214 us
    pallas_call x1, Pallas kernels: 82.7 us -> 96 us  [feed_forward(): pl.pallas_call(feed_kernel, out_shape=outs, in_specs=[VMEM_SPEC] * len(in...]
where the time goes in v10:
time: 220 us; the launch traced here: 218 us
  Pallas kernels  214 us (97%)
  other arithmetic  3.28 us (1%)
    pallas_call x2, Pallas kernels, comm_call(): pl.pallas_call(kernel, out_shape=tuple(out_shapes), in_specs=[spec] * len...  98.7 us
    pallas_call x1, Pallas kernels, feed_forward(): pl.pallas_call(feed_kernel, out_shape=outs, in_specs=[VMEM_SPEC] * len(in...  96 us
    pallas_call x1, Pallas kernels, attend(): pl.pallas_call(attend_kernel, out_shape=(jax.ShapeDtypeStruct((2, full_le...  17.6 us

profile of v10, /device:TPU:0, one launch (start us, length us, event | category | flops | bytes accessed | tf_op | source)
XLA Modules:
  0.0 217.6 jit_solution(2404477241870406874)
XLA Ops:
  0.6 0.7 convert_element_type.7
  1.3 0.7 fusion.9
  2.0 1.3 fusion.11.vec_ref
  3.3 42.7 %gather_inputs.1 = (bf16[8,128,768]{2,1,0:T(8,128)(2,1)S(1)}, bf16[8,3,96,192]{3,2,1,0:T(8,128)(2,1)S(1)}, bf16[2,4,4,96,192]{4,3,2,1,0:T(8,128)(2,1)S(1)}, bf16...) custom-call(bf16[128,768]{1,0:T(8,128)(2,1)} %bitcast.8, ...), custom_call_target="tpu_custom_call" | custom-call | tf_op jit(solution)/shard_map/gather_inputs/pallas_call | solution.py:634
  46.0 0.0 copy-start
  46.0 0.0 copy-start.1
  46.0 0.0 copy-start.2
  46.0 0.0 copy-start.3
  46.1 17.6 %attend.1 = (bf16[2,1024,64]{2,1,0:T(8,128)(2,1)S(1)}, bf16[2,1024,64]{2,1,0:T(8,128)(2,1)S(1)}, bf16[2,1024,64]{2,1,0:T(8,128)(2,1)S(1)}, bf16[2,512,64]{2,1,0:...) custom-call(bf16[8,128,768]{2,1,0:T(8,128)(2,1)S(1)} %get-tuple-elem, ...), custom_call_target="tpu_custom_call" | custom-call | tf_op jit(solution)/shard_map/attend/pallas_call | solution.py:348
  63.6 0.0 copy-done
  63.7 0.0 copy-done.1
  63.7 0.0 copy-done.2
  63.7 0.0 copy-done.3
  63.7 96.0 %feed_forward.1 = (bf16[128,768]{1,0:T(8,128)(2,1)S(1)}, f32[128,768]{1,0:T(8,128)S(1)}, f32[8,8,128]{2,1,0:T(8,128)S(1)}, bf16[8,128,768]{2,1,0:T(8,128)(2,1)S(...) custom-call(bf16[8,128,128]{2,1,0:T(8,128)(2,1)S(1)} %get-tuple-elem, ...), custom_call_target="tpu_custom_call" | custom-call | tf_op jit(solution)/shard_map/feed_forward/pallas_call | solution.py:1276
  159.7 56.0 %settle_grads.1 = (f32[128,768]{1,0:T(8,128)S(1)}, f32[4,8,128]{2,1,0:T(8,128)S(1)}, f32[8,8,384]{2,1,0:T(8,128)S(1)}, bf16[2,96,384]{2,1,0:T(8,128)(2,1)S(1)}, ...) custom-call(bf16[2,1024,64]{2,1,0:T(8,128)(2,1)S(1)} %get-tuple-element.67.q_ref, ...), custom_call_target="tpu_custom_call" | custom-call | tf_op jit(solution)/shard_map/settle_grads/pallas_call | solution.py:634
  215.7 1.3 finish.1
  217.0 0.6 reduce
Async XLA Ops:
  46.0 17.6 %copy-start = (bf16[768,384]{1,0:T(8,128)(2,1)S(1)}, bf16[768,384]{1,0:T(8,128)(2,1)}, u32[]{:S(2)}) copy-start(bf16[768,384]{1,0:T(8,128)(2,1)} %up_ref.3) | copy-start | bytes 1769476
  46.0 17.6 %copy-start.1 = (bf16[384,768]{1,0:T(8,128)(2,1)S(1)}, bf16[384,768]{1,0:T(8,128)(2,1)}, u32[]{:S(2)}) copy-start(bf16[384,768]{1,0:T(8,128)(2,1)} %down_ref.3) | copy-start | bytes 1769476
  46.0 17.6 %copy-start.2 = (bf16[1,128,768]{2,1,0:T(8,128)(2,1)S(1)}, bf16[1,128,768]{2,1,0:T(8,128)(2,1)}, u32[]{:S(2)}) copy-start(bf16[1,128,768]{2,1,0:T(8,128)(2,1)} %param.15) | copy-start | bytes 589828
  46.0 17.6 %copy-start.3 = (bf16[1,128,768]{2,1,0:T(8,128)(2,1)S(1)}, bf16[1,128,768]{2,1,0:T(8,128)(2,1)}, u32[]{:S(2)}) copy-start(bf16[1,128,768]{2,1,0:T(8,128)(2,1)} %param.29) | copy-start | bytes 589828

commit v11 on v10

--- a/solution.py
+++ b/solution.py
@@ -233,6 +233,7 @@
     wide_ref,
     ends_ref,
     held_ref,
+    between,
 ):
     at = Place()
     full_len = xs_ref.shape[0] * xs_ref.shape[1]
@@ -299,6 +300,7 @@
         lax.fori_loop(0, blocks, key_block, 0, unroll=8)
 
     first = at.core * (blocks // 2)
+    between()
 
     def unit(u, carry):
         g = u + first
@@ -334,42 +336,6 @@
     for part in range(at.tokens):
         rows = slice(part * BLOCK, (part + 1) * BLOCK)
         ctx_ref[part] = jnp.concatenate([held_ref[0, rows], held_ref[1, rows]], axis=1)
-
-
-def attend(xs, qkvs, tables, vecs):
-    tokens, local_len, width = xs.shape
-    full_len = tokens * local_len
-    buckets = tokens * tables.shape[3]
-    blocks = full_len // BLOCK
-    units = 3 * blocks // 2
-    band_width = buckets + BLOCK
-    low, wide = jnp.bfloat16, jnp.float32
-    pad_blocks = blocks + band_width // BLOCK - 1
-    return pl.pallas_call(
-        attend_kernel,
-        out_shape=(
-            jax.ShapeDtypeStruct((2, full_len, DH), low),
-            jax.ShapeDtypeStruct((2, full_len, DH), low),
-            jax.ShapeDtypeStruct((2, full_len, DH), low),
-            jax.ShapeDtypeStruct((2, buckets, DH), low),
-            jax.ShapeDtypeStruct((2, buckets, DH), low),
-            jax.ShapeDtypeStruct((units, BLOCK, full_len), low),
-            jax.ShapeDtypeStruct((tokens, local_len, 2 * DH), low),
-            jax.ShapeDtypeStruct((width, 6 * DH), low),
-            jax.ShapeDtypeStruct((buckets, width), low),
-        ),
-        in_specs=[pl.BlockSpec(memory_space=pltpu.VMEM)] * 4,
-        out_specs=[pl.BlockSpec(memory_space=pltpu.VMEM)] * 9,
-        scratch_shapes=[
-            pltpu.VMEM((full_len, BLOCK), wide),
-            pltpu.VMEM((2, pad_blocks, BLOCK, band_width), wide),
-            pltpu.VMEM((2, BLOCK, full_len + buckets), wide),
-            pltpu.VMEM((2, 2, 16, full_len), wide),
-            pltpu.VMEM((2, full_len, DH), low),
-        ],
-        compiler_params=pltpu.CompilerParams(vmem_limit_bytes=ATTEND_VMEM),
-        name="attend",
-    )(xs, qkvs, tables, vecs)
 
 
 def attend_back_kernel(
@@ -812,8 +778,8 @@
     def pass_on(self, order):
         @pl.when(self.at.inside())
         def _():
-            for h in range(CHUNKS):
-                for j in order:
+            for j in order:
+                for h in range(CHUNKS):
                     self.pass_chunk(j, h)
 
     def clear(self):
@@ -863,7 +829,9 @@
 
 def gather_kernel(
     x_ref, wq_ref, wk_ref, wv_ref, mix_ref, table_ref, vec_ref, up_ref, down_ref,
-    xs_ref, qkvs_ref, mixs_ref, tables_ref, vecs_ref, up2_ref, down2_ref,
+    xs_ref, mixs_ref, vecs_ref, up2_ref, down2_ref,
+    q_ref, k_ref, v_ref, qrev_ref, krev_ref, p_ref, ctx_ref, w_ref, table_all_ref,
+    qkvs_ref, tables_ref, segc_ref, place_ref, wide_ref, ends_ref, held_ref,
     line_send, line_recv, *sems,
 ):
     at = Place()
@@ -959,11 +927,6 @@
         last.append(wires.send(home, home, at.partner()))
 
     arrived(0)
-    for copy in mix_sends:
-        copy.wait_recv()
-    mine = mixs_ref.at[c, b]
-    mix_rows = [wires.send(mine, mine, at.along_rows(k)[1]) for k in range(1, at.batches)]
-    last.append(wires.send(mine, mine, at.partner()))
     arrived(1)
     for k in range(1, at.batches):
         qkv_sends[k - 1].wait_recv()
@@ -975,14 +938,30 @@
         last.append(wires.send(home, home, at.partner()))
     for t in range(2, at.chips - 1):
         arrived(t)
-    for k in range(1, at.batches):
-        mix_rows[k - 1].wait_recv()
-        home = mixs_ref.at[c, at.from_rows(k)]
-        last.append(wires.send(home, home, at.partner()))
     for copy in last:
         copy.wait_recv()
     for copy in own:
         copy.wait()
+    mix_rows, mix_last = [], []
+
+    def between():
+        for copy in mix_sends:
+            copy.wait_recv()
+        mine = mixs_ref.at[c, b]
+        for k in range(1, at.batches):
+            mix_rows.append(wires.send(mine, mine, at.along_rows(k)[1]))
+        mix_last.append(wires.send(mine, mine, at.partner()))
+
+    attend_kernel(
+        xs_ref, qkvs_ref, tables_ref, vecs_ref, q_ref, k_ref, v_ref, qrev_ref, krev_ref, p_ref,
+        ctx_ref, w_ref, table_all_ref, segc_ref, place_ref, wide_ref, ends_ref, held_ref, between,
+    )
+    for k in range(1, at.batches):
+        mix_rows[k - 1].wait_recv()
+        home = mixs_ref.at[c, at.from_rows(k)]
+        mix_last.append(wires.send(home, home, at.partner()))
+    for copy in mix_last:
+        copy.wait_recv()
     wires.finish()
     line.drain(order)
 
@@ -995,15 +974,38 @@
 def gather_inputs(x, w_query, w_key, w_value, w_mix, rel_table, vec, up, down):
     tokens, batches = lax.axis_size("seq"), lax.axis_size("batch")
     chips = tokens // 2
+    local_len, width = x.shape
+    full_len = tokens * local_len
+    buckets = tokens * rel_table.shape[0]
+    units = 3 * full_len // BLOCK // 2
+    band_width = buckets + BLOCK
+    pad_blocks = full_len // BLOCK + band_width // BLOCK - 1
+    low, wide = jnp.bfloat16, jnp.float32
     outs = (
         like(x, tokens),
-        like(w_query, tokens, 3),
         like(w_mix, 2, batches, chips),
-        like(rel_table, 2, batches, chips),
         like(vec, tokens),
         like(up),
         like(down),
-    )
+        jax.ShapeDtypeStruct((2, full_len, DH), low),
+        jax.ShapeDtypeStruct((2, full_len, DH), low),
+        jax.ShapeDtypeStruct((2, full_len, DH), low),
+        jax.ShapeDtypeStruct((2, buckets, DH), low),
+        jax.ShapeDtypeStruct((2, buckets, DH), low),
+        jax.ShapeDtypeStruct((units, BLOCK, full_len), low),
+        jax.ShapeDtypeStruct((tokens, local_len, 2 * DH), low),
+        jax.ShapeDtypeStruct((width, 6 * DH), low),
+        jax.ShapeDtypeStruct((buckets, width), low),
+    )
+    scratch = [
+        pltpu.VMEM((tokens, 3) + w_query.shape, low),
+        pltpu.VMEM((2, batches, chips) + rel_table.shape, low),
+        pltpu.VMEM((full_len, BLOCK), wide),
+        pltpu.VMEM((2, pad_blocks, BLOCK, band_width), wide),
+        pltpu.VMEM((2, BLOCK, full_len + buckets), wide),
+        pltpu.VMEM((2, 2, 16, full_len), wide),
+        pltpu.VMEM((2, full_len, DH), low),
+    ]
     sends = 3 + 2 * (chips - 1) + tokens - 1 + 3 + 6 * (batches - 1) + 3 + chips - 1
     inputs = (x, w_query, w_key, w_value, w_mix, rel_table, vec, up, down)
     return comm_call(
@@ -1014,8 +1016,9 @@
         inputs,
         sends,
         7,
-        scratch=gather_sems(chips),
+        scratch=scratch + gather_sems(chips),
         spec=HBM_SPEC,
+        limit=ATTEND_VMEM,
     )
 
 
@@ -1157,10 +1160,10 @@
     up_acc_ref[...] = dot_tn(hid_ref[z], inner_ref[z])
     down_acc_ref[...] = dot_tn(grad_ref[z], act_ref[z])
     line_pass(grad_line, back_line, order, back)
+    for j in order:
+        weight_grads(j)
     back_line.pass_on(returns[:1])
     back_line.pass_on(returns[1:])
-    for j in order:
-        weight_grads(j)
     width = x_ref.shape[1]
     columns = width // at.batches
     inner_all = inner_ref[...].reshape(at.chips * BLOCK, 2 * hidden_here)
@@ -1666,10 +1669,11 @@
     )
     pack = jnp.pad(pack, ((0, 16 - pack.shape[0]), (0, 0)))
     weights = (w_query, w_key, w_value, w_mix, rel_table, pack, w_up, w_down)
-    xs, qkvs, mixs, tables, vecs, up2, down2 = gather_inputs(
+    gathered = gather_inputs(
         *[pltpu.with_memory_space_constraint(a, pltpu.HBM) for a in (x,) + weights]
     )
-    q, k, v, qrev, krev, probs, ctx, w_cat, table = attend(xs, qkvs, tables, vecs)
+    xs, mixs, vecs, up2, down2 = gathered[:5]
+    q, k, v, qrev, krev, probs, ctx, w_cat, table = gathered[5:]
     output, pre_grad, sums, attn_all, m_mix, ups, downs, upbs = feed_forward(
         ctx, x, mixs, vecs, w_up, w_down, up2, down2, out_grad[0], 1
     )

time: 220 us -> 199 us (0.905)
  Pallas kernels: 214 us -> 195 us
    pallas_call x1 -> x0, Pallas kernels: 17.6 us -> none  [attend(): pl.pallas_call(attend_kernel, out_shape=(jax.ShapeDtypeStruct((2, full_le...]
    pallas_call x1, Pallas kernels: 96 us -> 80.9 us  [feed_forward(): pl.pallas_call(feed_kernel, out_shape=outs, in_specs=[VMEM_SPEC] * len(in...]
    pallas_call x2, Pallas kernels: 98.7 us -> 112 us  [comm_call(): pl.pallas_call(kernel, out_shape=tuple(out_shapes), in_specs=[spec] * len...]
where the time goes in v11:
time: 199 us
  Pallas kernels  195 us (98%)
  other arithmetic  3.39 us (2%)
    pallas_call x2, Pallas kernels, comm_call(): pl.pallas_call(kernel, out_shape=tuple(out_shapes), in_specs=[spec] * len...  112 us
    pallas_call x1, Pallas kernels, feed_forward(): pl.pallas_call(feed_kernel, out_shape=outs, in_specs=[VMEM_SPEC] * len(in...  80.9 us

profile of v11, /device:TPU:0, one launch (start us, length us, event | category | flops | bytes accessed | tf_op | source)
XLA Modules:
  0.0 198.7 jit_solution(3933703151355170961)
XLA Ops:
  0.6 0.0 copy-start.1
  0.7 0.0 copy-start
  0.7 0.0 copy-start.3
  0.7 0.0 copy-start.2
  0.7 0.8 convert_element_type.7
  1.5 0.7 fusion.9
  2.2 1.3 fusion.11.vec_ref
  3.5 56.5 %gather_inputs.1 = (bf16[8,128,768]{2,1,0:T(8,128)(2,1)S(1)}, bf16[2,4,4,96,192]{4,3,2,1,0:T(8,128)(2,1)S(1)}, bf16[8,16,128]{2,1,0:T(8,128)(2,1)S(1)}, bf16[768...) custom-call(bf16[128,768]{1,0:T(8,128)(2,1)} %bitcast.8, ...), custom_call_target="tpu_custom_call" | custom-call | tf_op jit(solution)/shard_map/gather_inputs/pallas_call | solution.py:600
  60.0 0.0 copy-done.1
  60.0 0.0 copy-done
  60.0 0.0 copy-done.3
  60.0 0.0 copy-done.2
  60.0 80.9 %feed_forward.1 = (bf16[128,768]{1,0:T(8,128)(2,1)S(1)}, f32[128,768]{1,0:T(8,128)S(1)}, f32[8,8,128]{2,1,0:T(8,128)S(1)}, bf16[8,128,768]{2,1,0:T(8,128)(2,1)S(...) custom-call(bf16[8,128,128]{2,1,0:T(8,128)(2,1)S(1)} %get-tuple-elem, ...), custom_call_target="tpu_custom_call" | custom-call | tf_op jit(solution)/shard_map/feed_forward/pallas_call | solution.py:1279
  141.0 55.8 %settle_grads.1 = (f32[128,768]{1,0:T(8,128)S(1)}, f32[4,8,128]{2,1,0:T(8,128)S(1)}, f32[8,8,384]{2,1,0:T(8,128)S(1)}, bf16[2,96,384]{2,1,0:T(8,128)(2,1)S(1)}, ...) custom-call(bf16[2,1024,64]{2,1,0:T(8,128)(2,1)S(1)} %get-tuple-element.62.q_ref, ...), custom_call_target="tpu_custom_call" | custom-call | tf_op jit(solution)/shard_map/settle_grads/pallas_call | solution.py:600
  196.8 1.3 finish.1
  198.1 0.6 reduce
Async XLA Ops:
  0.6 59.4 %copy-start.1 = (bf16[384,768]{1,0:T(8,128)(2,1)S(1)}, bf16[384,768]{1,0:T(8,128)(2,1)}, u32[]{:S(2)}) copy-start(bf16[384,768]{1,0:T(8,128)(2,1)} %down_ref.3) | copy-start | bytes 1769476
  0.7 59.4 %copy-start = (bf16[768,384]{1,0:T(8,128)(2,1)S(1)}, bf16[768,384]{1,0:T(8,128)(2,1)}, u32[]{:S(2)}) copy-start(bf16[768,384]{1,0:T(8,128)(2,1)} %up_ref.3) | copy-start | bytes 1769476
  0.7 59.4 %copy-start.3 = (bf16[1,128,768]{2,1,0:T(8,128)(2,1)S(1)}, bf16[1,128,768]{2,1,0:T(8,128)(2,1)}, u32[]{:S(2)}) copy-start(bf16[1,128,768]{2,1,0:T(8,128)(2,1)} %param.29) | copy-start | bytes 589828
  0.7 59.4 %copy-start.2 = (bf16[1,128,768]{2,1,0:T(8,128)(2,1)S(1)}, bf16[1,128,768]{2,1,0:T(8,128)(2,1)}, u32[]{:S(2)}) copy-start(bf16[1,128,768]{2,1,0:T(8,128)(2,1)} %param.15) | copy-start | bytes 589828
